TPU v7x, 256 devices: a whole 4x4x8 slice. The times are simulated.
256 devices in a mesh: grp: 2 (over core), gx: 8 (over z), gy: 16 (over x, y).
Axes of the slice: x: 4, y: 4, z: 8, core: 2. Of those that a mesh axis runs over, the one named last changes fastest.
Arguments:
- ocean_state: float32 [4, 60, 128, 2048], P(None, None, ('grp', 'gx'), 'gy'), may hold values from -6 to 6
- diffusivity: float32 [128, 2048], P(('grp', 'gx'), 'gy'), may hold values from 0.03 to 0.24
- wet_mask: int32 [128, 2048], P(('grp', 'gx'), 'gy'), may hold values 0 or 1
- coast_column: int32 [16, 16, 256], P(('grp', 'gx'), 'gy'), may hold values from 0 to 1023, as said below
- coast_slot: int32 [16, 16, 256], P(('grp', 'gx'), 'gy'), may hold values from 0 to 511, as said below
- owner_node: int32 [16, 16, 128, 4], P(('grp', 'gx'), 'gy'), may hold values from -1 to 16383, as said below
- thickness: float32 [2048, 2048], P(('grp', 'gx'), 'gy'), may hold values from 1 to 3
- viscosity: float32 [2048, 2048], P(('grp', 'gx'), 'gy'), may hold values from 0.5 to 2
- friction: float32 [2048, 2048], P(('grp', 'gx'), 'gy'), may hold values from 0.3 to 3
- grounded: int32 [2048, 2048], P(('grp', 'gx'), 'gy'), may hold values 0 or 1
- coupling: float32 [2048, 2048], P(('grp', 'gx'), 'gy'), may hold values from -1 to 1
- driving: float32 [2, 2048, 2048], P(None, ('grp', 'gx'), 'gy'), may hold values from -16 to 16
- first_guess: float32 [2, 2048, 2048], P(None, ('grp', 'gx'), 'gy'), may hold values from -2 to 2
Outputs:
- ocean_next: float32 [4, 60, 128, 2048], P(None, None, ('grp', 'gx'), 'gy')
- melt_mean: float32 [128, 2048], P(('grp', 'gx'), 'gy')
- velocity: float32 [2, 2048, 2048], P(None, ('grp', 'gx'), 'gy')
- residual: float32 [2, 2048, 2048], P(None, ('grp', 'gx'), 'gy')
Inputs may be any that keep to these rules, and one draw needn't show every extreme that they name: `coast_column`: within a device the 256 numbers are distinct cells of its block. `coast_slot`: within a device the 256 slots are distinct, so at most 4 items go to one peer; every device sends 4 items to some peer. owner_node of an ice device at (peer p, s) is a node of its block exactly when peer p has an item with slot (this device's peer number) * 4 + s, else -1; the nodes of one device are distinct.
All inputs are finite; a program needn't handle non-finite values. No bound on the sum of `wet_mask` or of `grounded` on one device may be relied on, other than what follows from the above.
Results may differ from a plain program's by a relative error of at most 0.00012.
Values sent between devices are 32-bit elements; how exact they have to be, the bound alone decides.
No kernel may reach another device: no remote copies, remote signals or barrier semaphores. Data moves between devices by JAX's collectives and lax.ppermute only.
A program may use at most 64 MiB of HBM per device.

v0:
```python
import functools

import jax
import jax.numpy as jnp
from jax import lax
from jax.sharding import Mesh
from jax.sharding import PartitionSpec as P

NSUB = 4
ITERS = 2
GRP_GX_GY = ("grp", "gx", "gy_0", "gy_1")
GY = ("gy_0", "gy_1")
GX_GY = ("gx", "gy_0", "gy_1")


def extended(value, sides, width):
    edges = {}
    for axis, dim in sides:
        size, length = (lax.axis_size(axis), value.shape[dim])
        up = [(i, (i + 1) % size) for i in range(size - 1)]
        last = lax.slice_in_dim(value, length - width, length, axis=dim)
        first = lax.slice_in_dim(value, 0, width, axis=dim)
        edges[dim] = (
            lax.ppermute(last, axis, up),
            lax.ppermute(first, axis, [(b, a) for a, b in up]),
        )
    done = []
    for _, dim in sides:
        low, high = edges[dim]
        around = [(width, width) if d in done else (0, 0) for d in range(value.ndim)]
        value = jnp.concatenate([jnp.pad(low, around), value, jnp.pad(high, around)], axis=dim)
        done.append(dim)
    return value


def by_axis(value, axes):
    return functools.reduce(lax.psum, axes, value)


def padded_2(block, sides, width):
    for axis, dim in sides:
        count = lax.axis_size(axis)
        forward = [(i, i + 1) for i in range(count - 1)]
        backward = [(target, source) for source, target in forward]
        low = lax.ppermute(
            lax.slice_in_dim(block, block.shape[dim] - width, None, axis=dim), axis, forward
        )
        high = lax.ppermute(lax.slice_in_dim(block, 0, width, axis=dim), axis, backward)
        block = jnp.concatenate([low, block, high], axis=dim)
    return block


def advance(padded, diff_pad, wet_pad, cover, draft_field):
    fields = padded[:, :, 1:-1, 1:-1]
    row_total = fields.shape[2]
    col_total = fields.shape[3]
    diff_here = diff_pad[1:-1, 1:-1]
    wet_here = wet_pad[1:-1, 1:-1]
    flux_sum = jnp.zeros_like(fields)
    for offset in ((2, 1), (0, 1), (1, 2), (1, 0)):
        diff_side = diff_pad[offset[0] : offset[0] + row_total, offset[1] : offset[1] + col_total]
        wet_side = wet_pad[offset[0] : offset[0] + row_total, offset[1] : offset[1] + col_total]
        side_vals = padded[
            :, :, offset[0] : offset[0] + row_total, offset[1] : offset[1] + col_total
        ]
        weight = 0.5 * (diff_here + diff_side) * wet_here * wet_side
        flux_sum = flux_sum + weight * (side_vals - fields)
    top_temp = fields[0, 0]
    top_salt = fields[1, 0]
    top_east = fields[2, 0]
    top_north = fields[3, 0]
    current_speed = jnp.sqrt(top_east * top_east + top_north * top_north + 0.01)
    freezing = -0.5 * top_salt + 0.3 * draft_field - 0.2
    melt_rate = 0.5 * cover * (top_temp - freezing) * current_speed
    updated = fields + flux_sum
    drag_rate = 0.05 * cover * current_speed
    top_rows = jnp.stack(
        [
            updated[0, 0] - 0.3 * melt_rate,
            updated[1, 0] - 0.2 * melt_rate,
            updated[2, 0] - drag_rate * top_east,
            updated[3, 0] - drag_rate * top_north,
        ]
    )
    updated = updated.at[:, 0].set(top_rows)
    return (updated, melt_rate)


def operator_parts(depth_visc, visc_pad, friction, grounded, coupling):
    weight_east = 0.5 * (depth_visc + visc_pad[2:, 1:-1])
    weight_west = 0.5 * (depth_visc + visc_pad[:-2, 1:-1])
    weight_north = 0.5 * (depth_visc + visc_pad[1:-1, 2:])
    weight_south = 0.5 * (depth_visc + visc_pad[1:-1, :-2])
    base_friction = friction * grounded.astype(jnp.float32) + 0.2
    cross_term = 0.9 * base_friction * coupling
    diagonal = weight_east + weight_west + weight_north + weight_south + base_friction
    return (diagonal, weight_east, weight_west, weight_north, weight_south, cross_term)


def apply_padded(vector_pad, parts):
    diagonal, weight_east, weight_west, weight_north, weight_south, cross_term = parts
    inner = vector_pad[:, 1:-1, 1:-1]
    beside = weight_east * vector_pad[:, 2:, 1:-1] + weight_west * vector_pad[:, :-2, 1:-1]
    beside = (
        beside + weight_north * vector_pad[:, 1:-1, 2:] + weight_south * vector_pad[:, 1:-1, :-2]
    )
    return diagonal * inner - beside + cross_term * inner[::-1]


def ice_rim(stacked):
    return extended(stacked, ((("grp", "gx"), 1), (GY, 2)), 1)


def joint_sums(first_value, second_value):
    return (by_axis(first_value, GRP_GX_GY), by_axis(second_value, GRP_GX_GY))


def shards(
    ocean_state,
    diffusivity,
    wet_mask,
    coast_column,
    coast_slot,
    owner_node,
    thickness,
    viscosity,
    friction,
    grounded,
    coupling,
    driving,
    first_guess,
):
    field_count, level_count, row_count, col_count = ocean_state.shape
    layers = field_count * level_count
    owner = owner_node[0, 0]
    valid = owner >= 0
    safe_node = jnp.where(valid, owner, 0)
    thick_flat = thickness.reshape(-1)
    draft_send = jnp.where(valid, 0.9 * thick_flat[safe_node], 0.0)
    draft_recv = lax.all_to_all(draft_send, GX_GY, split_axis=0, concat_axis=0, tiled=True)
    columns = coast_column[0, 0]
    slots = coast_slot[0, 0]
    draft_item = draft_recv.reshape(-1)[slots]
    cell_count = row_count * col_count
    cover = jnp.zeros((cell_count,), jnp.float32).at[columns].set(1.0).reshape(row_count, col_count)
    draft_field = (
        jnp.zeros((cell_count,), jnp.float32)
        .at[columns]
        .set(draft_item)
        .reshape(row_count, col_count)
    )
    wet_field = wet_mask.astype(jnp.float32)
    total = jnp.zeros((row_count, col_count), jnp.float32)
    fields = ocean_state
    stacked = jnp.concatenate(
        [
            fields.reshape(layers, row_count, col_count),
            diffusivity[None],
            wet_field[None],
            cover[None],
            draft_field[None],
        ],
        0,
    )
    padded = padded_2(stacked, ((("grp", "gx"), 1), (GY, 2)), NSUB)
    current = padded[:layers].reshape(
        field_count, level_count, row_count + 2 * NSUB, col_count + 2 * NSUB
    )
    for substep in range(NSUB):
        stop_row = row_count + 2 * NSUB - substep
        stop_col = col_count + 2 * NSUB - substep
        diff_part = padded[layers, substep:stop_row, substep:stop_col]
        wet_part = padded[layers + 1, substep:stop_row, substep:stop_col]
        cover_part = padded[layers + 2, substep + 1 : stop_row - 1, substep + 1 : stop_col - 1]
        draft_part = padded[layers + 3, substep + 1 : stop_row - 1, substep + 1 : stop_col - 1]
        current, melt_rate = advance(current, diff_part, wet_part, cover_part, draft_part)
        margin = NSUB - substep - 1
        total = total + melt_rate[margin : margin + row_count, margin : margin + col_count]
    fields = current
    melt_mean = total / NSUB
    melt_item = melt_mean.reshape(-1)[columns]
    melt_send = jnp.zeros((owner.size,), jnp.float32).at[slots].set(melt_item).reshape(owner.shape)
    melt_recv = lax.all_to_all(melt_send, GX_GY, split_axis=0, concat_axis=0, tiled=True)
    melt_node = (
        jnp.zeros((thick_flat.shape[0],), jnp.float32)
        .at[safe_node.reshape(-1)]
        .add(melt_recv.reshape(-1))
    )
    thinned = thickness * jnp.exp(-0.3 * melt_node.reshape(thickness.shape))
    depth_visc = viscosity * thinned
    padded_first = ice_rim(jnp.concatenate([depth_visc[None], first_guess], 0))
    parts = operator_parts(depth_visc, padded_first[0], friction, grounded, coupling)
    rhs = driving * thinned
    velocity = first_guess
    residual = rhs - apply_padded(padded_first[1:], parts)
    precond = residual / parts[0]
    image = apply_padded(ice_rim(precond), parts)
    norm_now, curvature = joint_sums(jnp.sum(residual * precond), jnp.sum(precond * image))
    step_size = norm_now / curvature
    direction = precond
    along = image
    for iteration in range(ITERS):
        velocity = velocity + step_size * direction
        residual = residual - step_size * along
        if iteration + 1 < ITERS:
            precond = residual / parts[0]
            image = apply_padded(ice_rim(precond), parts)
            norm_next, curvature = joint_sums(jnp.sum(residual * precond), jnp.sum(precond * image))
            ratio = norm_next / norm_now
            step_size = norm_next / (curvature - ratio * norm_next / step_size)
            direction = precond + ratio * direction
            along = image + ratio * along
            norm_now = norm_next
    return (fields, melt_mean, velocity, residual)


def solution(mesh):
    split = Mesh(
        mesh.devices.reshape(mesh.shape["grp"], mesh.shape["gx"], 4, 4),
        ("grp", "gx", "gy_0", "gy_1"),
    )
    placed = (
        P(None, None, ("grp", "gx"), GY),
        P(("grp", "gx"), GY),
        P(("grp", "gx"), GY),
        P(("grp", "gx"), GY, None),
        P(("grp", "gx"), GY, None),
        P(("grp", "gx"), GY, None, None),
        P(("grp", "gx"), GY),
        P(("grp", "gx"), GY),
        P(("grp", "gx"), GY),
        P(("grp", "gx"), GY),
        P(("grp", "gx"), GY),
        P(None, ("grp", "gx"), GY),
        P(None, ("grp", "gx"), GY),
    )
    return jax.shard_map(
        shards,
        mesh=split,
        in_specs=placed,
        out_specs=(
            P(None, None, ("grp", "gx"), GY),
            P(("grp", "gx"), GY),
            P(None, ("grp", "gx"), GY),
            P(None, ("grp", "gx"), GY),
        ),
        check_vma=False,
    )
```

profile of v0, /device:TPU:8, one launch (start us, length us, event | category | flops | bytes accessed | tf_op | source)
XLA Modules:
  0.0 269.6 jit_solution(17035357107964336686)
XLA Ops:
  3.1 3.1 %gather_fusion = f32[512]{0:T(512)S(1)} fusion(f32[16384]{0:T(1024)S(1)} %bitcast.394, s32[1024]{0:T(1024)S(1)} %get-tuple-element.172), kind=kCustom, calls=%fused_computation | custom fusion | bytes 6144 | tf_op jit(solution)/shard_map/gather | solution.py:139
  7.0 15.3 %all-to-all-start = ((f32[128,1,4]{2,1,0:T(1,128)}), f32[128,1,4]{2,1,0:T(1,128)S(1)}, u32[]{:S(2)}, u32[]{:S(2)}) async-start(f32[128,1,4]{2,1,0:T(1,128)} %bitcast.9), calls=%async_computation | async-start | bytes 131072 | tf_op jit(solution)/shard_map/all_to_all | solution.py:140
  24.0 9.7 %all-to-all-done = f32[128,1,4]{2,1,0:T(1,128)S(1)} async-done(((f32[128,1,4]{2,1,0:T(1,128)}), f32[128,1,4]{2,1,0:T(1,128)S(1)}, u32[]{:S(2)}, u32[]{:S(2)}) %all-to-all-start) | async-done | bytes 2080 | tf_op jit(solution)/shard_map/all_to_all | solution.py:140
  38.6 2.6 collective-permute-start
  42.7 7.8 %collective-permute-done = f32[244,4,128]{2,1,0:T(4,128)S(1)} collective-permute-done((f32[244,4,128]{2,1,0:T(4,128)S(1)}, f32[244,4,128]{2,1,0:T(4,128)S(1)}, u32[]{:S(2)}, u32[]{:S(2)}) %collective-permute-start) | collective-permute-done | bytes 499744 | tf_op jit(solution)/shard_map/ppermute | solution.py:45
  50.4 4.1 %collective-permute-done.1 = f32[244,4,128]{2,1,0:T(4,128)S(1)} collective-permute-done((f32[244,4,128]{2,1,0:T(4,128)S(1)}, f32[244,4,128]{2,1,0:T(4,128)S(1)}, u32[]{:S(2)}, u32[]{:S(2)}) %collective-permute-start.1) | collective-permute-done | bytes 499744 | tf_op jit(solution)/shard_map/ppermute | solution.py:48
  62.4 3.4 %collective-permute-start.3 = (f32[244,16,4]{0,1,2:T(8,128)S(1)}, f32[244,16,4]{0,1,2:T(8,128)S(1)}, u32[]{:S(2)}, u32[]{:S(2)}) collective-permute-start(f32[244,16,4]{0,1,2:T(8,128)S(1)} %copy.57), channel_id=1, source_target_pairs={{1,0},{2,1},{3,2},{4,3},{5,4},{6,5},{7,6},{8,7},{9,8},{10,9},{11,1... | collective-permute-start | bytes 187400 | tf_op jit(solution)/shard_map/ppermute | solution.py:48
  65.8 2.7 collective-permute-start.2
  68.5 3.5 %collective-permute-done.2 = f32[244,16,4]{0,1,2:T(8,128)S(1)} collective-permute-done((f32[244,16,4]{0,1,2:T(8,128)S(1)}, f32[244,16,4]{0,1,2:T(8,128)S(1)}, u32[]{:S(2)}, u32[]{:S(2)}) %collective-permute-start.2) | collective-permute-done | bytes 62496 | tf_op jit(solution)/shard_map/ppermute | solution.py:45
  75.5 4.5 %pad_maximum_fusion = f32[244,16,136]{2,1,0:T(8,128)S(1)} fusion(f32[244,16,4]{2,1,0:T(8,128)} %copy.59, f32[244,4,128]{2,1,0:T(4,128)} %copy-done.5, f32[244,8,128]{2,1,0:T(8,128)S(1)} %constant_dynamic-update-slice_fusion, f32[244,4,128]{2,1,0:T(4,128)} %copy-done.3, f32[244,16,4]{2,1,0:T(8,128)S(1)} %copy.58), kind=kLoop, calls=%fused_computation.7 | loop fusion | flops 2123776 | bytes 4247552 | tf_op jit(solution)/shard_map/concatenate | solution.py:49
  82.0 4.3 %fusion.18 = f32[4,60,14,134]{3,2,1,0:T(8,128)S(1)} fusion(f32[4,60,16,136]{3,2,1,0:T(8,128)S(1)} %bitcast.397, f32[14,134]{1,0:T(8,128)S(1)} %get-tuple-element.170, f32[14,134]{1,0:T(8,128)S(1)} %get-tuple-element.168, f32[14,134]{1,0:T(8,128)S(1)} %get-tuple-element.169, f32[14,134]{1,0:T(8,128)S(1)} %get-tuple-element.167), kind=kLoop, calls=%fused_computation.35 | loop fusion | flops 5402880 | bytes 10835776 | tf_op jit(solution)/shard_map/add | solution.py:75
  86.9 4.3 %fusion.10 = f32[4,60,12,132]{3,2,1,0:T(8,128)S(1)} fusion(f32[4,60,14,134]{3,2,1,0:T(8,128)S(1)} %constant_dynamic-update-slice_fusion.7, f32[12,132]{1,0:T(8,128)S(1)} %get-tuple-element.166, f32[12,132]{1,0:T(8,128)S(1)} %get-tuple-element.164, f32[12,132]{1,0:T(8,128)S(1)} %get-tuple-element.165, f32[12,132]{1,0:T(8,128)S(1)} %get-tuple-element.163), kind=kLoop, calls=%fused_computation.23 | loop fusion | flops 4561920 | bytes 9149184 | tf_op jit(solution)/shard_map/add | solution.py:75
  91.6 4.3 %fusion.2 = f32[4,60,10,130]{3,2,1,0:T(8,128)S(1)} fusion(f32[4,60,12,132]{3,2,1,0:T(8,128)S(1)} %constant_dynamic-update-slice_fusion.6, f32[10,130]{1,0:T(8,128)S(1)} %get-tuple-element.162, f32[10,130]{1,0:T(8,128)S(1)} %get-tuple-element.160, f32[10,130]{1,0:T(8,128)S(1)} %get-tuple-element.161, f32[10,130]{1,0:T(8,128)S(1)} %get-tuple-element.159), kind=kLoop, calls=%fused_computation.11 | loop fusion | flops 3744000 | bytes 7508800 | tf_op jit(solution)/shard_map/add | solution.py:75
  101.7 9.1 %all-to-all-start.1 = ((f32[128,1,4]{2,1,0:T(1,128)}), f32[128,1,4]{2,1,0:T(1,128)S(1)}, u32[]{:S(2)}, u32[]{:S(2)}) async-start(f32[128,1,4]{2,1,0:T(1,128)} %bitcast.85), calls=%async_computation.1 | async-start | bytes 131072 | tf_op jit(solution)/shard_map/all_to_all | solution.py:183
  110.9 6.8 %fusion.26 = f32[4,60,8,128]{3,2,1,0:T(8,128)S(1)} fusion(f32[4,60,10,130]{3,2,1,0:T(8,128)} %copy-done.7, f32[8,128]{1,0:T(8,128)S(1)} %get-tuple-element.158, f32[8,128]{1,0:T(8,128)S(1)} %get-tuple-element.156, f32[8,128]{1,0:T(8,128)S(1)} %get-tuple-element.157, f32[8,128]{1,0:T(8,128)S(1)} %get-tuple-element.155), kind=kLoop, calls=%fused_computation.48 | loop fusion | flops 2949120 | bytes 5914624 | tf_op jit(solution)/shard_map/add | solution.py:75
  117.8 4.3 %all-to-all-done.1 = f32[128,1,4]{2,1,0:T(1,128)S(1)} async-done(((f32[128,1,4]{2,1,0:T(1,128)}), f32[128,1,4]{2,1,0:T(1,128)S(1)}, u32[]{:S(2)}, u32[]{:S(2)}) %all-to-all-start.1) | async-done | bytes 2080 | tf_op jit(solution)/shard_map/all_to_all | solution.py:183
  123.0 3.3 %scatter_custom_fusion.3 = f32[16384]{0:T(1024)S(1)} fusion(s32[512]{0:T(512)S(1)} %bitcast.412, f32[512]{0:T(512)S(1)} %reshape.815, f32[]{:T(128)} %constant.135.clone.1), kind=kCustom, calls=%fused_computation.162 | custom fusion | flops 512 | bytes 65540 | tf_op jit(solution)/shard_map/scatter-add | solution.py:187
  132.5 3.7 %collective-permute-start.7 = (f32[3,128,1]{2,1,0:T(8,128)S(1)}, f32[3,128,1]{2,1,0:T(8,128)S(1)}, u32[]{:S(2)}, u32[]{:S(2)}) collective-permute-start(f32[3,128,1]{2,1,0:T(8,128)S(1)} %get-tuple-element.136), channel_id=1, source_target_pairs={{1,0},{2,1},{3,2},{4,3},{5,4},{6,5},{7,6},{8,7},{9,8},{10,9},{11,1... | collective-permute-start | bytes 4616 | tf_op jit(solution)/shard_map/ppermute | solution.py:25
  136.4 3.3 %collective-permute-done.4 = f32[3,128,1]{2,1,0:T(8,128)S(1)} collective-permute-done((f32[3,128,1]{2,1,0:T(8,128)S(1)}, f32[3,128,1]{2,1,0:T(8,128)S(1)}, u32[]{:S(2)}, u32[]{:S(2)}) %collective-permute-start.4) | collective-permute-done | bytes 1568 | tf_op jit(solution)/shard_map/ppermute | solution.py:24
  142.4 2.9 %collective-permute-start.9 = (f32[2,1,128]{2,1,0:T(1,128)S(1)}, f32[2,1,128]{2,1,0:T(1,128)S(1)}, u32[]{:S(2)}, u32[]{:S(2)}) collective-permute-start(f32[2,1,128]{2,1,0:T(1,128)S(1)} %get-tuple-element.143), channel_id=1, source_target_pairs={{0,16},{16,32},{32,48},{48,64},{64,80},{80,96},{96,112},{112,128},... | collective-permute-start | bytes 3080 | tf_op jit(solution)/shard_map/ppermute | solution.py:24
  146.6 3.7 %collective-permute-start.10 = (f32[2,128,1]{2,1,0:T(8,128)S(1)}, f32[2,128,1]{2,1,0:T(8,128)S(1)}, u32[]{:S(2)}, u32[]{:S(2)}) collective-permute-start(f32[2,128,1]{2,1,0:T(8,128)S(1)} %get-tuple-element.141), channel_id=1, source_target_pairs={{1,0},{2,1},{3,2},{4,3},{5,4},{6,5},{7,6},{8,7},{9,8},{10,9},{11,1... | collective-permute-start | bytes 3080 | tf_op jit(solution)/shard_map/ppermute | solution.py:25
  153.5 4.7 %collective-permute-done.11 = f32[2,128,1]{2,1,0:T(8,128)S(1)} collective-permute-done((f32[2,128,1]{2,1,0:T(8,128)S(1)}, f32[2,128,1]{2,1,0:T(8,128)S(1)}, u32[]{:S(2)}, u32[]{:S(2)}) %collective-permute-start.11) | collective-permute-done | bytes 1056 | tf_op jit(solution)/shard_map/ppermute | solution.py:24
  158.9 3.1 %all-reduce.13 = (f32[]{:T(128)}, f32[]{:T(128)}) all-reduce(f32[]{:T(128)} %get-tuple-element.59, f32[]{:T(128)} %get-tuple-element.58), channel_id=1, replica_groups=mesh['grp'=2,'gx'=8,'gy_0'=4,'gy_1'=4] {'grp'}, use_global_device_ids=true, to_apply=%region_5.6 | all-reduce | flops 2 | bytes 16 | tf_op jit(solution)/shard_map/psum | solution.py:37
  162.0 16.5 %all-reduce.7 = (f32[]{:T(128)}, f32[]{:T(128)}) all-reduce(f32[]{:T(128)} %get-tuple-element.74, f32[]{:T(128)} %get-tuple-element.75), channel_id=1, replica_groups=mesh['grp'=2,'gx'=8,'gy_0'=4,'gy_1'=4] {'gx'}, use_global_device_ids=true, to_apply=%region_6.7 | all-reduce | flops 2 | bytes 16 | tf_op jit(solution)/shard_map/psum | solution.py:37
  178.5 13.0 %all-reduce.11 = (f32[]{:T(128)}, f32[]{:T(128)}) all-reduce(f32[]{:T(128)} %get-tuple-element.62, f32[]{:T(128)} %get-tuple-element.63), channel_id=1, replica_groups=mesh['grp'=2,'gx'=8,'gy_0'=4,'gy_1'=4] {'gy_0'}, use_global_device_ids=true, to_apply=%region_7.8 | all-reduce | flops 2 | bytes 16 | tf_op jit(solution)/shard_map/psum | solution.py:37
  191.5 12.5 %all-reduce.9 = (f32[]{:T(128)}, f32[]{:T(128)}) all-reduce(f32[]{:T(128)} %get-tuple-element.70, f32[]{:T(128)} %get-tuple-element.71), channel_id=1, replica_groups=mesh['grp'=2,'gx'=8,'gy_0'=4,'gy_1'=4] {'gy_1'}, use_global_device_ids=true, to_apply=%region_8.9 | all-reduce | flops 2 | bytes 16 | tf_op jit(solution)/shard_map/psum | solution.py:37
  205.5 3.1 %collective-permute-start.13 = (f32[2,1,128]{2,1,0:T(1,128)S(1)}, f32[2,1,128]{2,1,0:T(1,128)S(1)}, u32[]{:S(2)}, u32[]{:S(2)}) collective-permute-start(f32[2,1,128]{2,1,0:T(1,128)S(1)} %get-tuple-element.139), channel_id=1, source_target_pairs={{0,16},{16,32},{32,48},{48,64},{64,80},{80,96},{96,112},{112,128},... | collective-permute-start | bytes 3080 | tf_op jit(solution)/shard_map/ppermute | solution.py:24
  211.8 3.9 %collective-permute-start.15 = (f32[2,128,1]{2,1,0:T(8,128)S(1)}, f32[2,128,1]{2,1,0:T(8,128)S(1)}, u32[]{:S(2)}, u32[]{:S(2)}) collective-permute-start(f32[2,128,1]{2,1,0:T(8,128)S(1)} %get-tuple-element.138), channel_id=1, source_target_pairs={{0,1},{1,2},{2,3},{3,4},{4,5},{5,6},{6,7},{7,8},{8,9},{9,10},{10,1... | collective-permute-start | bytes 3080 | tf_op jit(solution)/shard_map/ppermute | solution.py:24
  219.9 3.6 %all-reduce.12 = (f32[]{:T(128)}, f32[]{:T(128)}) all-reduce(f32[]{:T(128)} %get-tuple-element.57, f32[]{:T(128)} %get-tuple-element.56), channel_id=1, replica_groups=mesh['grp'=2,'gx'=8,'gy_0'=4,'gy_1'=4] {'grp'}, use_global_device_ids=true, to_apply=%region_15.16 | all-reduce | flops 2 | bytes 16 | tf_op jit(solution)/shard_map/psum | solution.py:37
  223.5 17.8 %all-reduce.6 = (f32[]{:T(128)}, f32[]{:T(128)}) all-reduce(f32[]{:T(128)} %get-tuple-element.72, f32[]{:T(128)} %get-tuple-element.73), channel_id=1, replica_groups=mesh['grp'=2,'gx'=8,'gy_0'=4,'gy_1'=4] {'gx'}, use_global_device_ids=true, to_apply=%region_16.17 | all-reduce | flops 2 | bytes 16 | tf_op jit(solution)/shard_map/psum | solution.py:37
  241.3 9.9 %all-reduce.10 = (f32[]{:T(128)}, f32[]{:T(128)}) all-reduce(f32[]{:T(128)} %get-tuple-element.60, f32[]{:T(128)} %get-tuple-element.61), channel_id=1, replica_groups=mesh['grp'=2,'gx'=8,'gy_0'=4,'gy_1'=4] {'gy_0'}, use_global_device_ids=true, to_apply=%region_17.18 | all-reduce | flops 2 | bytes 16 | tf_op jit(solution)/shard_map/psum | solution.py:37
  251.2 12.5 %all-reduce.8 = (f32[]{:T(128)}, f32[]{:T(128)}) all-reduce(f32[]{:T(128)} %get-tuple-element.68, f32[]{:T(128)} %get-tuple-element.69), channel_id=1, replica_groups=mesh['grp'=2,'gx'=8,'gy_0'=4,'gy_1'=4] {'gy_1'}, use_global_device_ids=true, to_apply=%region_18.19 | all-reduce | flops 2 | bytes 16 | tf_op jit(solution)/shard_map/psum | solution.py:37
  (140 shorter events, 54.9 us)
Async XLA Ops:
  3.1 19.3 %copy-start.18 = (s32[1,1,256]{2,1,0:T(1,128)S(1)}, s32[1,1,256]{2,1,0:T(1,128)}, u32[]{:S(2)}) copy-start(s32[1,1,256]{2,1,0:T(1,128)} %param.25) | copy-start | bytes 3076
  3.1 19.3 %copy-start.10 = (f32[4,60,8,128]{3,2,1,0:T(8,128)S(1)}, f32[4,60,8,128]{3,2,1,0:T(8,128)}, u32[]{:S(2)}) copy-start(f32[4,60,8,128]{3,2,1,0:T(8,128)} %param.21) | copy-start | bytes 2949124
  3.1 20.8 %copy-start.16 = (f32[8,128]{1,0:T(8,128)S(1)}, f32[8,128]{1,0:T(8,128)}, u32[]{:S(2)}) copy-start(f32[8,128]{1,0:T(8,128)} %param.22) | copy-start | bytes 12292
  3.1 20.8 %copy-start.17 = (s32[8,128]{1,0:T(8,128)S(1)}, s32[8,128]{1,0:T(8,128)}, u32[]{:S(2)}) copy-start(s32[8,128]{1,0:T(8,128)} %param.23) | copy-start | bytes 12292
  7.0 26.6 %all-to-all-start = ((f32[128,1,4]{2,1,0:T(1,128)}), f32[128,1,4]{2,1,0:T(1,128)S(1)}, u32[]{:S(2)}, u32[]{:S(2)}) async-start(f32[128,1,4]{2,1,0:T(1,128)} %bitcast.9), calls=%async_computation | async-start | bytes 131072 | tf_op jit(solution)/shard_map/all_to_all | solution.py:140
  38.6 11.8 %collective-permute-start = (f32[244,4,128]{2,1,0:T(4,128)S(1)}, f32[244,4,128]{2,1,0:T(4,128)S(1)}, u32[]{:S(2)}, u32[]{:S(2)}) collective-permute-start(f32[244,4,128]{2,1,0:T(4,128)S(1)} %get-tuple-element.131), channel_id=1, source_target_pairs={{0,16},{16,32},{32,48},{48,64},{64,80},{80,96},{96,112},{112,128},... | collective-permute-start | bytes 1499144 | tf_op jit(solution)/shard_map/ppermute | solution.py:45
  41.3 13.3 %collective-permute-start.1 = (f32[244,4,128]{2,1,0:T(4,128)S(1)}, f32[244,4,128]{2,1,0:T(4,128)S(1)}, u32[]{:S(2)}, u32[]{:S(2)}) collective-permute-start(f32[244,4,128]{2,1,0:T(4,128)S(1)} %get-tuple-element.132), channel_id=1, source_target_pairs={{16,0},{32,16},{48,32},{64,48},{80,64},{96,80},{112,96},{128,112},... | collective-permute-start | bytes 1499144 | tf_op jit(solution)/shard_map/ppermute | solution.py:48
  50.4 7.0 %copy-start.3 = (f32[244,4,128]{2,1,0:T(4,128)}, f32[244,4,128]{2,1,0:T(4,128)S(1)}, u32[]{:S(2)}) copy-start(f32[244,4,128]{2,1,0:T(4,128)S(1)} %collective-permute-done) | copy-start | bytes 1499140
  54.5 2.9 %copy-start.5 = (f32[244,4,128]{2,1,0:T(4,128)}, f32[244,4,128]{2,1,0:T(4,128)S(1)}, u32[]{:S(2)}) copy-start(f32[244,4,128]{2,1,0:T(4,128)S(1)} %collective-permute-done.1) | copy-start | bytes 1499140
  62.4 10.7 %collective-permute-start.3 = (f32[244,16,4]{0,1,2:T(8,128)S(1)}, f32[244,16,4]{0,1,2:T(8,128)S(1)}, u32[]{:S(2)}, u32[]{:S(2)}) collective-permute-start(f32[244,16,4]{0,1,2:T(8,128)S(1)} %copy.57), channel_id=1, source_target_pairs={{1,0},{2,1},{3,2},{4,3},{5,4},{6,5},{7,6},{8,7},{9,8},{10,9},{11,1... | collective-permute-start | bytes 187400 | tf_op jit(solution)/shard_map/ppermute | solution.py:48
  65.8 6.2 %collective-permute-start.2 = (f32[244,16,4]{0,1,2:T(8,128)S(1)}, f32[244,16,4]{0,1,2:T(8,128)S(1)}, u32[]{:S(2)}, u32[]{:S(2)}) collective-permute-start(f32[244,16,4]{0,1,2:T(8,128)S(1)} %copy.56), channel_id=1, source_target_pairs={{0,1},{1,2},{2,3},{3,4},{4,5},{5,6},{6,7},{7,8},{8,9},{9,10},{10,1... | collective-permute-start | bytes 187400 | tf_op jit(solution)/shard_map/ppermute | solution.py:45
  96.2 30.1 %copy-start.15 = (f32[128,128]{1,0:T(8,128)S(1)}, f32[128,128]{1,0:T(8,128)}, u32[]{:S(2)}) copy-start(f32[128,128]{1,0:T(8,128)} %param.28) | copy-start | bytes 196612
  98.1 28.2 %copy-start.1 = (f32[8,128]{1,0:T(8,128)}, f32[8,128]{1,0:T(8,128)S(1)}, u32[]{:S(2)}) copy-start(f32[8,128]{1,0:T(8,128)S(1)} %fusion.139) | copy-start | bytes 12292
  98.2 28.2 %copy-start.8 = (f32[2,128,128]{2,1,0:T(8,128)S(1)}, f32[2,128,128]{2,1,0:T(8,128)}, u32[]{:S(2)}) copy-start(f32[2,128,128]{2,1,0:T(8,128)} %param.33) | copy-start | bytes 393220
  101.7 20.4 %all-to-all-start.1 = ((f32[128,1,4]{2,1,0:T(1,128)}), f32[128,1,4]{2,1,0:T(1,128)S(1)}, u32[]{:S(2)}, u32[]{:S(2)}) async-start(f32[128,1,4]{2,1,0:T(1,128)} %bitcast.85), calls=%async_computation.1 | async-start | bytes 131072 | tf_op jit(solution)/shard_map/all_to_all | solution.py:183
  110.9 31.0 %copy-start.12 = (f32[128,128]{1,0:T(8,128)S(1)}, f32[128,128]{1,0:T(8,128)}, u32[]{:S(2)}) copy-start(f32[128,128]{1,0:T(8,128)} %param.29) | copy-start | bytes 196612
  110.9 31.0 %copy-start.13 = (s32[128,128]{1,0:T(8,128)S(1)}, s32[128,128]{1,0:T(8,128)}, u32[]{:S(2)}) copy-start(s32[128,128]{1,0:T(8,128)} %param.30) | copy-start | bytes 196612
  110.9 31.0 %copy-start.14 = (f32[128,128]{1,0:T(8,128)S(1)}, f32[128,128]{1,0:T(8,128)}, u32[]{:S(2)}) copy-start(f32[128,128]{1,0:T(8,128)} %param.31) | copy-start | bytes 196612
  110.9 31.2 %copy-start.11 = (f32[2,128,128]{2,1,0:T(8,128)S(1)}, f32[2,128,128]{2,1,0:T(8,128)}, u32[]{:S(2)}) copy-start(f32[2,128,128]{2,1,0:T(8,128)} %param.32) | copy-start | bytes 393220
  126.5 15.3 %collective-permute-start.5 = (f32[3,1,128]{2,1,0:T(1,128)S(1)}, f32[3,1,128]{2,1,0:T(1,128)S(1)}, u32[]{:S(2)}, u32[]{:S(2)}) collective-permute-start(f32[3,1,128]{2,1,0:T(1,128)S(1)} %get-tuple-element.133), channel_id=1, source_target_pairs={{0,16},{16,32},{32,48},{48,64},{64,80},{80,96},{96,112},{112,128},... | collective-permute-start | bytes 4616 | tf_op jit(solution)/shard_map/ppermute | solution.py:24
  129.1 12.7 %collective-permute-start.6 = (f32[3,1,128]{2,1,0:T(1,128)S(1)}, f32[3,1,128]{2,1,0:T(1,128)S(1)}, u32[]{:S(2)}, u32[]{:S(2)}) collective-permute-start(f32[3,1,128]{2,1,0:T(1,128)S(1)} %get-tuple-element.134), channel_id=1, source_target_pairs={{16,0},{32,16},{48,32},{64,48},{80,64},{96,80},{112,96},{128,112},... | collective-permute-start | bytes 4616 | tf_op jit(solution)/shard_map/ppermute | solution.py:25
  130.4 9.2 %collective-permute-start.4 = (f32[3,128,1]{2,1,0:T(8,128)S(1)}, f32[3,128,1]{2,1,0:T(8,128)S(1)}, u32[]{:S(2)}, u32[]{:S(2)}) collective-permute-start(f32[3,128,1]{2,1,0:T(8,128)S(1)} %get-tuple-element.135), channel_id=1, source_target_pairs={{0,1},{1,2},{2,3},{3,4},{4,5},{5,6},{6,7},{7,8},{8,9},{9,10},{10,1... | collective-permute-start | bytes 4616 | tf_op jit(solution)/shard_map/ppermute | solution.py:24
  132.5 9.2 %collective-permute-start.7 = (f32[3,128,1]{2,1,0:T(8,128)S(1)}, f32[3,128,1]{2,1,0:T(8,128)S(1)}, u32[]{:S(2)}, u32[]{:S(2)}) collective-permute-start(f32[3,128,1]{2,1,0:T(8,128)S(1)} %get-tuple-element.136), channel_id=1, source_target_pairs={{1,0},{2,1},{3,2},{4,3},{5,4},{6,5},{7,6},{8,7},{9,8},{10,9},{11,1... | collective-permute-start | bytes 4616 | tf_op jit(solution)/shard_map/ppermute | solution.py:25
  142.4 10.1 %collective-permute-start.9 = (f32[2,1,128]{2,1,0:T(1,128)S(1)}, f32[2,1,128]{2,1,0:T(1,128)S(1)}, u32[]{:S(2)}, u32[]{:S(2)}) collective-permute-start(f32[2,1,128]{2,1,0:T(1,128)S(1)} %get-tuple-element.143), channel_id=1, source_target_pairs={{0,16},{16,32},{32,48},{48,64},{64,80},{80,96},{96,112},{112,128},... | collective-permute-start | bytes 3080 | tf_op jit(solution)/shard_map/ppermute | solution.py:24
  145.3 7.2 %collective-permute-start.8 = (f32[2,1,128]{2,1,0:T(1,128)S(1)}, f32[2,1,128]{2,1,0:T(1,128)S(1)}, u32[]{:S(2)}, u32[]{:S(2)}) collective-permute-start(f32[2,1,128]{2,1,0:T(1,128)S(1)} %get-tuple-element.144), channel_id=1, source_target_pairs={{16,0},{32,16},{48,32},{64,48},{80,64},{96,80},{112,96},{128,112},... | collective-permute-start | bytes 3080 | tf_op jit(solution)/shard_map/ppermute | solution.py:25
  146.6 6.9 %collective-permute-start.10 = (f32[2,128,1]{2,1,0:T(8,128)S(1)}, f32[2,128,1]{2,1,0:T(8,128)S(1)}, u32[]{:S(2)}, u32[]{:S(2)}) collective-permute-start(f32[2,128,1]{2,1,0:T(8,128)S(1)} %get-tuple-element.141), channel_id=1, source_target_pairs={{1,0},{2,1},{3,2},{4,3},{5,4},{6,5},{7,6},{8,7},{9,8},{10,9},{11,1... | collective-permute-start | bytes 3080 | tf_op jit(solution)/shard_map/ppermute | solution.py:25
  150.3 7.8 %collective-permute-start.11 = (f32[2,128,1]{2,1,0:T(8,128)S(1)}, f32[2,128,1]{2,1,0:T(8,128)S(1)}, u32[]{:S(2)}, u32[]{:S(2)}) collective-permute-start(f32[2,128,1]{2,1,0:T(8,128)S(1)} %get-tuple-element.142), channel_id=1, source_target_pairs={{0,1},{1,2},{2,3},{3,4},{4,5},{5,6},{6,7},{7,8},{8,9},{9,10},{10,1... | collective-permute-start | bytes 3080 | tf_op jit(solution)/shard_map/ppermute | solution.py:24
  205.5 10.3 %collective-permute-start.13 = (f32[2,1,128]{2,1,0:T(1,128)S(1)}, f32[2,1,128]{2,1,0:T(1,128)S(1)}, u32[]{:S(2)}, u32[]{:S(2)}) collective-permute-start(f32[2,1,128]{2,1,0:T(1,128)S(1)} %get-tuple-element.139), channel_id=1, source_target_pairs={{0,16},{16,32},{32,48},{48,64},{64,80},{80,96},{96,112},{112,128},... | collective-permute-start | bytes 3080 | tf_op jit(solution)/shard_map/ppermute | solution.py:24
  208.6 7.2 %collective-permute-start.12 = (f32[2,1,128]{2,1,0:T(1,128)S(1)}, f32[2,1,128]{2,1,0:T(1,128)S(1)}, u32[]{:S(2)}, u32[]{:S(2)}) collective-permute-start(f32[2,1,128]{2,1,0:T(1,128)S(1)} %get-tuple-element.140), channel_id=1, source_target_pairs={{16,0},{32,16},{48,32},{64,48},{80,64},{96,80},{112,96},{128,112},... | collective-permute-start | bytes 3080 | tf_op jit(solution)/shard_map/ppermute | solution.py:25
  209.9 7.3 %collective-permute-start.14 = (f32[2,128,1]{2,1,0:T(8,128)S(1)}, f32[2,128,1]{2,1,0:T(8,128)S(1)}, u32[]{:S(2)}, u32[]{:S(2)}) collective-permute-start(f32[2,128,1]{2,1,0:T(8,128)S(1)} %get-tuple-element.137), channel_id=1, source_target_pairs={{1,0},{2,1},{3,2},{4,3},{5,4},{6,5},{7,6},{8,7},{9,8},{10,9},{11,1... | collective-permute-start | bytes 3080 | tf_op jit(solution)/shard_map/ppermute | solution.py:25
  211.8 7.3 %collective-permute-start.15 = (f32[2,128,1]{2,1,0:T(8,128)S(1)}, f32[2,128,1]{2,1,0:T(8,128)S(1)}, u32[]{:S(2)}, u32[]{:S(2)}) collective-permute-start(f32[2,128,1]{2,1,0:T(8,128)S(1)} %get-tuple-element.138), channel_id=1, source_target_pairs={{0,1},{1,2},{2,3},{3,4},{4,5},{5,6},{6,7},{7,8},{8,9},{9,10},{10,1... | collective-permute-start | bytes 3080 | tf_op jit(solution)/shard_map/ppermute | solution.py:24
  215.8 53.8 %copy-start.9 = (f32[4,60,8,128]{3,2,1,0:T(8,128)}, f32[4,60,8,128]{3,2,1,0:T(8,128)S(1)}, u32[]{:S(2)}) copy-start(f32[4,60,8,128]{3,2,1,0:T(8,128)S(1)} %fusion.112) | copy-start | bytes 2949124
  (5 other events, 9.3 us)
where the time goes:
time: 271 us; the launch traced here: 270 us
  blocking collectives  88.8 us (33%)
  starting transfers between devices  64.4 us (24%)
  waiting for transfers between devices  43.7 us (16%)
  other arithmetic  36.8 us (14%)
  local copies, waits for them, and re-layouts  28.5 us (11%)
  between operations  7.45 us (3%)
    psum x8, blocking collectives, by_axis(): return functools.reduce(lax.psum, axes, value)  88.8 us
    add x4, other arithmetic, advance(): updated = fields + flux_sum  19.7 us
    ppermute x6, starting transfers between devices, extended(): lax.ppermute(last, axis, up)  16.7 us
    all_to_all x1, starting transfers between devices, shards(): lax.all_to_all(draft_send, GX_GY, split_axis=0, concat_axis=0, tiled=True)  15.3 us
    ppermute x6, starting transfers between devices, extended(): lax.ppermute(first, axis, [(b, a) for a, b in up])  13.3 us
    ppermute x2, waiting for transfers between devices, padded_2(): lax.ppermute(lax.slice_in_dim(block, block.shape[dim] - width, None, axis...  11.2 us
    ppermute x6, waiting for transfers between devices, extended(): lax.ppermute(last, axis, up)  9.89 us
    all_to_all x1, waiting for transfers between devices, shards(): lax.all_to_all(draft_send, GX_GY, split_axis=0, concat_axis=0, tiled=True)  9.68 us
  transfers between devices with their start and end apart: 18, of which 11 were waited for; matrix products, arithmetic and copies ran while one was open for 4% of the time, Pallas kernels for 0%

commit v1 on v0

v1 whole, which is shorter than its diff:
```python
import jax
import jax.numpy as jnp
from jax import lax
from jax.experimental import pallas as pl
from jax.experimental.pallas import tpu as pltpu
from jax.sharding import Mesh
from jax.sharding import PartitionSpec as P

NSUB = 4
HALO = 4
GY = ("gy_0", "gy_1")
XAXES = ("grp", "gx")
ALL = ("grp", "gx", "gy_0", "gy_1")
LEAD = 24
F32 = jnp.float32
BF16 = jnp.bfloat16
I32 = jnp.int32


def iota(shape, dim):
    return lax.broadcasted_iota(I32, shape, dim)


def split3(x):
    high = x.astype(BF16)
    rest = x - high.astype(F32)
    mid = rest.astype(BF16)
    low = (rest - mid.astype(F32)).astype(BF16)
    return high, mid, low


def onehot(hit):
    return jnp.where(hit, 1.0, 0.0).astype(BF16)


def dot_tn(a, b):
    return lax.dot_general(a, b, (((0,), (0,)), ((), ())), preferred_element_type=F32)


def dot_nt(a, b):
    return lax.dot_general(a, b, (((1,), (1,)), ((), ())), preferred_element_type=F32)


def spread(table, half, out_ref):
    row = iota((128, 128), 0) & 15
    group = iota((128, 128), 1) >> 2
    after = pltpu.roll(table, 127, 0)
    before = pltpu.roll(table, 1, 0)
    parts = []
    for dx in range(3):
        part = jnp.where((group == 3 * dx) & (row > 0), before, 0.0)
        part = jnp.where(group == 3 * dx + 1, table, part)
        part = jnp.where((group == 3 * dx + 2) & (row < 15), after, part)
        parts.append(part)
    none = jnp.zeros((16, 128), F32)
    own = parts[1] + jnp.concatenate([none, parts[0][:112]], 0)
    own = own + jnp.concatenate([parts[2][16:], none], 0)
    first = jnp.where(half == 0, parts[0][112:], 0.0)
    last = jnp.where(half == 1, parts[2][:16], 0.0)
    out_ref[pl.ds(half * 128, 128), :] = own
    out_ref[pl.ds((1 - half) * 128, 128), :] = jnp.concatenate(
        [first, jnp.zeros((96, 128), F32), last], 0
    )


def draft_kernel(pos_ref, owner_ref, thick_ref, out_ref):
    lane = iota((128, 128), 1)
    parts = split3(thick_ref[...])
    node = owner_ref[...]
    table = jnp.zeros((128, 128), F32)
    for s in range(4):
        column = node[:, s : s + 1]
        pick = onehot(lane == (column >> 7))
        rows = jnp.dot(pick, parts[0], preferred_element_type=F32)
        rows = rows + jnp.dot(pick, parts[1], preferred_element_type=F32)
        rows = rows + jnp.dot(pick, parts[2], preferred_element_type=F32)
        value = jnp.sum(jnp.where(lane == (column & 127), rows, 0.0), 1, keepdims=True)
        table = jnp.where((lane & 3) == s, 0.9 * value, table)
    spread(table, pos_ref[0], out_ref)


def ice_fields(refs):
    thick, visc, fric, ground, coup, drive, guess = refs
    return (
        lambda at: thick[at],
        lambda at: visc[at],
        lambda at: fric[at] * ground[at].astype(F32),
        lambda at: coup[at],
        lambda at: drive[(0,) + at],
        lambda at: drive[(1,) + at],
        lambda at: guess[(0,) + at],
        lambda at: guess[(1,) + at],
    )


def pack_x_kernel(
    state_ref, diff_ref, wet_ref, col_ref, slot_ref, owner_ref,
    thick, visc, fric, ground, coup, drive, guess,
    up_ref, down_ref, slotmap_ref, nodemap_ref,
):
    col = col_ref[...]
    slot = slot_ref[...]
    hit = iota((8, 256), 0) == (col >> 7)
    peer = jnp.where(hit, ((slot >> 2) + 1).astype(F32), 0.0)
    which = jnp.where(hit, (slot & 3).astype(F32), 0.0)
    lanes = onehot(iota((128, 256), 0) == (col & 127))
    both = dot_nt(jnp.concatenate([peer, which], 0).astype(BF16), lanes)
    slotmap = jnp.where(both[:8] > 0.5, 4.0 * both[:8] + both[8:] - 3.0, 0.0)
    slotmap_ref[...] = slotmap

    node = owner_ref[...]
    lane = iota((128, 128), 1)
    number = iota((128, 128), 0).astype(F32) + 1.0
    peers = []
    whichs = []
    cols = []
    for s in range(4):
        column = node[:, s : s + 1]
        hit = lane == (column >> 7)
        peers.append(jnp.where(hit, number, 0.0).astype(BF16))
        whichs.append(jnp.where(hit, float(s), 0.0).astype(BF16))
        cols.append(onehot(lane == (column & 127)))
    cols = jnp.concatenate(cols, 0)
    peer = dot_tn(jnp.concatenate(peers, 0), cols)
    which = dot_tn(jnp.concatenate(whichs, 0), cols)
    nodemap_ref[...] = jnp.where(peer > 0.5, 4.0 * peer + which - 3.0, 0.0)

    for f in range(4):
        up_ref[f] = state_ref[f, 0, 4:8]
        down_ref[f] = state_ref[f, 0, 0:4]
        up_ref[LEAD + 59 * f : LEAD + 59 * f + 59] = state_ref[f, 1:, 4:8]
        down_ref[LEAD + 59 * f : LEAD + 59 * f + 59] = state_ref[f, 1:, 0:4]
    up_ref[4] = diff_ref[4:8]
    down_ref[4] = diff_ref[0:4]
    wet = wet_ref[...].astype(F32)
    up_ref[5] = wet[4:8]
    down_ref[5] = wet[0:4]
    up_ref[6] = slotmap[4:8]
    down_ref[6] = slotmap[0:4]
    up_ref[7] = jnp.zeros((4, 128), F32)
    down_ref[7] = jnp.zeros((4, 128), F32)
    top = (pl.ds(0, 4), slice(None))
    end = (pl.ds(124, 4), slice(None))
    for a, get in enumerate(ice_fields((thick, visc, fric, ground, coup, drive, guess))):
        up_ref[8 + a] = get(end)
        down_ref[8 + a] = get(top)
    up_ref[16] = nodemap_ref[124:128]
    down_ref[16] = nodemap_ref[0:4]
    for a in range(17, LEAD):
        up_ref[a] = jnp.zeros((4, 128), F32)
        down_ref[a] = jnp.zeros((4, 128), F32)


def pack_y_kernel(
    state_ref, diff_ref, wet_ref, slotmap_ref, lo_ref, hi_ref,
    thick, visc, fric, ground, coup, drive, guess, nodemap_ref,
    up_ref, down_ref,
):
    lane = iota((16, 128), 1)
    at_first = lane >> 2
    at_last = ((lane + 4) & 127) >> 2

    def add(i, own, entry, acc):
        whole = jnp.concatenate([own, hi_ref[entry], lo_ref[entry]], 0)
        rolled = whole if i == 0 else pltpu.roll(whole, 4 * i, 1)
        return (
            jnp.where(at_last == i, rolled, acc[0]),
            jnp.where(at_first == i, rolled, acc[1]),
        )

    for group in range(8):
        acc = (jnp.zeros((16, 128), F32), jnp.zeros((16, 128), F32))
        for i in range(32):
            index = group * 32 + i
            if index < 4:
                acc = add(i, state_ref[index, 0], index, acc)
            elif index == 4:
                acc = add(i, diff_ref[...], index, acc)
            elif index == 5:
                acc = add(i, wet_ref[...].astype(F32), index, acc)
            elif index == 6:
                acc = add(i, slotmap_ref[...], index, acc)
            elif 8 <= index < 244:
                b = index - 8
                acc = add(i, state_ref[b // 59, b % 59 + 1], LEAD + b, acc)
        up_ref[16 * group : 16 * group + 16] = acc[0]
        down_ref[16 * group : 16 * group + 16] = acc[1]

    lane = iota((136, 128), 1)
    at_first = lane >> 2
    at_last = ((lane + 4) & 127) >> 2
    last = jnp.zeros((136, 128), F32)
    first = jnp.zeros((136, 128), F32)
    whole_at = (slice(None), slice(None))
    gets = ice_fields((thick, visc, fric, ground, coup, drive, guess))
    gets = gets + (lambda at: nodemap_ref[...],)
    for a, get in enumerate(gets):
        whole = jnp.concatenate([get(whole_at), hi_ref[8 + a], lo_ref[8 + a]], 0)
        rolled = whole if a == 0 else pltpu.roll(whole, 4 * a, 1)
        last = jnp.where(at_last == a, rolled, last)
        first = jnp.where(at_first == a, rolled, first)
    up_ref[128:264] = last
    down_ref[128:264] = first


def side_lanes(left, right, i, keep):
    lane = iota(left.shape, 1)
    both = jnp.where(((lane + 4) & 127) >> 2 == i, left, right)
    both = pltpu.roll(both, 128 - 4 * i, 1) if i else both
    return jnp.where((lane < 4) | (lane >= 124), both, 0.0) if keep else both


def turn(x, shift, axis):
    return pltpu.roll(x, shift % x.shape[axis], axis)


def lookup(parts, owner, lane_of):
    pick = onehot(iota((256, 128), 0) == owner)
    found = jnp.dot(parts, pick, preferred_element_type=F32)
    found = found[0:48] + found[48:96] + found[96:144]
    return jnp.sum(jnp.where(iota((48, 128), 0) == lane_of, found, 0.0), 0, keepdims=True)


def table_parts(table):
    turned = jnp.transpose(table)[0:48]
    return jnp.concatenate(split3(turned), 0)


def decode(code, half, group):
    number = code.astype(I32) - 1
    owner = jnp.where(number >= 0, half * 128 + (number >> 2), -1)
    return owner, 4 * group + (number & 3)


def pack_rows(x):
    lane = iota((16, 128), 1)
    moved = jnp.where(lane < 8, pltpu.roll(x, 4, 1), 0.0)
    moved = pltpu.roll(moved, 0, 1, stride=8, stride_axis=0)
    return jnp.sum(moved, 0, keepdims=True)


def unpack_rows(row):
    lane = iota((16, 128), 1)
    turned = [row] + [pltpu.roll(row, 128 - 8 * r, 1) for r in range(1, 16)]
    moved = jnp.where(lane < 8, jnp.concatenate(turned, 0), 0.0)
    return pltpu.roll(moved, 124, 1)


def top_kernel(
    pos_ref, state_ref, diff_ref, wet_ref, slotmap_ref, lo_ref, hi_ref, left_ref, right_ref, table_ref,
    top_ref, melt_ref, weight_ref, send_ref,
):
    half = pos_ref[0]
    half_lo = pos_ref[1]
    half_hi = pos_ref[2]
    left = left_ref[0:16]
    right = right_ref[0:16]

    def padded(i, own):
        centre = jnp.concatenate([own, hi_ref[i], lo_ref[i]], 0)
        return jnp.concatenate([centre, side_lanes(left, right, i, True)], 1)

    fields = [padded(f, state_ref[f, 0]) for f in range(4)]
    diff = padded(4, diff_ref[...])
    wet = padded(5, wet_ref[...].astype(F32))
    code = padded(6, slotmap_ref[...])
    weights = []
    for axis, shift in ((0, -1), (0, 1), (1, -1), (1, 1)):
        weights.append(0.5 * (diff + turn(diff, shift, axis)) * wet * turn(wet, shift, axis))
    for j in range(4):
        weight_ref[j] = weights[j]
    weight_ref[4] = 1.0 - (weights[0] + weights[1] + weights[2] + weights[3])

    row = iota((16, 256), 0)
    col = iota((16, 256), 1)
    half_at = jnp.where(row < 8, half, jnp.where(row < 12, half_hi, half_lo))
    dx = jnp.where(row < 8, 1, jnp.where(row < 12, 2, 0))
    dy = jnp.where(col < 128, 1, jnp.where(col < 192, 2, 0))
    owner, lane_of = decode(code, half_at, 3 * dx + dy)
    side_owner = (pack_rows((owner[:, 128:] + 1).astype(F32))).astype(I32) - 1
    side_lane = pack_rows(lane_of[:, 128:].astype(F32)).astype(I32)
    parts = table_parts(table_ref[...])
    found = [lookup(parts, owner[r : r + 1, :128], lane_of[r : r + 1, :128]) for r in range(16)]
    side = unpack_rows(lookup(parts, side_owner, side_lane))
    draft = jnp.concatenate([jnp.concatenate(found, 0), side], 1)
    cover = jnp.where(code > 0.5, 1.0, 0.0)

    total = jnp.zeros((8, 128), F32)
    for substep in range(NSUB):
        temp, salt, east, north = fields
        speed = jnp.sqrt(east * east + north * north + 0.01)
        freezing = -0.5 * salt + 0.3 * draft - 0.2
        melt = 0.5 * cover * (temp - freezing) * speed
        drag = 0.05 * cover * speed
        total = total + melt[0:8, 0:128]
        loss = (0.3 * melt, 0.2 * melt, drag * east, drag * north)
        changed = []
        for f in range(4):
            x = fields[f]
            flux = weights[0] * (turn(x, -1, 0) - x) + weights[1] * (turn(x, 1, 0) - x)
            flux = flux + weights[2] * (turn(x, -1, 1) - x) + weights[3] * (turn(x, 1, 1) - x)
            changed.append(x + flux - loss[f])
        fields = changed
    for f in range(4):
        top_ref[f] = fields[f][0:8, 0:128]
    mean = total * (1.0 / NSUB)
    melt_ref[...] = mean

    number = slotmap_ref[...].astype(I32) - 1
    peers = []
    values = []
    for r in range(8):
        at = number[r : r + 1]
        peers.append(onehot(iota((128, 128), 0) == (at >> 2)))
        values.append(jnp.where((iota((128, 128), 0) & 3) == (at & 3), mean[r : r + 1], 0.0))
    peers = jnp.concatenate(peers, 1)
    values = jnp.concatenate(split3(jnp.concatenate(values, 1)), 0)
    table = dot_nt(peers, values)
    spread(table[:, 0:128] + table[:, 128:256] + table[:, 256:384], half, send_ref)


def bulk_kernel(
    state_ref, lo_ref, hi_ref, left_ref, right_ref, weight_ref, top_ref, out_ref,
):
    for f in range(4):
        out_ref[f, 0] = top_ref[f]
    lane = iota((16, 128), 1)
    last_group = ((lane + 4) & 127) >> 2

    def level(step, carry):
        for f in range(4):
            b = 59 * f + step
            index = b + 8
            i = index & 31
            at = pl.multiple_of((index >> 5) * 16, 16)
            left = left_ref[pl.ds(at, 16), :]
            right = right_ref[pl.ds(at, 16), :]
            both = pltpu.roll(jnp.where(last_group == i, left, right), (128 - 4 * i) & 127, 1)
            centre = jnp.concatenate([state_ref[f, step + 1], hi_ref[LEAD + b], lo_ref[LEAD + b]], 0)
            x = jnp.concatenate([centre, both], 1)
            for substep in range(NSUB):
                y = weight_ref[4] * x
                y = y + weight_ref[0] * turn(x, -1, 0) + weight_ref[1] * turn(x, 1, 0)
                x = y + weight_ref[2] * turn(x, -1, 1) + weight_ref[3] * turn(x, 1, 1)
            out_ref[f, step + 1] = x[0:8, 0:128]
        return carry

    lax.fori_loop(0, 59, level, 0)


def ice_kernel(
    pos_ref, owner_ref, table_ref, lo_ref, hi_ref, left_ref, right_ref,
    thick, visc, fric, ground, coup, drive, guess, nodemap_ref,
    send_ref, res_ref, z_ref, y_ref, w_ref, v_ref,
):
    half = pos_ref[0]
    half_lo = pos_ref[1]
    half_hi = pos_ref[2]
    left = left_ref[...]
    right = right_ref[...]
    whole_at = (slice(None), slice(None))

    gets = ice_fields((thick, visc, fric, ground, coup, drive, guess))
    gets = gets + (lambda at: nodemap_ref[...],)

    def padded(a):
        centre = jnp.concatenate([gets[a](whole_at), hi_ref[8 + a], lo_ref[8 + a]], 0)
        return jnp.concatenate([centre, side_lanes(left, right, a, True)], 1)

    table = table_ref[...]
    mine = table_ref[pl.ds(half * 128, 128), :]
    node = owner_ref[...]
    lane = iota((128, 128), 1)
    rows = []
    cols = []
    for s in range(4):
        column = node[:, s : s + 1]
        rows.append(onehot(lane == (column >> 7)))
        cols.append(jnp.where(lane == (column & 127), mine[:, 16 + s : 17 + s], 0.0))
    cols = jnp.concatenate(split3(jnp.concatenate(cols, 0)), 1)
    melt = dot_tn(jnp.concatenate(rows, 0), cols)
    melt = melt[:, 0:128] + melt[:, 128:256] + melt[:, 256:384]

    code = padded(8)
    row = iota((136, 256), 0)
    col = iota((136, 256), 1)
    half_at = jnp.where(row < 128, half, jnp.where(row < 132, half_hi, half_lo))
    dx = jnp.where(row < 128, 1, jnp.where(row < 132, 2, 0))
    dy = jnp.where(col < 128, 1, jnp.where(col < 192, 2, 0))
    owner, lane_of = decode(code, half_at, 3 * dx + dy)
    parts = table_parts(table)
    rim = [
        lookup(parts, owner[r : r + 1, :128], lane_of[r : r + 1, :128]) for r in range(128, 136)
    ]
    side_owner = (owner[:, 128:] + 1).astype(F32)
    side_lane = lane_of[:, 128:].astype(F32)
    spare = jnp.zeros((8, 128), F32)
    sides = []
    for block in range(9):
        if block < 8:
            piece_owner = side_owner[16 * block : 16 * block + 16]
            piece_lane = side_lane[16 * block : 16 * block + 16]
        else:
            piece_owner = jnp.concatenate([side_owner[128:136], spare], 0)
            piece_lane = jnp.concatenate([side_lane[128:136], spare], 0)
        at_owner = pack_rows(piece_owner).astype(I32) - 1
        at_lane = pack_rows(piece_lane).astype(I32)
        piece = unpack_rows(lookup(parts, at_owner, at_lane))
        sides.append(piece if block < 8 else piece[0:8])
    melt = jnp.concatenate([melt] + rim, 0)
    melt = jnp.concatenate([melt, jnp.concatenate(sides, 0)], 1)

    thickness = padded(0)
    inside = thickness > 0.0
    thinned = thickness * jnp.exp(-0.3 * melt)
    depth = padded(1) * thinned
    base = padded(2) + 0.2
    cross = 0.9 * base * padded(3)
    w_e = 0.5 * (depth + turn(depth, -1, 0))
    w_w = 0.5 * (depth + turn(depth, 1, 0))
    w_n = 0.5 * (depth + turn(depth, -1, 1))
    w_s = 0.5 * (depth + turn(depth, 1, 1))
    diagonal = w_e + w_w + w_n + w_s + base
    inverse = jnp.where(inside, 1.0 / diagonal, 0.0)

    def apply(pair):
        out = []
        for a in range(2):
            x = pair[a]
            beside = w_e * turn(x, -1, 0) + w_w * turn(x, 1, 0)
            beside = beside + w_n * turn(x, -1, 1) + w_s * turn(x, 1, 1)
            out.append(diagonal * x - beside + cross * pair[1 - a])
        return out

    first = [padded(6), padded(7)]
    image = apply(first)
    res = [padded(4 + a) * thinned - image[a] for a in range(2)]
    z = [res[a] * inverse for a in range(2)]
    y = apply(z)
    w = [y[a] * inverse for a in range(2)]
    v = apply(w)
    inner = (slice(0, 128), slice(0, 128))
    sums = []
    for one, two in ((res, z), (z, y), (y, w), (w, v)):
        product = one[0][inner] * two[0][inner] + one[1][inner] * two[1][inner]
        sums.append(jnp.sum(jnp.sum(product, 0, keepdims=True), 1, keepdims=True))
    lane = iota((256, 128), 1)
    message = jnp.zeros((256, 128), F32)
    for k in range(4):
        message = jnp.where(lane == k, sums[k], message)
    send_ref[...] = message
    for a in range(2):
        res_ref[a] = res[a][inner]
        z_ref[a] = z[a][inner]
        y_ref[a] = y[a][inner]
        w_ref[a] = w[a][inner]
        v_ref[a] = v[a][inner]


def update_kernel(sum_ref, guess_ref, res_ref, z_ref, y_ref, w_ref, v_ref, vel_ref, left_ref):
    total = jnp.sum(sum_ref[...], 0, keepdims=True)
    norm, curve, mixed, far = (total[:, k : k + 1] for k in range(4))
    step = norm / curve
    norm_next = norm - 2.0 * step * curve + step * step * mixed
    ratio = norm_next / norm
    along = curve - step * mixed
    curve_next = curve - 2.0 * step * mixed + step * step * far
    curve_next = curve_next + 2.0 * ratio * along + ratio * ratio * curve
    step_next = norm_next / curve_next
    one = step + step_next * (1.0 + ratio)
    two = step_next * step
    for a in range(2):
        vel_ref[a] = guess_ref[a] + one * z_ref[a] - two * w_ref[a]
        left_ref[a] = res_ref[a] - one * y_ref[a] + two * v_ref[a]


def sds(*shape):
    return jax.ShapeDtypeStruct(shape, F32)


SMEM = pl.BlockSpec(memory_space=pltpu.SMEM)


def whole(*shape):
    return pl.BlockSpec(shape, lambda *_: (0,) * len(shape))


def call(kernel, name, in_specs, outs, **kw):
    return pl.pallas_call(
        kernel,
        name=name,
        grid=(1,),
        in_specs=in_specs,
        out_specs=[whole(*o.shape) for o in outs],
        out_shape=outs,
        **kw,
    )


def swap(value, axes, dim_up):
    size = lax.axis_size(axes)
    forward = [(i, i + 1) for i in range(size - 1)]
    up, down = dim_up
    low = lax.ppermute(up, axes, forward)
    high = lax.ppermute(down, axes, [(b, a) for a, b in forward])
    return low, high


def exchange(table):
    return lax.all_to_all(table, ALL, split_axis=0, concat_axis=0, tiled=True)


def shards(
    ocean_state, diffusivity, wet_mask, coast_column, coast_slot, owner_node,
    thickness, viscosity, friction, grounded, coupling, driving, first_guess,
):
    grp = lax.axis_index("grp")
    bx = grp * 8 + lax.axis_index("gx")
    pos = jnp.stack([grp, jnp.maximum(bx - 1, 0) // 8, jnp.minimum(bx + 1, 15) // 8]).astype(I32)
    owner = owner_node[0, 0]
    columns = coast_column.reshape(1, 256)
    slots = coast_slot.reshape(1, 256)
    ice = (thickness, viscosity, friction, grounded, coupling, driving, first_guess)
    ice_specs = [whole(128, 128)] * 5 + [whole(2, 128, 128)] * 2
    state_spec = whole(4, 60, 8, 128)
    entries = LEAD + 236

    (send_draft,) = call(
        draft_kernel, "draft", [SMEM, whole(128, 4), whole(128, 128)], [sds(256, 128)]
    )(pos, owner, thickness)
    up, down, slotmap, nodemap = call(
        pack_x_kernel,
        "pack_x",
        [state_spec, whole(8, 128), whole(8, 128), whole(1, 256), whole(1, 256), whole(128, 4)] + ice_specs,
        [sds(entries, 4, 128), sds(entries, 4, 128), sds(8, 128), sds(128, 128)],
    )(ocean_state, diffusivity, wet_mask, columns, slots, owner, *ice)
    lo, hi = swap(None, XAXES, (up, down))
    got_draft = exchange(send_draft)
    up, down = call(
        pack_y_kernel,
        "pack_y",
        [state_spec, whole(8, 128), whole(8, 128), whole(8, 128), whole(entries, 4, 128), whole(entries, 4, 128)]
        + ice_specs
        + [whole(128, 128)],
        [sds(264, 128), sds(264, 128)],
    )(ocean_state, diffusivity, wet_mask, slotmap, lo, hi, *ice, nodemap)
    left, right = swap(None, GY, (up, down))

    top, melt_mean, weights, send_melt = call(
        top_kernel,
        "top",
        [SMEM, whole(4, 1, 8, 128), whole(8, 128), whole(8, 128), whole(8, 128), whole(8, 4, 128), whole(8, 4, 128)]
        + [whole(16, 128), whole(16, 128), whole(256, 128)],
        [sds(4, 8, 128), sds(8, 128), sds(5, 16, 256), sds(256, 128)],
    )(pos, ocean_state, diffusivity, wet_mask, slotmap, lo, hi, left, right, got_draft)
    got_melt = exchange(send_melt)
    (fields,) = call(
        bulk_kernel,
        "bulk",
        [state_spec, whole(entries, 4, 128), whole(entries, 4, 128), whole(128, 128), whole(128, 128)]
        + [whole(5, 16, 256), whole(4, 8, 128)],
        [sds(4, 60, 8, 128)],
    )(ocean_state, lo, hi, left, right, weights, top)

    side = pl.BlockSpec((136, 128), lambda *_: (0, 0))
    pair = sds(2, 128, 128)
    send_sums, res, z, y, w, v = call(
        ice_kernel,
        "ice",
        [SMEM, whole(128, 4), whole(256, 128), whole(LEAD, 4, 128), whole(LEAD, 4, 128), side, side]
        + ice_specs
        + [whole(128, 128)],
        [sds(256, 128), pair, pair, pair, pair, pair],
    )(pos, owner, got_melt, lo, hi, left[128:], right[128:], *ice, nodemap)
    got_sums = exchange(send_sums)
    velocity, residual = call(
        update_kernel,
        "update",
        [whole(256, 128)] + [whole(2, 128, 128)] * 6,
        [pair, pair],
    )(got_sums, first_guess, res, z, y, w, v)
    return (fields, melt_mean, velocity, residual)


def solution(mesh):
    split = Mesh(
        mesh.devices.reshape(mesh.shape["grp"], mesh.shape["gx"], 4, 4),
        ("grp", "gx", "gy_0", "gy_1"),
    )
    field = P(("grp", "gx"), GY)
    pair = P(None, ("grp", "gx"), GY)
    levels = P(None, None, ("grp", "gx"), GY)
    lists = P(("grp", "gx"), GY, None)
    placed = (levels, field, field, lists, lists, P(("grp", "gx"), GY, None, None))
    placed = placed + (field,) * 5 + (pair, pair)
    return jax.shard_map(
        shards,
        mesh=split,
        in_specs=placed,
        out_specs=(levels, field, pair, pair),
        check_vma=False,
    )
```

time: 271 us -> 118 us (0.44)
  blocking collectives: 88.8 us -> 0 us
  Pallas kernels: 0 us -> 44.6 us
  other arithmetic: 36.8 us -> 0.67 us
  waiting for transfers between devices: 43.7 us -> 15.6 us
  local copies, waits for them, and re-layouts: 28.5 us -> 5.64 us
  starting transfers between devices: 64.4 us -> 49.1 us
  between operations: 7.45 us -> 0.77 us
    psum x8 -> x0, blocking collectives: 88.8 us -> none  [by_axis(): return functools.reduce(lax.psum, axes, value)]
    pallas_call x0 -> x7, Pallas kernels: none -> 44.6 us  [the longest x1 25.9 us: shards(): call(bulk_kernel, 'bulk', [state_spec, whole(entries, 4, 128), whole(entr...]
    ppermute x16 -> x4, starting transfers between devices: 39.9 us -> 11 us  [the longest x2 7.21 us: swap(): low = lax.ppermute(up, axes, forward)]
    ppermute x16 -> x4, waiting for transfers between devices: 29.7 us -> 3.1 us  [the longest x2 3.02 us: swap(): high = lax.ppermute(down, axes, [(b, a) for a, b in forward])]
    add x6 -> x0, other arithmetic: 20.5 us -> none  [the longest x4 19.7 us: advance(): updated = fields + flux_sum]
    all_to_all x2 -> x3, starting transfers between devices: 24.5 us -> 38.1 us  [exchange(): return lax.all_to_all(table, ALL, split_axis=0, concat_axis=0, tiled=True)]
    slice x9 -> x2, local copies, waits for them, and re-layouts: 8.23 us -> 1.27 us  [the longest x1 0.64 us: shards(): left[128:]]
    gather x3 -> x0, local copies, waits for them, and re-layouts: 6.46 us -> none  [the longest x1 3.14 us: shards(): draft_send = jnp.where(valid, 0.9 * thick_flat[safe_node], 0.0)]
  transfers between devices with their start and end apart: 18 -> 7, of which waited for: 11 -> 4; matrix products, arithmetic and copies ran while one was open for 4% -> 2% of each run, Pallas kernels for 0% -> 27%
where the time goes in v1:
time: 118 us; the launch traced here: 116 us
  starting transfers between devices  49.1 us (42%)
  Pallas kernels  44.6 us (38%)
  waiting for transfers between devices  15.6 us (13%)
  local copies, waits for them, and re-layouts  5.64 us (5%)
    all_to_all x3, starting transfers between devices, exchange(): return lax.all_to_all(table, ALL, split_axis=0, concat_axis=0, tiled=True)  38.1 us
    pallas_call x1, Pallas kernels, shards(): call(bulk_kernel, 'bulk', [state_spec, whole(entries, 4, 128), whole(entr...  25.9 us
    all_to_all x3, waiting for transfers between devices, exchange(): return lax.all_to_all(table, ALL, split_axis=0, concat_axis=0, tiled=True)  12.5 us
    ppermute x2, starting transfers between devices, swap(): low = lax.ppermute(up, axes, forward)  7.21 us
    pallas_call x1, Pallas kernels, shards(): call(ice_kernel, 'ice', [SMEM, whole(128, 4), whole(256, 128), whole(LEAD...  4.89 us
    unnamed x19, local copies, waits for them, and re-layouts  4.37 us
    ppermute x2, starting transfers between devices, swap(): high = lax.ppermute(down, axes, [(b, a) for a, b in forward])  3.76 us
    pallas_call x1, Pallas kernels, shards(): call(pack_y_kernel, 'pack_y', [state_spec, whole(8, 128), whole(8, 128),...  3.17 us
  transfers between devices with their start and end apart: 7, of which 4 were waited for; matrix products, arithmetic and copies ran while one was open for 2% of the time, Pallas kernels for 27%

profile of v1, /device:TPU:8, one launch (start us, length us, event | category | flops | bytes accessed | tf_op | source)
XLA Modules:
  0.0 116.3 jit_solution(10031020010194826107)
XLA Ops:
  0.6 1.4 %copy.18 = s32[1,1,128,4]{3,2,1,0:T(8,128)} copy(s32[1,1,128,4]{2,3,1,0:T(4,128)} %param.18) | data formatting | bytes 4096 | tf_op args[5]
  2.0 3.0 %pack_x.1 = (f32[260,4,128]{2,1,0:T(4,128)}, f32[260,4,128]{2,1,0:T(4,128)}, f32[8,128]{1,0:T(8,128)}, f32[128,128]{1,0:T(8,128)}) custom-call(f32[4,60,8,128]{3,2,1,0:T(8,128)} %state_ref.7, f32[8,128]{1,0:T(8,128)} %diff_ref.5, s32[8,128]{1,0:T(8,128)} %wet_ref.5, s32[1,256]{1,0:T(1,128)} %bitcast.27, s32[1,256]{1,0:T(1,128)} %bitcast.28, ...), custom_call_target="tpu_custom_call" | custom-call | tf_op jit(solution)/shard_map/pack_x/pallas_call | solution.py:531
  5.1 3.8 %collective-permute-start = (f32[260,4,128]{2,1,0:T(4,128)}, f32[260,4,128]{2,1,0:T(4,128)S(1)}, u32[]{:S(2)}, u32[]{:S(2)}) collective-permute-start(f32[260,4,128]{2,1,0:T(4,128)} %get-tuple-element.22), channel_id=1, source_target_pairs={{0,16},{16,32},{32,48},{48,64},{64,80},{80,96},{96,112},{112,128},... | collective-permute-start | bytes 1597448 | tf_op jit(solution)/shard_map/ppermute | solution.py:504
  8.9 1.3 %collective-permute-start.1 = (f32[260,4,128]{2,1,0:T(4,128)}, f32[260,4,128]{2,1,0:T(4,128)S(1)}, u32[]{:S(2)}, u32[]{:S(2)}) collective-permute-start(f32[260,4,128]{2,1,0:T(4,128)} %get-tuple-element.23), channel_id=1, source_target_pairs={{16,0},{32,16},{48,32},{64,48},{80,64},{96,80},{112,96},{128,112},... | collective-permute-start | bytes 1597448 | tf_op jit(solution)/shard_map/ppermute | solution.py:505
  10.2 0.7 pad_add_fusion.pos_ref
  10.9 2.1 %draft.1 = f32[256,128]{1,0:T(8,128)} custom-call(s32[3]{0:T(128)} %pad_add_fusion.pos_ref, s32[128,4]{1,0:T(8,128)} %bitcast.19, f32[128,128]{1,0:T(8,128)} %thick.5), custom_call_target="tpu_custom_call" | custom-call | tf_op jit(solution)/shard_map/draft/pallas_call | solution.py:528
  13.0 16.5 %all-to-all-start = ((f32[256,1,128]{2,1,0:T(1,128)}), f32[256,1,128]{2,1,0:T(1,128)S(1)}, u32[]{:S(2)}, u32[]{:S(2)}) async-start(f32[256,1,128]{2,1,0:T(1,128)} %bitcast.23), calls=%async_computation | async-start | bytes 262144 | tf_op jit(solution)/shard_map/all_to_all | solution.py:510
  29.5 0.0 collective-permute-done.lo_ref
  29.5 0.0 collective-permute-done.1.hi_ref
  29.5 0.0 copy-start.1
  29.5 0.8 copy-done
  30.3 0.2 copy-done.1
  30.5 3.2 %pack_y.1 = (f32[264,128]{1,0:T(8,128)}, f32[264,128]{1,0:T(8,128)}) custom-call(f32[4,60,8,128]{3,2,1,0:T(8,128)} %state_ref.7, f32[8,128]{1,0:T(8,128)} %diff_ref.5, s32[8,128]{1,0:T(8,128)} %wet_ref.5, f32[8,128]{1,0:T(8,128)} %get-tuple-element.24.slotmap_ref, f32[260,4,128]{2,1,0:T(4,128)} %copy-done, f32[260,4,128]{2,1,0:T(4,128)} %copy-done.1, ...), custom_call_target="tpu_custom_call" | custom-call | tf_op jit(solution)/shard_map/pack_y/pallas_call | solution.py:539
  33.7 3.4 %collective-permute-start.2 = (f32[264,128]{1,0:T(8,128)}, f32[264,128]{1,0:T(8,128)S(1)}, u32[]{:S(2)}, u32[]{:S(2)}) collective-permute-start(f32[264,128]{1,0:T(8,128)} %get-tuple-element.26), channel_id=1, source_target_pairs={{0,1},{1,2},{2,3},{3,4},{4,5},{5,6},{6,7},{7,8},{8,9},{9,10},{10,1... | collective-permute-start | bytes 405512 | tf_op jit(solution)/shard_map/ppermute | solution.py:504
  37.0 2.5 %collective-permute-start.3 = (f32[264,128]{1,0:T(8,128)}, f32[264,128]{1,0:T(8,128)S(1)}, u32[]{:S(2)}, u32[]{:S(2)}) collective-permute-start(f32[264,128]{1,0:T(8,128)} %get-tuple-element.27), channel_id=1, source_target_pairs={{1,0},{2,1},{3,2},{4,3},{5,4},{6,5},{7,6},{8,7},{9,8},{10,9},{11,1... | collective-permute-start | bytes 405512 | tf_op jit(solution)/shard_map/ppermute | solution.py:505
  39.5 1.9 %all-to-all-done = f32[256,1,128]{2,1,0:T(1,128)S(1)} async-done(((f32[256,1,128]{2,1,0:T(1,128)}), f32[256,1,128]{2,1,0:T(1,128)S(1)}, u32[]{:S(2)}, u32[]{:S(2)}) %all-to-all-start) | async-done | bytes 131104 | tf_op jit(solution)/shard_map/all_to_all | solution.py:510
  41.4 0.1 collective-permute-done.2.left_ref
  41.5 3.0 %collective-permute-done.3.right_ref = f32[264,128]{1,0:T(8,128)S(1)} collective-permute-done((f32[264,128]{1,0:T(8,128)}, f32[264,128]{1,0:T(8,128)S(1)}, u32[]{:S(2)}, u32[]{:S(2)}) %collective-permute-start.3) | collective-permute-done | bytes 135200 | tf_op jit(solution)/shard_map/ppermute | solution.py:505
  44.5 0.0 copy-done.2
  44.5 0.6 copy-done.4
  45.1 3.1 %top.1 = (f32[4,8,128]{2,1,0:T(8,128)}, f32[8,128]{1,0:T(8,128)}, f32[5,16,256]{2,1,0:T(8,128)}, f32[256,128]{1,0:T(8,128)}) custom-call(s32[3]{0:T(128)} %pad_add_fusion.pos_ref, f32[4,60,8,128]{3,2,1,0:T(8,128)} %state_ref.7, f32[8,128]{1,0:T(8,128)} %diff_ref.5, s32[8,128]{1,0:T(8,128)} %wet_ref.5, f32[8,128]{1,0:T(8,128)} %get-tuple-element.24.slotmap_ref, ...), custom_call_target="tpu_custom_call" | custom-call | tf_op jit(solution)/shard_map/top/pallas_call | solution.py:549
  48.3 15.1 %all-to-all-start.1 = ((f32[256,1,128]{2,1,0:T(1,128)}), f32[256,1,128]{2,1,0:T(1,128)S(1)}, u32[]{:S(2)}, u32[]{:S(2)}) async-start(f32[256,1,128]{2,1,0:T(1,128)} %bitcast.26), calls=%async_computation.1 | async-start | bytes 262144 | tf_op jit(solution)/shard_map/all_to_all | solution.py:510
  63.4 0.6 slice.8.left_ref
  64.1 0.6 slice.9.right_ref
  64.7 10.6 %all-to-all-done.1 = f32[256,1,128]{2,1,0:T(1,128)S(1)} async-done(((f32[256,1,128]{2,1,0:T(1,128)}), f32[256,1,128]{2,1,0:T(1,128)S(1)}, u32[]{:S(2)}, u32[]{:S(2)}) %all-to-all-start.1) | async-done | bytes 131104 | tf_op jit(solution)/shard_map/all_to_all | solution.py:510
  75.3 0.7 copy-done.7
  76.0 4.9 %ice.1 = (f32[256,128]{1,0:T(8,128)}, f32[2,128,128]{2,1,0:T(8,128)}, f32[2,128,128]{2,1,0:T(8,128)}, f32[2,128,128]{2,1,0:T(8,128)}, f32[2,128,128]{2,1,0:T(8,128)}, /*index=5*/f32[2,128,128]{2,1,0:T(8,128)}) custom-call(s32[3]{0:T(128)} %pad_add_fusion.pos_ref, s32[128,4]{1,0:T(8,128)} %bitcast.20, f32[256,128]{1,0:T(8,128)} %bitcast.22, ...), custom_call_target="tpu_custom_call" | custom-call | tf_op jit(solution)/shard_map/ice/pallas_call | solution.py:567
  80.9 6.5 %all-to-all-start.2 = ((f32[256,1,128]{2,1,0:T(1,128)}), f32[256,1,128]{2,1,0:T(1,128)S(1)}, u32[]{:S(2)}, u32[]{:S(2)}) async-start(f32[256,1,128]{2,1,0:T(1,128)} %bitcast.25), calls=%async_computation.2 | async-start | bytes 262144 | tf_op jit(solution)/shard_map/all_to_all | solution.py:510
  87.4 25.9 %bulk.1 = f32[4,60,8,128]{3,2,1,0:T(8,128)} custom-call(f32[4,60,8,128]{3,2,1,0:T(8,128)} %state_ref.7, f32[260,4,128]{2,1,0:T(4,128)} %copy-done, f32[260,4,128]{2,1,0:T(4,128)} %copy-done.1, f32[264,128]{1,0:T(8,128)} %copy-done.2, f32[264,128]{1,0:T(8,128)} %copy-done.4, f32[5,16,256]{2,1,0:T(8,128)} %get-tuple-element.28.weight_ref, ...), custom_call_target="tpu_custom_call" | custom-call | tf_op jit(solution)/shard_map/bulk/pallas_call | solution.py:557
  113.3 0.0 all-to-all-done.2
  113.3 0.6 copy-done.6
  113.9 2.4 %update.1 = (f32[2,128,128]{2,1,0:T(8,128)}, f32[2,128,128]{2,1,0:T(8,128)}) custom-call(f32[256,128]{1,0:T(8,128)} %bitcast.21, f32[2,128,128]{2,1,0:T(8,128)} %guess_ref.1, f32[2,128,128]{2,1,0:T(8,128)} %get-tuple-element.33.res_ref, f32[2,128,128]{2,1,0:T(8,128)} %get-tuple-element.34.z_ref, f32[2,128,128]{2,1,0:T(8,128)} %get-tuple-element.35.y_ref, ...), custom_call_target="tpu_custom_call" | custom-call | tf_op jit(solution)/shard_map/update/pallas_call | solution.py:576
  (11 shorter events, 0.0 us)
Async XLA Ops:
  5.1 24.4 %collective-permute-start = (f32[260,4,128]{2,1,0:T(4,128)}, f32[260,4,128]{2,1,0:T(4,128)S(1)}, u32[]{:S(2)}, u32[]{:S(2)}) collective-permute-start(f32[260,4,128]{2,1,0:T(4,128)} %get-tuple-element.22), channel_id=1, source_target_pairs={{0,16},{16,32},{32,48},{48,64},{64,80},{80,96},{96,112},{112,128},... | collective-permute-start | bytes 1597448 | tf_op jit(solution)/shard_map/ppermute | solution.py:504
  8.9 20.6 %collective-permute-start.1 = (f32[260,4,128]{2,1,0:T(4,128)}, f32[260,4,128]{2,1,0:T(4,128)S(1)}, u32[]{:S(2)}, u32[]{:S(2)}) collective-permute-start(f32[260,4,128]{2,1,0:T(4,128)} %get-tuple-element.23), channel_id=1, source_target_pairs={{16,0},{32,16},{48,32},{64,48},{80,64},{96,80},{112,96},{128,112},... | collective-permute-start | bytes 1597448 | tf_op jit(solution)/shard_map/ppermute | solution.py:505
  13.0 28.4 %all-to-all-start = ((f32[256,1,128]{2,1,0:T(1,128)}), f32[256,1,128]{2,1,0:T(1,128)S(1)}, u32[]{:S(2)}, u32[]{:S(2)}) async-start(f32[256,1,128]{2,1,0:T(1,128)} %bitcast.23), calls=%async_computation | async-start | bytes 262144 | tf_op jit(solution)/shard_map/all_to_all | solution.py:510
  29.5 0.8 copy-start
  29.5 1.0 copy-start.1
  33.7 7.8 %collective-permute-start.2 = (f32[264,128]{1,0:T(8,128)}, f32[264,128]{1,0:T(8,128)S(1)}, u32[]{:S(2)}, u32[]{:S(2)}) collective-permute-start(f32[264,128]{1,0:T(8,128)} %get-tuple-element.26), channel_id=1, source_target_pairs={{0,1},{1,2},{2,3},{3,4},{4,5},{5,6},{6,7},{7,8},{8,9},{9,10},{10,1... | collective-permute-start | bytes 405512 | tf_op jit(solution)/shard_map/ppermute | solution.py:504
  37.0 7.4 %collective-permute-start.3 = (f32[264,128]{1,0:T(8,128)}, f32[264,128]{1,0:T(8,128)S(1)}, u32[]{:S(2)}, u32[]{:S(2)}) collective-permute-start(f32[264,128]{1,0:T(8,128)} %get-tuple-element.27), channel_id=1, source_target_pairs={{1,0},{2,1},{3,2},{4,3},{5,4},{6,5},{7,6},{8,7},{9,8},{10,9},{11,1... | collective-permute-start | bytes 405512 | tf_op jit(solution)/shard_map/ppermute | solution.py:505
  41.4 3.1 %copy-start.8 = (f32[256,1,128]{2,1,0:T(1,128)}, f32[256,1,128]{2,1,0:T(1,128)S(1)}, u32[]{:S(2)}) copy-start(f32[256,1,128]{2,1,0:T(1,128)S(1)} %all-to-all-done) | copy-start | bytes 393220
  41.5 3.0 %copy-start.2 = (f32[264,128]{1,0:T(8,128)}, f32[264,128]{1,0:T(8,128)S(1)}, u32[]{:S(2)}) copy-start(f32[264,128]{1,0:T(8,128)S(1)} %collective-permute-done.2.left_ref) | copy-start | bytes 405508
  44.5 0.7 copy-start.4
  48.3 15.1 %copy-start.3 = (f32[264,128]{1,0:T(8,128)S(1)}, f32[264,128]{1,0:T(8,128)}, u32[]{:S(2)}) copy-start(f32[264,128]{1,0:T(8,128)} %copy-done.2) | copy-start | bytes 405508
  48.3 15.8 %copy-start.5 = (f32[264,128]{1,0:T(8,128)S(1)}, f32[264,128]{1,0:T(8,128)}, u32[]{:S(2)}) copy-start(f32[264,128]{1,0:T(8,128)} %copy-done.4) | copy-start | bytes 405508
  48.3 27.0 %all-to-all-start.1 = ((f32[256,1,128]{2,1,0:T(1,128)}), f32[256,1,128]{2,1,0:T(1,128)S(1)}, u32[]{:S(2)}, u32[]{:S(2)}) async-start(f32[256,1,128]{2,1,0:T(1,128)} %bitcast.26), calls=%async_computation.1 | async-start | bytes 262144 | tf_op jit(solution)/shard_map/all_to_all | solution.py:510
  75.3 0.7 copy-start.7
  80.9 32.4 %all-to-all-start.2 = ((f32[256,1,128]{2,1,0:T(1,128)}), f32[256,1,128]{2,1,0:T(1,128)S(1)}, u32[]{:S(2)}, u32[]{:S(2)}) async-start(f32[256,1,128]{2,1,0:T(1,128)} %bitcast.25), calls=%async_computation.2 | async-start | bytes 262144 | tf_op jit(solution)/shard_map/all_to_all | solution.py:510
  113.3 0.7 copy-start.6

commit v2 on v1

v2 whole, which is shorter than its diff:
```python
import jax
import jax.numpy as jnp
from jax import lax
from jax.experimental import pallas as pl
from jax.experimental.pallas import tpu as pltpu
from jax.sharding import Mesh
from jax.sharding import PartitionSpec as P


NSUB = 4
GY = ("gy_0", "gy_1")
XAXES = ("grp", "gx")
ALL = ("grp", "gx", "gy_0", "gy_1")
LEAD = 72
DEEP = 960
SIDE_Y = 248
F32 = jnp.float32
BF16 = jnp.bfloat16
I32 = jnp.int32


def iota(shape, dim):
    return lax.broadcasted_iota(I32, shape, dim)


def split3(x):
    high = x.astype(BF16)
    rest = x - high.astype(F32)
    mid = rest.astype(BF16)
    low = (rest - mid.astype(F32)).astype(BF16)
    return high, mid, low


def onehot(hit):
    return jnp.where(hit, 1.0, 0.0).astype(BF16)


def dot_tn(a, b):
    return lax.dot_general(a, b, (((0,), (0,)), ((), ())), preferred_element_type=F32)


def dot_nt(a, b):
    return lax.dot_general(a, b, (((1,), (1,)), ((), ())), preferred_element_type=F32)


def spread(table, half, out_ref):
    row = iota((128, 128), 0) & 15
    group = iota((128, 128), 1) >> 2
    after = pltpu.roll(table, 127, 0)
    before = pltpu.roll(table, 1, 0)
    parts = []
    for dx in range(3):
        part = jnp.where((group == 3 * dx) & (row > 0), before, 0.0)
        part = jnp.where(group == 3 * dx + 1, table, part)
        part = jnp.where((group == 3 * dx + 2) & (row < 15), after, part)
        parts.append(part)
    none = jnp.zeros((16, 128), F32)
    own = parts[1] + jnp.concatenate([none, parts[0][:112]], 0)
    own = own + jnp.concatenate([parts[2][16:], none], 0)
    first = jnp.where(half == 0, parts[0][112:], 0.0)
    last = jnp.where(half == 1, parts[2][:16], 0.0)
    out_ref[pl.ds(half * 128, 128), :] = own
    out_ref[pl.ds((1 - half) * 128, 128), :] = jnp.concatenate(
        [first, jnp.zeros((96, 128), F32), last], 0
    )


def columns_of(owner_ref):
    node = owner_ref[...].astype(F32)
    return jnp.transpose(jnp.concatenate([node, node], 0)).astype(I32)


def draft_kernel(owner_ref, thick_ref, out_ref):
    lane = iota((128, 128), 1)
    parts = split3(thick_ref[...])
    node = columns_of(owner_ref)
    table = jnp.zeros((128, 128), F32)
    for s in range(4):
        column = node[:, s : s + 1]
        pick = onehot(lane == (column >> 7))
        rows = jnp.dot(pick, parts[0], preferred_element_type=F32)
        rows = rows + jnp.dot(pick, parts[1], preferred_element_type=F32)
        rows = rows + jnp.dot(pick, parts[2], preferred_element_type=F32)
        value = jnp.sum(jnp.where(lane == (column & 127), rows, 0.0), 1, keepdims=True)
        table = jnp.where((lane & 3) == s, 0.9 * value, table)
    spread(table, lax.axis_index("grp"), out_ref)


def ice_fields(refs):
    thick, visc, fric, ground, coup, drive, guess = refs
    return (
        lambda at: thick[at],
        lambda at: visc[at],
        lambda at: fric[at] * ground[at].astype(F32),
        lambda at: coup[at],
        lambda at: drive[(0,) + at],
        lambda at: drive[(1,) + at],
        lambda at: guess[(0,) + at],
        lambda at: guess[(1,) + at],
    )


WHOLE = (slice(None), slice(None))


def pack_y_kernel(
    state_ref, diff_ref, wet_ref, col_ref, slot_ref, owner_ref,
    thick, visc, fric, ground, coup, drive, guess,
    side_ref, slotmap_ref, nodemap_ref, lead_ref,
):
    col = col_ref[...]
    slot = slot_ref[...]
    hit = iota((8, 256), 0) == (col >> 7)
    peer = jnp.where(hit, ((slot >> 2) + 1).astype(F32), 0.0)
    which = jnp.where(hit, (slot & 3).astype(F32), 0.0)
    lanes = onehot(iota((128, 256), 0) == (col & 127))
    both = dot_nt(jnp.concatenate([peer, which], 0).astype(BF16), lanes)
    slotmap = jnp.where(both[:8] > 0.5, 4.0 * both[:8] + both[8:] - 3.0, 0.0)
    slotmap_ref[...] = slotmap

    node = columns_of(owner_ref)
    lane = iota((128, 128), 1)
    number = iota((128, 128), 0).astype(F32) + 1.0
    peers = []
    whichs = []
    cols = []
    for s in range(4):
        column = node[:, s : s + 1]
        hit = lane == (column >> 7)
        peers.append(jnp.where(hit, number, 0.0).astype(BF16))
        whichs.append(jnp.where(hit, float(s), 0.0).astype(BF16))
        cols.append(onehot(lane == (column & 127)))
    cols = jnp.concatenate(cols, 0)
    peer = dot_tn(jnp.concatenate(peers, 0), cols)
    which = dot_tn(jnp.concatenate(whichs, 0), cols)
    nodemap_ref[...] = jnp.where(peer > 0.5, 4.0 * peer + which - 3.0, 0.0)

    for f in range(4):
        lead_ref[8 * f : 8 * f + 8] = state_ref[480 * f : 480 * f + 8]
    lead_ref[32:40] = diff_ref[...]
    lead_ref[40:48] = wet_ref[...].astype(F32)
    lead_ref[48:56] = slotmap
    lead_ref[56:64] = jnp.zeros((8, 128), F32)

    place = iota((8, 128), 1) >> 3

    def edges(get):
        acc = jnp.zeros((8, 128), F32)
        for r in range(8):
            acc = jnp.where(place == r + 4, pltpu.roll(get(r), (8 * (r + 4) + 4) % 128, 1), acc)
        return acc

    side_ref[0:8] = edges(lambda r: lead_ref[pl.ds(r, 8, stride=8), :])

    def group(g, carry):
        at = pl.multiple_of(g * 64, 64)
        side_ref[pl.ds(pl.multiple_of(8 + 8 * g, 8), 8), :] = edges(
            lambda r: state_ref[pl.ds(at + r, 8, stride=8), :]
        )
        return carry

    lax.fori_loop(0, 30, group, 0)

    gets = ice_fields((thick, visc, fric, ground, coup, drive, guess))
    gets = gets + (lambda at: nodemap_ref[...],)
    place = lane >> 3
    acc = jnp.zeros((128, 128), F32)
    for a, get in enumerate(gets):
        acc = jnp.where(place == a, pltpu.roll(get(WHOLE), 8 * a + 4, 1), acc)
    side_ref[SIDE_Y : SIDE_Y + 128] = acc


def merged(left, right):
    return jnp.where((iota(left.shape, 1) & 4) == 0, left, right)


def pack_x_kernel(
    lead_ref, nodemap_ref, left_ref, right_ref,
    thick, visc, fric, ground, coup, drive, guess,
    up_ref, down_ref,
):
    for i in range(8):
        up_ref[4 * i : 4 * i + 4] = lead_ref[8 * i + 4 : 8 * i + 8]
        down_ref[4 * i : 4 * i + 4] = lead_ref[8 * i : 8 * i + 4]
    top = (pl.ds(0, 4), slice(None))
    end = (pl.ds(124, 4), slice(None))
    gets = ice_fields((thick, visc, fric, ground, coup, drive, guess))
    for a, get in enumerate(gets):
        up_ref[32 + 4 * a : 36 + 4 * a] = get(end)
        down_ref[32 + 4 * a : 36 + 4 * a] = get(top)
    up_ref[64:68] = nodemap_ref[124:128]
    down_ref[64:68] = nodemap_ref[0:4]
    up_ref[68:72] = merged(left_ref[SIDE_Y + 124 : SIDE_Y + 128], right_ref[SIDE_Y + 124 : SIDE_Y + 128])
    down_ref[68:72] = merged(left_ref[SIDE_Y : SIDE_Y + 4], right_ref[SIDE_Y : SIDE_Y + 4])
    side = merged(left_ref[0:8], right_ref[0:8])
    up_ref[LEAD : LEAD + 8] = side
    down_ref[LEAD : LEAD + 8] = side


def pack_deep_kernel(state_ref, left_ref, right_ref, up_ref, down_ref):
    def group(g, carry):
        at = pl.multiple_of(g * 64, 64)
        to = pl.multiple_of(g * 32, 32)
        for r in range(4):
            up_ref[pl.ds(to + r, 8, stride=4), :] = state_ref[pl.ds(at + 4 + r, 8, stride=8), :]
            down_ref[pl.ds(to + r, 8, stride=4), :] = state_ref[pl.ds(at + r, 8, stride=8), :]
        return carry

    lax.fori_loop(0, 30, group, 0)
    side = merged(left_ref[8:SIDE_Y], right_ref[8:SIDE_Y])
    up_ref[DEEP : DEEP + 240] = side
    down_ref[DEEP : DEEP + 240] = side


def whole_side(left, right, lo, hi):
    lane = iota(left.shape, 1)
    far = pltpu.roll(jnp.where(lane < 64, hi, lo), 64, 1)
    return jnp.where((lane < 32) | (lane >= 96), far, merged(left, right))


def turn(x, shift, axis):
    return pltpu.roll(x, shift % x.shape[axis], axis)


def lookup(parts, owner, lane_of):
    pick = onehot(iota((256, 128), 0) == owner)
    found = jnp.dot(parts, pick, preferred_element_type=F32)
    found = found[0:48] + found[48:96] + found[96:144]
    return jnp.sum(jnp.where(iota((48, 128), 0) == lane_of, found, 0.0), 0, keepdims=True)


def table_parts(table):
    turned = jnp.transpose(table)[0:48]
    return jnp.concatenate(split3(turned), 0)


def decode(code, half, group):
    number = code.astype(I32) - 1
    owner = jnp.where(number >= 0, half * 128 + (number >> 2), -1)
    return owner, 4 * group + (number & 3)


def pack_rows(x):
    lane = iota((16, 128), 1)
    moved = jnp.where(lane < 8, pltpu.roll(x, 4, 1), 0.0)
    moved = pltpu.roll(moved, 0, 1, stride=8, stride_axis=0)
    return jnp.sum(moved, 0, keepdims=True)


def unpack_rows(row):
    lane = iota((16, 128), 1)
    turned = [row] + [pltpu.roll(row, 128 - 8 * r, 1) for r in range(1, 16)]
    moved = jnp.where(lane < 8, jnp.concatenate(turned, 0), 0.0)
    return pltpu.roll(moved, 124, 1)


def halves():
    half = lax.axis_index("grp")
    bx = half * 8 + lax.axis_index("gx")
    return half, jnp.maximum(bx - 1, 0) >> 3, jnp.minimum(bx + 1, 15) >> 3


def top_kernel(
    lead_ref, lo_ref, hi_ref, left_ref, right_ref, table_ref,
    top_ref, melt_ref, weight_ref, send_ref, turn_ref,
):
    half, half_lo, half_hi = halves()
    side = whole_side(
        left_ref[0:8], right_ref[0:8], lo_ref[LEAD : LEAD + 8], hi_ref[LEAD : LEAD + 8]
    )
    for c in range(16):
        p = (c + 4) % 16
        turn_ref[8 * c : 8 * c + 8] = pltpu.roll(side, (128 - 8 * p - 4) % 128, 1)
    lane = iota((16, 128), 1)
    edge = (lane < 4) | (lane >= 124)

    def padded(i):
        centre = jnp.concatenate(
            [lead_ref[8 * i : 8 * i + 8], hi_ref[4 * i : 4 * i + 4], lo_ref[4 * i : 4 * i + 4]], 0
        )
        edges = jnp.where(edge, turn_ref[pl.ds(i, 16, stride=8), :], 0.0)
        return jnp.concatenate([centre, edges], 1)

    fields = [padded(f) for f in range(4)]
    diff = padded(4)
    wet = padded(5)
    code = padded(6)
    weights = []
    for axis, shift in ((0, -1), (0, 1), (1, -1), (1, 1)):
        weights.append(0.5 * (diff + turn(diff, shift, axis)) * wet * turn(wet, shift, axis))
    keep = 1.0 - (weights[0] + weights[1] + weights[2] + weights[3])
    for j, w in enumerate(weights + [keep]):
        centre = w[:, 0:128]
        weight_ref[16 * j : 16 * j + 12] = jnp.concatenate([w[12:16, 0:128], w[0:8, 0:128]], 0)
        weight_ref[16 * j + 12 : 16 * j + 16] = w[8:12, 0:128]
        east = jnp.where(lane < 4, pltpu.roll(centre, 4, 1), pltpu.roll(w[:, 128:256], 4, 1))
        west = jnp.where(lane < 4, pltpu.roll(w[:, 128:256], 4, 1), pltpu.roll(centre, 4, 1))
        for k, strip in enumerate((east, west)):
            strip = jnp.where(lane < 8, strip, 0.0)
            strip = jnp.sum(pltpu.roll(strip, 0, 1, stride=8, stride_axis=0), 0, keepdims=True)
            weight_ref[80 + 2 * j + k : 81 + 2 * j + k] = pltpu.roll(strip, 32, 1)
    weight_ref[90:96] = jnp.zeros((6, 128), F32)

    row = iota((16, 128), 0)
    half_at = jnp.where(row < 8, half, jnp.where(row < 12, half_hi, half_lo))
    dx = jnp.where(row < 8, 1, jnp.where(row < 12, 2, 0))
    owner, lane_of = decode(code[:, 0:128], half_at, 3 * dx + 1)
    flat = iota((1, 128), 1)
    place = flat >> 3
    half_at = jnp.where(place < 4, half_lo, jnp.where(place < 12, half, half_hi))
    dx = jnp.where(place < 4, 0, jnp.where(place < 12, 1, 2))
    dy = jnp.where((flat & 4) == 0, 0, 2)
    side_owner, side_lane = decode(side[6:7], half_at, 3 * dx + dy)
    parts = table_parts(table_ref[...])
    none = jnp.zeros((1, 128), F32)
    found = [
        none if r in (11, 12) else lookup(parts, owner[r : r + 1], lane_of[r : r + 1]) for r in range(16)
    ]
    side_found = lookup(parts, side_owner, side_lane)
    turned = []
    for c in range(16):
        p = (c + 4) % 16
        turned.append(pltpu.roll(side_found, (128 - 8 * p - 4) % 128, 1))
    edges = jnp.where(edge, jnp.concatenate(turned, 0), 0.0)
    draft = jnp.concatenate([jnp.concatenate(found, 0), edges], 1)
    cover = jnp.where(code > 0.5, 1.0, 0.0)

    total = jnp.zeros((8, 128), F32)
    for _ in range(NSUB):
        temp, salt, east, north = fields
        speed = jnp.sqrt(east * east + north * north + 0.01)
        freezing = -0.5 * salt + 0.3 * draft - 0.2
        melt = 0.5 * cover * (temp - freezing) * speed
        drag = 0.05 * cover * speed
        total = total + melt[0:8, 0:128]
        loss = (0.3 * melt, 0.2 * melt, drag * east, drag * north)
        changed = []
        for f in range(4):
            x = fields[f]
            flux = weights[0] * (turn(x, -1, 0) - x) + weights[1] * (turn(x, 1, 0) - x)
            flux = flux + weights[2] * (turn(x, -1, 1) - x) + weights[3] * (turn(x, 1, 1) - x)
            changed.append(x + flux - loss[f])
        fields = changed
    for f in range(4):
        top_ref[8 * f : 8 * f + 8] = fields[f][0:8, 0:128]
    mean = total * (1.0 / NSUB)
    melt_ref[...] = mean

    number = lead_ref[48:56].astype(I32) - 1
    peers = []
    values = []
    for r in range(8):
        at = number[r : r + 1]
        peers.append(onehot(iota((128, 128), 0) == (at >> 2)))
        values.append(jnp.where((iota((128, 128), 0) & 3) == (at & 3), mean[r : r + 1], 0.0))
    peers = jnp.concatenate(peers, 1)
    values = jnp.concatenate(split3(jnp.concatenate(values, 1)), 0)
    table = dot_nt(peers, values)
    spread(table[:, 0:128] + table[:, 128:256] + table[:, 256:384], half, send_ref)


def bulk_kernel(
    state_ref, lo_ref, hi_ref, left_ref, right_ref, weight_ref, top_ref, out_ref, wide_ref,
):
    lane = iota((8, 128), 1)
    outer = (lane & 4) == 0

    for k in range(90):
        wide_ref[8 * k : 8 * k + 8] = jnp.broadcast_to(weight_ref[k : k + 1], (8, 128))

    def weight(k):
        return wide_ref[8 * k : 8 * k + 8]

    def group(g, carry):
        at = pl.multiple_of(g * 64, 64)
        far = pl.multiple_of(g * 32, 32)
        side = pl.multiple_of(8 * g, 8)
        x = [lo_ref[pl.ds(far + r, 8, stride=4), :] for r in range(4)]
        x = x + [state_ref[pl.ds(at + r, 8, stride=8), :] for r in range(8)]
        x = x + [hi_ref[pl.ds(far + r, 8, stride=4), :] for r in range(4)]
        own = jnp.zeros((8, 128), F32)
        for p in range(16):
            own = jnp.where((lane >> 3) == p, pltpu.roll(x[p], (8 * p + 4) % 128, 1), own)
        near = whole_side(
            left_ref[pl.ds(pl.multiple_of(side + 8, 8), 8), :],
            right_ref[pl.ds(pl.multiple_of(side + 8, 8), 8), :],
            lo_ref[pl.ds(pl.multiple_of(side + DEEP, 8), 8), :],
            hi_ref[pl.ds(pl.multiple_of(side + DEEP, 8), 8), :],
        )
        strips = [jnp.where(outer, own, near), jnp.where(outer, near, own)]
        for substep in range(NSUB):
            ends = jnp.where((lane & 7) == 4, strips[0], strips[1])
            new = [None] * 16
            for p in range(substep + 1, 15 - substep):
                end = pltpu.roll(ends, (128 - 8 * p - 4) % 128, 1)
                here = x[p]
                after = pltpu.roll(jnp.where(lane == 0, end, here), 127, 1)
                before = pltpu.roll(jnp.where(lane == 127, end, here), 1, 1)
                y = weight(64 + p) * here + weight(p) * x[p + 1] + weight(16 + p) * x[p - 1]
                new[p] = y + weight(32 + p) * after + weight(48 + p) * before
            if substep + 1 < NSUB:
                moved = []
                for k in range(2):
                    s = strips[k]
                    y = weight(88 + k) * s + weight(80 + k) * pltpu.roll(s, 120, 1)
                    y = y + weight(82 + k) * pltpu.roll(s, 8, 1)
                    moved.append(y + weight(84 + k) * pltpu.roll(s, 127, 1) + weight(86 + k) * pltpu.roll(s, 1, 1))
                strips = moved
            x = new
        for r in range(8):
            out_ref[pl.ds(at + r, 8, stride=8), :] = x[r + 4]
        return carry

    lax.fori_loop(0, 30, group, 0, unroll=2)
    for f in range(4):
        out_ref[480 * f : 480 * f + 8] = top_ref[8 * f : 8 * f + 8]


def two_sum(a, b):
    s = a + b
    t = s - a
    return s, (a - (s - t)) + (b - t)


def two_product(a, b):
    def split(v):
        c = 4097.0 * v
        high = c - (c - v)
        return high, v - high

    p = a * b
    a1, a2 = split(a)
    b1, b2 = split(b)
    return p, ((a1 * b1 - p) + a1 * b2 + a2 * b1) + a2 * b2


def add_pair(a, b):
    s, e = two_sum(a[0], b[0])
    e = e + (a[1] + b[1])
    return two_sum(s, e)


def less_scaled(a, k, b):
    p, e = two_product(k, b[0])
    return add_pair(a, (-p, -(e + k * b[1])))


def fold(pair, axis, sizes):
    for size in sizes:
        turned = tuple(pltpu.roll(v, size, axis) for v in pair)
        pair = add_pair(pair, turned)
    return pair


def tiles_sum(x, low=None):
    total = x[0:8]
    error = jnp.zeros((8, 128), F32) if low is None else low[0:8]
    for r in range(8, x.shape[0], 8):
        total, e = two_sum(total, x[r : r + 8])
        error = error + e
        if low is not None:
            error = error + low[r : r + 8]
    return fold(two_sum(total, error), 0, (4, 2, 1))


def ice_kernel(
    owner_ref, table_ref, lo_ref, hi_ref, left_ref, right_ref,
    thick, visc, fric, ground, coup, drive, guess, nodemap_ref,
    send_ref, res_ref, z_ref, y_ref, w_ref, v_ref,
):
    half, half_lo, half_hi = halves()
    side = merged(left_ref[SIDE_Y : SIDE_Y + 128], right_ref[SIDE_Y : SIDE_Y + 128])
    side = jnp.concatenate([side, hi_ref[68:72], lo_ref[68:72]], 0)
    gets = ice_fields((thick, visc, fric, ground, coup, drive, guess))
    gets = gets + (lambda at: nodemap_ref[...],)
    lane = iota((136, 128), 1)
    edge = (lane < 4) | (lane >= 124)

    def padded(a):
        at = 32 + 4 * a
        centre = jnp.concatenate([gets[a](WHOLE), hi_ref[at : at + 4], lo_ref[at : at + 4]], 0)
        edges = jnp.where(edge, pltpu.roll(side, (128 - 8 * a - 4) % 128, 1), 0.0)
        return jnp.concatenate([centre, edges], 1)

    table = table_ref[...]
    mine = table_ref[pl.ds(pl.multiple_of(half * 128, 128), 128), :]
    node = columns_of(owner_ref)
    lane = iota((128, 128), 1)
    rows = []
    cols = []
    for s in range(4):
        column = node[:, s : s + 1]
        rows.append(onehot(lane == (column >> 7)))
        cols.append(jnp.where(lane == (column & 127), mine[:, 16 + s : 17 + s], 0.0))
    cols = jnp.concatenate(split3(jnp.concatenate(cols, 0)), 1)
    melt = dot_tn(jnp.concatenate(rows, 0), cols)
    melt = melt[:, 0:128] + melt[:, 128:256] + melt[:, 256:384]

    code = padded(8)
    row = iota((136, 256), 0)
    col = iota((136, 256), 1)
    half_at = jnp.where(row < 128, half, jnp.where(row < 132, half_hi, half_lo))
    dx = jnp.where(row < 128, 1, jnp.where(row < 132, 2, 0))
    dy = jnp.where(col < 128, 1, jnp.where(col < 192, 2, 0))
    owner, lane_of = decode(code, half_at, 3 * dx + dy)
    parts = table_parts(table)
    rim = [
        lookup(parts, owner[r : r + 1, :128], lane_of[r : r + 1, :128]) for r in range(128, 136)
    ]
    side_owner = (owner[:, 128:] + 1).astype(F32)
    side_lane = lane_of[:, 128:].astype(F32)
    spare = jnp.zeros((8, 128), F32)
    sides = []
    for block in range(9):
        if block < 8:
            piece_owner = side_owner[16 * block : 16 * block + 16]
            piece_lane = side_lane[16 * block : 16 * block + 16]
        else:
            piece_owner = jnp.concatenate([side_owner[128:136], spare], 0)
            piece_lane = jnp.concatenate([side_lane[128:136], spare], 0)
        at_owner = pack_rows(piece_owner).astype(I32) - 1
        at_lane = pack_rows(piece_lane).astype(I32)
        piece = unpack_rows(lookup(parts, at_owner, at_lane))
        sides.append(piece if block < 8 else piece[0:8])
    melt = jnp.concatenate([melt] + rim, 0)
    melt = jnp.concatenate([melt, jnp.concatenate(sides, 0)], 1)

    thickness = padded(0)
    inside = thickness > 0.0
    thinned = thickness * jnp.exp(-0.3 * melt)
    depth = padded(1) * thinned
    base = padded(2) + 0.2
    cross = 0.9 * base * padded(3)
    w_e = 0.5 * (depth + turn(depth, -1, 0))
    w_w = 0.5 * (depth + turn(depth, 1, 0))
    w_n = 0.5 * (depth + turn(depth, -1, 1))
    w_s = 0.5 * (depth + turn(depth, 1, 1))
    diagonal = w_e + w_w + w_n + w_s + base
    inverse = jnp.where(inside, 1.0 / diagonal, 0.0)

    def apply(pair):
        out = []
        for a in range(2):
            x = pair[a]
            beside = w_e * turn(x, -1, 0) + w_w * turn(x, 1, 0)
            beside = beside + w_n * turn(x, -1, 1) + w_s * turn(x, 1, 1)
            out.append(diagonal * x - beside + cross * pair[1 - a])
        return out

    first = [padded(6), padded(7)]
    image = apply(first)
    res = [padded(4 + a) * thinned - image[a] for a in range(2)]
    z = [res[a] * inverse for a in range(2)]
    y = apply(z)
    w = [y[a] * inverse for a in range(2)]
    v = apply(w)
    inner = (slice(0, 128), slice(0, 128))
    lane = iota((256, 128), 1)
    message = jnp.zeros((256, 128), F32)
    for k, (one, two) in enumerate(((res, z), (z, y), (y, w), (w, v))):
        product = jnp.concatenate([one[a][inner] * two[a][inner] for a in range(2)], 0)
        pair = fold(tiles_sum(product), 1, (64, 32, 16, 8, 4, 2, 1))
        message = jnp.where(lane == k, pair[0][0:1], message)
        message = jnp.where(lane == k + 4, pair[1][0:1], message)
    send_ref[...] = message
    for a in range(2):
        res_ref[a] = res[a][inner]
        z_ref[a] = z[a][inner]
        y_ref[a] = y[a][inner]
        w_ref[a] = w[a][inner]
        v_ref[a] = v[a][inner]


def update_kernel(sum_ref, guess_ref, res_ref, z_ref, y_ref, w_ref, v_ref, vel_ref, left_ref):
    got = sum_ref[...]
    pair = tiles_sum(got, pltpu.roll(got, 124, 1))
    norm, curve, mixed, far = ((pair[0][0:1, k : k + 1], pair[1][0:1, k : k + 1]) for k in range(4))
    step = norm[0] / curve[0]
    rest = less_scaled(norm, step, curve)
    along = less_scaled(curve, step, mixed)
    norm_next = (rest[0] - step * along[0]) + (rest[1] - step * along[1])
    ratio = norm_next / norm[0]
    curve_next = less_scaled(along, step, less_scaled(mixed, step, far))[0]
    curve_next = curve_next + 2.0 * ratio * along[0] + ratio * ratio * curve[0]
    step_next = norm_next / curve_next
    one = step + step_next * (1.0 + ratio)
    two = step_next * step
    for a in range(2):
        vel_ref[a] = guess_ref[a] + one * z_ref[a] - two * w_ref[a]
        left_ref[a] = res_ref[a] - one * y_ref[a] + two * v_ref[a]


def sds(*shape):
    return jax.ShapeDtypeStruct(shape, F32)


SMALL = 24 << 20


def near(*shape):
    return pltpu.VMEM(shape, F32)


def call(kernel, outs, *args, stay=(), limit=None, **kw):
    args = [x if any(x is y for y in stay) else here(x) for x in args]
    vmem = pl.BlockSpec(memory_space=pltpu.VMEM)
    return pl.pallas_call(
        kernel,
        in_specs=[vmem] * len(args),
        out_specs=[vmem] * len(outs),
        out_shape=outs,
        compiler_params=pltpu.CompilerParams(vmem_limit_bytes=limit),
        **kw,
    )(*args)


def here(x):
    return pltpu.with_memory_space_constraint(x, pltpu.VMEM)


def swap(up, down, axes):
    size = lax.axis_size(axes)
    forward = [(i, i + 1) for i in range(size - 1)]
    low = lax.ppermute(up, axes, forward)
    high = lax.ppermute(down, axes, [(b, a) for a, b in forward])
    return here(low), here(high)


def exchange(table):
    return here(lax.all_to_all(table, ALL, split_axis=0, concat_axis=0, tiled=True))


def shards(
    ocean_state, diffusivity, wet_mask, coast_column, coast_slot, owner_node,
    thickness, viscosity, friction, grounded, coupling, driving, first_guess,
):
    owner = owner_node[0, 0].T
    columns = coast_column.reshape(1, 256)
    slots = coast_slot.reshape(1, 256)
    ice = (thickness, viscosity, friction, grounded, coupling, driving, first_guess)
    state = ocean_state.reshape(1920, 128)
    given = (state, diffusivity, wet_mask, columns, slots, owner) + ice

    side, _, nodemap, lead = call(
        pack_y_kernel,
        [sds(SIDE_Y + 128, 128), near(8, 128), near(128, 128), near(64, 128)],
        state, diffusivity, wet_mask, columns, slots, owner, *ice,
        stay=given,
    )
    left, right = swap(side, side, GY)
    (send_draft,) = call(draft_kernel, [sds(256, 128)], owner, thickness, stay=given, limit=SMALL)
    up, down = call(
        pack_x_kernel,
        [sds(LEAD + 8, 128), sds(LEAD + 8, 128)],
        lead, nodemap, left, right, *ice,
        stay=given,
        limit=SMALL,
    )
    lo, hi = swap(up, down, XAXES)
    up, down = call(
        pack_deep_kernel,
        [sds(DEEP + 240, 128), sds(DEEP + 240, 128)],
        state, left, right,
        stay=given,
        limit=SMALL,
    )
    deep_lo, deep_hi = swap(up, down, XAXES)
    got_draft = exchange(send_draft)

    top, melt_mean, weights, send_melt = call(
        top_kernel,
        [sds(32, 128), sds(8, 128), sds(96, 128), sds(256, 128)],
        lead, lo, hi, left, right, got_draft,
        scratch_shapes=[pltpu.VMEM((128, 128), F32)],
        limit=SMALL,
    )
    got_melt = exchange(send_melt)
    (fields,) = call(
        bulk_kernel,
        [sds(1920, 128)],
        state, deep_lo, deep_hi, left, right, weights, top,
        stay=given + (weights, top),
        limit=SMALL,
        scratch_shapes=[pltpu.VMEM((720, 128), F32)],
    )

    pair = sds(2, 128, 128)
    send_sums, res, z, y, w, v = call(
        ice_kernel,
        [sds(256, 128), pair, pair, pair, pair, pair],
        owner, got_melt, lo, hi, left, right, *ice, nodemap,
    )
    got_sums = exchange(send_sums)
    pair = sds(2, 128, 128)
    velocity, residual = call(
        update_kernel, [pair, pair], got_sums, first_guess, res, z, y, w, v,
        stay=(first_guess, res, z, y, w, v), limit=SMALL,
    )
    return (fields.reshape(ocean_state.shape), melt_mean, velocity, residual)


def solution(mesh):
    split = Mesh(
        mesh.devices.reshape(mesh.shape["grp"], mesh.shape["gx"], 4, 4),
        ("grp", "gx", "gy_0", "gy_1"),
    )
    field = P(("grp", "gx"), GY)
    pair = P(None, ("grp", "gx"), GY)
    levels = P(None, None, ("grp", "gx"), GY)
    lists = P(("grp", "gx"), GY, None)
    placed = (levels, field, field, lists, lists, P(("grp", "gx"), GY, None, None))
    placed = placed + (field,) * 5 + (pair, pair)
    return jax.shard_map(
        shards,
        mesh=split,
        in_specs=placed,
        out_specs=(levels, field, pair, pair),
        check_vma=False,
    )
```

time: 118 us -> 122 us (1.034)
  the two profiles are of different devices: /device:TPU:8 before, /device:TPU:1 now
where the time goes in v2:
time: 122 us; the launch traced here: 121 us
  blocking collectives  46.9 us (38%)
  starting transfers between devices  38.6 us (32%)
  Pallas kernels  26.3 us (22%)
  waiting for transfers between devices  5.91 us (5%)
  local copies, waits for them, and re-layouts  2.77 us (2%)
    all_to_all x2, blocking collectives, exchange(): lax.all_to_all(table, ALL, split_axis=0, concat_axis=0, tiled=True)  46.9 us
    pallas_call x8, Pallas kernels, call(): pl.pallas_call(kernel, in_specs=[vmem] * len(args), out_specs=[vmem] * le...  26.3 us
    all_to_all x1, starting transfers between devices, exchange(): lax.all_to_all(table, ALL, split_axis=0, concat_axis=0, tiled=True)  17.5 us
    ppermute x3, starting transfers between devices, swap(): high = lax.ppermute(down, axes, [(b, a) for a, b in forward])  11.2 us
    ppermute x3, starting transfers between devices, swap(): low = lax.ppermute(up, axes, forward)  9.96 us
    ppermute x3, waiting for transfers between devices, swap(): high = lax.ppermute(down, axes, [(b, a) for a, b in forward])  3.67 us
    unnamed x28, local copies, waits for them, and re-layouts  2.77 us
  transfers between devices with their start and end apart: 7, of which 2 were waited for; matrix products, arithmetic and copies ran while one was open for 0% of the time, Pallas kernels for 8%

profile of v2, /device:TPU:1, one launch (start us, length us, event | category | flops | bytes accessed | tf_op | source)
XLA Modules:
  0.0 121.3 jit_solution(15445644170732868709)
XLA Ops:
  0.7 5.3 %shard_map.156 = (f32[376,128]{1,0:T(8,128)}, f32[8,128]{1,0:T(8,128)}, f32[128,128]{1,0:T(8,128)S(1)}, f32[64,128]{1,0:T(8,128)S(1)}) custom-call(f32[1920,128]{1,0:T(8,128)} %bitcast.19, f32[8,128]{1,0:T(8,128)} %diff_ref.1, s32[8,128]{1,0:T(8,128)} %wet_ref.1, s32[1,256]{1,0:T(1,128)} %bitcast.31, s32[1,256]{1,0:T(1,128)} %bitcast.32, s32[4,128]{1,0:T(4,128)} %bitcast.26, ...), custom_call_target="tpu_custom_call" | custom-call | tf_op jit(solution)/shard_map/pallas_call | solution.py:607
  6.0 1.3 %collective-permute-start.1 = (f32[376,128]{1,0:T(8,128)}, f32[376,128]{1,0:T(8,128)S(1)}, u32[]{:S(2)}, u32[]{:S(2)}) collective-permute-start(f32[376,128]{1,0:T(8,128)} %get-tuple-element.23), channel_id=1, source_target_pairs={{1,0},{2,1},{3,2},{4,3},{5,4},{6,5},{7,6},{8,7},{9,8},{10,9},{11,1... | collective-permute-start | bytes 577544 | tf_op jit(solution)/shard_map/ppermute | solution.py:625
  7.3 4.7 %collective-permute-start = (f32[376,128]{1,0:T(8,128)}, f32[376,128]{1,0:T(8,128)S(1)}, u32[]{:S(2)}, u32[]{:S(2)}) collective-permute-start(f32[376,128]{1,0:T(8,128)} %get-tuple-element.23), channel_id=1, source_target_pairs={{0,1},{1,2},{2,3},{3,4},{4,5},{5,6},{6,7},{7,8},{8,9},{9,10},{10,1... | collective-permute-start | bytes 577544 | tf_op jit(solution)/shard_map/ppermute | solution.py:624
  11.9 1.2 %shard_map.159 = f32[256,128]{1,0:T(8,128)} custom-call(s32[4,128]{1,0:T(4,128)S(1)} %bitcast.27, f32[128,128]{1,0:T(8,128)S(1)} %copy-done.3), custom_call_target="tpu_custom_call" | custom-call | tf_op jit(solution)/shard_map/pallas_call | solution.py:607
  13.2 17.5 %all-to-all-start = ((f32[256,1,128]{2,1,0:T(1,128)}), f32[256,1,128]{2,1,0:T(1,128)S(1)}, u32[]{:S(2)}, u32[]{:S(2)}) async-start(f32[256,1,128]{2,1,0:T(1,128)} %bitcast.7), calls=%async_computation | async-start | bytes 262144 | tf_op jit(solution)/shard_map/all_to_all | solution.py:630
  30.6 0.0 copy-start.1
  30.6 0.0 copy-start.2
  30.7 0.0 copy-start.4
  30.7 0.0 copy-start.5
  30.7 0.0 copy-start.6
  30.7 0.0 copy-start.7
  30.7 0.0 collective-permute-done.1.right_ref
  30.7 0.0 collective-permute-done.left_ref
  30.7 1.3 %shard_map.157 = (f32[1200,128]{1,0:T(8,128)}, f32[1200,128]{1,0:T(8,128)}) custom-call(f32[1920,128]{1,0:T(8,128)S(1)} %bitcast.20, f32[376,128]{1,0:T(8,128)S(1)} %collective-permute-done.left_ref, f32[376,128]{1,0:T(8,128)S(1)} %collective-permute-done.1.right_ref), custom_call_target="tpu_custom_call" | custom-call | tf_op jit(solution)/shard_map/pallas_call | solution.py:607
  32.1 3.4 %collective-permute-start.2 = (f32[1200,128]{1,0:T(8,128)}, f32[1200,128]{1,0:T(8,128)S(1)}, u32[]{:S(2)}, u32[]{:S(2)}) collective-permute-start(f32[1200,128]{1,0:T(8,128)} %get-tuple-element.24), channel_id=1, source_target_pairs={{0,16},{16,32},{32,48},{48,64},{64,80},{80,96},{96,112},{112,128},... | collective-permute-start | bytes 1843208 | tf_op jit(solution)/shard_map/ppermute | solution.py:624
  35.5 5.0 %collective-permute-start.3 = (f32[1200,128]{1,0:T(8,128)}, f32[1200,128]{1,0:T(8,128)}, u32[]{:S(2)}, u32[]{:S(2)}) collective-permute-start(f32[1200,128]{1,0:T(8,128)} %get-tuple-element.25), channel_id=1, source_target_pairs={{16,0},{32,16},{48,32},{64,48},{80,64},{96,80},{112,96},{128,112},... | collective-permute-start | bytes 1843208 | tf_op jit(solution)/shard_map/ppermute | solution.py:625
  40.6 1.9 %collective-permute-start.4 = (f32[80,128]{1,0:T(8,128)S(1)}, f32[80,128]{1,0:T(8,128)S(1)}, u32[]{:S(2)}, u32[]{:S(2)}) collective-permute-start(f32[80,128]{1,0:T(8,128)S(1)} %get-tuple-element.28), channel_id=1, source_target_pairs={{0,16},{16,32},{32,48},{48,64},{64,80},{80,96},{96,112},{112,128},... | collective-permute-start | bytes 122888 | tf_op jit(solution)/shard_map/ppermute | solution.py:624
  42.5 4.9 %collective-permute-start.5 = (f32[80,128]{1,0:T(8,128)S(1)}, f32[80,128]{1,0:T(8,128)S(1)}, u32[]{:S(2)}, u32[]{:S(2)}) collective-permute-start(f32[80,128]{1,0:T(8,128)S(1)} %get-tuple-element.29), channel_id=1, source_target_pairs={{16,0},{32,16},{48,32},{64,48},{80,64},{96,80},{112,96},{128,112},... | collective-permute-start | bytes 122888 | tf_op jit(solution)/shard_map/ppermute | solution.py:625
  47.4 2.2 %collective-permute-done.4.lo_ref = f32[80,128]{1,0:T(8,128)S(1)} collective-permute-done((f32[80,128]{1,0:T(8,128)S(1)}, f32[80,128]{1,0:T(8,128)S(1)}, u32[]{:S(2)}, u32[]{:S(2)}) %collective-permute-start.4) | collective-permute-done | bytes 40992 | tf_op jit(solution)/shard_map/ppermute | solution.py:624
  49.6 3.7 %collective-permute-done.5.hi_ref = f32[80,128]{1,0:T(8,128)S(1)} collective-permute-done((f32[80,128]{1,0:T(8,128)S(1)}, f32[80,128]{1,0:T(8,128)S(1)}, u32[]{:S(2)}, u32[]{:S(2)}) %collective-permute-start.5) | collective-permute-done | bytes 40992 | tf_op jit(solution)/shard_map/ppermute | solution.py:625
  53.3 0.0 all-to-all-done
  53.3 1.7 %shard_map.160 = (f32[32,128]{1,0:T(8,128)S(1)}, f32[8,128]{1,0:T(8,128)}, f32[96,128]{1,0:T(8,128)S(1)}, f32[256,128]{1,0:T(8,128)S(1)}) custom-call(f32[64,128]{1,0:T(8,128)S(1)} %get-tuple-element.26.lead_ref, f32[80,128]{1,0:T(8,128)S(1)} %collective-permute-done.4.lo_ref, f32[80,128]{1,0:T(8,128)S(1)} %collective-permute-done.5.hi_ref, ...), custom_call_target="tpu_custom_call" | custom-call | tf_op jit(solution)/shard_map/pallas_call | solution.py:607
  54.9 27.7 %all_to_all.33 = f32[256,1,128]{2,1,0:T(1,128)S(1)} all-to-all(f32[256,1,128]{2,1,0:T(1,128)S(1)} %bitcast.25), channel_id=1, replica_groups=mesh['grp'=2,'gx'=8,'gy_0'=4,'gy_1'=4] {'grp','gx','gy_0','gy_1'}, dimensions={0} | all-to-all | bytes 262144 | tf_op jit(solution)/shard_map/all_to_all | solution.py:630
  82.7 3.7 %shard_map.162 = (f32[256,128]{1,0:T(8,128)}, f32[2,128,128]{2,1,0:T(8,128)}, f32[2,128,128]{2,1,0:T(8,128)}, f32[2,128,128]{2,1,0:T(8,128)}, f32[2,128,128]{2,1,0:T(8,128)}, /*index=5*/f32[2,128,128]{2,1,0:T(8,128)}) custom-call(s32[4,128]{1,0:T(4,128)S(1)} %bitcast.28, f32[256,128]{1,0:T(8,128)S(1)} %bitcast.23, ...), custom_call_target="tpu_custom_call" | custom-call | tf_op jit(solution)/shard_map/pallas_call | solution.py:607
  86.4 19.2 %all_to_all.34 = f32[256,1,128]{2,1,0:T(1,128)S(1)} all-to-all(f32[256,1,128]{2,1,0:T(1,128)} %bitcast.30), channel_id=1, replica_groups=mesh['grp'=2,'gx'=8,'gy_0'=4,'gy_1'=4] {'grp','gx','gy_0','gy_1'}, dimensions={0} | all-to-all | bytes 262144 | tf_op jit(solution)/shard_map/all_to_all | solution.py:630
  105.5 0.9 copy-done.10
  106.4 0.9 copy-done.11
  107.4 0.9 copy-done.12
  108.3 1.6 %shard_map.163 = (f32[2,128,128]{2,1,0:T(8,128)}, f32[2,128,128]{2,1,0:T(8,128)}) custom-call(f32[256,128]{1,0:T(8,128)S(1)} %bitcast.24, f32[2,128,128]{2,1,0:T(8,128)S(1)} %copy-done.1, f32[2,128,128]{2,1,0:T(8,128)S(1)} %copy-done.8, f32[2,128,128]{2,1,0:T(8,128)S(1)} %copy-done.9, f32[2,128,128]{2,1,0:T(8,128)S(1)} %copy-done.10, ...), custom_call_target="tpu_custom_call" | custom-call | tf_op jit(solution)/shard_map/pallas_call | solution.py:607
  109.8 0.0 collective-permute-done.2.lo_ref
  109.8 0.0 collective-permute-done.3.hi_ref
  109.8 11.5 %shard_map.161 = f32[1920,128]{1,0:T(8,128)} custom-call(f32[1920,128]{1,0:T(8,128)S(1)} %bitcast.21, f32[1200,128]{1,0:T(8,128)S(1)} %collective-permute-done.2.lo_ref, f32[1200,128]{1,0:T(8,128)} %collective-permute-done.3.hi_ref, f32[376,128]{1,0:T(8,128)S(1)} %collective-permute-done.left_ref, f32[376,128]{1,0:T(8,128)S(1)} %collective-permute-done.1.right_ref, ...), custom_call_target="tpu_custom_call" | custom-call | tf_op jit(solution)/shard_map/pallas_call | solution.py:607
  (20 shorter events, 0.1 us)
Async XLA Ops:
  0.6 11.3 %copy-start.3 = (f32[128,128]{1,0:T(8,128)S(1)}, f32[128,128]{1,0:T(8,128)}, u32[]{:S(2)}) copy-start(f32[128,128]{1,0:T(8,128)} %thick.5) | copy-start | bytes 196612
  0.6 11.3 %copy-start.13 = (s32[1,1,128,4]{2,3,1,0:T(4,128)S(1)}, s32[1,1,128,4]{2,3,1,0:T(4,128)}, u32[]{:S(2)}) copy-start(s32[1,1,128,4]{2,3,1,0:T(4,128)} %param.18) | copy-start | bytes 6148
  0.7 30.1 %copy-start = (f32[4,60,8,128]{3,2,1,0:T(8,128)S(1)}, f32[4,60,8,128]{3,2,1,0:T(8,128)}, u32[]{:S(2)}) copy-start(f32[4,60,8,128]{3,2,1,0:T(8,128)} %param.13) | copy-start | bytes 2949124
  6.0 24.7 %collective-permute-start.1 = (f32[376,128]{1,0:T(8,128)}, f32[376,128]{1,0:T(8,128)S(1)}, u32[]{:S(2)}, u32[]{:S(2)}) collective-permute-start(f32[376,128]{1,0:T(8,128)} %get-tuple-element.23), channel_id=1, source_target_pairs={{1,0},{2,1},{3,2},{4,3},{5,4},{6,5},{7,6},{8,7},{9,8},{10,9},{11,1... | collective-permute-start | bytes 577544 | tf_op jit(solution)/shard_map/ppermute | solution.py:625
  7.3 23.5 %collective-permute-start = (f32[376,128]{1,0:T(8,128)}, f32[376,128]{1,0:T(8,128)S(1)}, u32[]{:S(2)}, u32[]{:S(2)}) collective-permute-start(f32[376,128]{1,0:T(8,128)} %get-tuple-element.23), channel_id=1, source_target_pairs={{0,1},{1,2},{2,3},{3,4},{4,5},{5,6},{6,7},{7,8},{8,9},{9,10},{10,1... | collective-permute-start | bytes 577544 | tf_op jit(solution)/shard_map/ppermute | solution.py:624
  13.2 40.1 %all-to-all-start = ((f32[256,1,128]{2,1,0:T(1,128)}), f32[256,1,128]{2,1,0:T(1,128)S(1)}, u32[]{:S(2)}, u32[]{:S(2)}) async-start(f32[256,1,128]{2,1,0:T(1,128)} %bitcast.7), calls=%async_computation | async-start | bytes 262144 | tf_op jit(solution)/shard_map/all_to_all | solution.py:630
  30.6 9.9 %copy-start.1 = (f32[2,128,128]{2,1,0:T(8,128)S(1)}, f32[2,128,128]{2,1,0:T(8,128)}, u32[]{:S(2)}) copy-start(f32[2,128,128]{2,1,0:T(8,128)} %guess_ref.1) | copy-start | bytes 393220
  30.6 9.9 %copy-start.2 = (f32[2,128,128]{2,1,0:T(8,128)S(1)}, f32[2,128,128]{2,1,0:T(8,128)}, u32[]{:S(2)}) copy-start(f32[2,128,128]{2,1,0:T(8,128)} %drive.5) | copy-start | bytes 393220
  30.7 9.9 %copy-start.4 = (f32[128,128]{1,0:T(8,128)S(1)}, f32[128,128]{1,0:T(8,128)}, u32[]{:S(2)}) copy-start(f32[128,128]{1,0:T(8,128)} %visc.5) | copy-start | bytes 196612
  30.7 9.9 %copy-start.5 = (f32[128,128]{1,0:T(8,128)S(1)}, f32[128,128]{1,0:T(8,128)}, u32[]{:S(2)}) copy-start(f32[128,128]{1,0:T(8,128)} %fric.5) | copy-start | bytes 196612
  30.7 9.8 %copy-start.6 = (s32[128,128]{1,0:T(8,128)S(1)}, s32[128,128]{1,0:T(8,128)}, u32[]{:S(2)}) copy-start(s32[128,128]{1,0:T(8,128)} %ground.5) | copy-start | bytes 196612
  30.7 9.8 %copy-start.7 = (f32[128,128]{1,0:T(8,128)S(1)}, f32[128,128]{1,0:T(8,128)}, u32[]{:S(2)}) copy-start(f32[128,128]{1,0:T(8,128)} %coup.5) | copy-start | bytes 196612
  32.1 77.7 %collective-permute-start.2 = (f32[1200,128]{1,0:T(8,128)}, f32[1200,128]{1,0:T(8,128)S(1)}, u32[]{:S(2)}, u32[]{:S(2)}) collective-permute-start(f32[1200,128]{1,0:T(8,128)} %get-tuple-element.24), channel_id=1, source_target_pairs={{0,16},{16,32},{32,48},{48,64},{64,80},{80,96},{96,112},{112,128},... | collective-permute-start | bytes 1843208 | tf_op jit(solution)/shard_map/ppermute | solution.py:624
  35.5 74.4 %collective-permute-start.3 = (f32[1200,128]{1,0:T(8,128)}, f32[1200,128]{1,0:T(8,128)}, u32[]{:S(2)}, u32[]{:S(2)}) collective-permute-start(f32[1200,128]{1,0:T(8,128)} %get-tuple-element.25), channel_id=1, source_target_pairs={{16,0},{32,16},{48,32},{64,48},{80,64},{96,80},{112,96},{128,112},... | collective-permute-start | bytes 1843208 | tf_op jit(solution)/shard_map/ppermute | solution.py:625
  40.6 9.0 %collective-permute-start.4 = (f32[80,128]{1,0:T(8,128)S(1)}, f32[80,128]{1,0:T(8,128)S(1)}, u32[]{:S(2)}, u32[]{:S(2)}) collective-permute-start(f32[80,128]{1,0:T(8,128)S(1)} %get-tuple-element.28), channel_id=1, source_target_pairs={{0,16},{16,32},{32,48},{48,64},{64,80},{80,96},{96,112},{112,128},... | collective-permute-start | bytes 122888 | tf_op jit(solution)/shard_map/ppermute | solution.py:624
  42.5 10.8 %collective-permute-start.5 = (f32[80,128]{1,0:T(8,128)S(1)}, f32[80,128]{1,0:T(8,128)S(1)}, u32[]{:S(2)}, u32[]{:S(2)}) collective-permute-start(f32[80,128]{1,0:T(8,128)S(1)} %get-tuple-element.29), channel_id=1, source_target_pairs={{16,0},{32,16},{48,32},{64,48},{80,64},{96,80},{112,96},{128,112},... | collective-permute-start | bytes 122888 | tf_op jit(solution)/shard_map/ppermute | solution.py:625
  86.4 19.2 %copy-start.8 = (f32[2,128,128]{2,1,0:T(8,128)S(1)}, f32[2,128,128]{2,1,0:T(8,128)}, u32[]{:S(2)}) copy-start(f32[2,128,128]{2,1,0:T(8,128)} %get-tuple-element.35.res_ref) | copy-start | bytes 393220
  86.4 19.2 %copy-start.9 = (f32[2,128,128]{2,1,0:T(8,128)S(1)}, f32[2,128,128]{2,1,0:T(8,128)}, u32[]{:S(2)}) copy-start(f32[2,128,128]{2,1,0:T(8,128)} %get-tuple-element.36.z_ref) | copy-start | bytes 393220
  105.5 0.9 copy-start.10
  106.4 0.9 copy-start.11
  107.4 0.9 copy-start.12

commit v3 on v2

--- a/solution.py
+++ b/solution.py
@@ -11,9 +11,9 @@
 GY = ("gy_0", "gy_1")
 XAXES = ("grp", "gx")
 ALL = ("grp", "gx", "gy_0", "gy_1")
-LEAD = 72
+LEAD = 24
 DEEP = 960
-SIDE_Y = 248
+SIDE_Y = 240
 F32 = jnp.float32
 BF16 = jnp.bfloat16
 I32 = jnp.int32
@@ -43,7 +43,7 @@
     return lax.dot_general(a, b, (((1,), (1,)), ((), ())), preferred_element_type=F32)
 
 
-def spread(table, half, out_ref):
+def spread(table, half, out_ref, stride):
     row = iota((128, 128), 0) & 15
     group = iota((128, 128), 1) >> 2
     after = pltpu.roll(table, 127, 0)
@@ -59,10 +59,27 @@
     own = own + jnp.concatenate([parts[2][16:], none], 0)
     first = jnp.where(half == 0, parts[0][112:], 0.0)
     last = jnp.where(half == 1, parts[2][:16], 0.0)
-    out_ref[pl.ds(half * 128, 128), :] = own
-    out_ref[pl.ds((1 - half) * 128, 128), :] = jnp.concatenate(
-        [first, jnp.zeros((96, 128), F32), last], 0
-    )
+    other = jnp.concatenate([first, jnp.zeros((96, 128), F32), last], 0)
+    size = 128 * stride
+    if stride > 1:
+        out_ref[...] = jnp.zeros(out_ref.shape, F32)
+    out_ref[pl.ds(pl.multiple_of(half * size, size), 128, stride=stride), :] = own
+    out_ref[pl.ds(pl.multiple_of((1 - half) * size, size), 128, stride=stride), :] = other
+
+
+def place_of():
+    half = lax.axis_index("grp")
+    bx = half * 8 + lax.axis_index("gx")
+    by = lax.axis_index("gy_0") * 4 + lax.axis_index("gy_1")
+    return half, bx, by
+
+
+def first_of(near, far):
+    return jnp.where((iota(near.shape, 1) & 4) == 0, near, pltpu.roll(far, 4, 1))
+
+
+def last_of(near, far):
+    return jnp.where((iota(near.shape, 1) & 4) == 0, pltpu.roll(near, 124, 1), far)
 
 
 def columns_of(owner_ref):
@@ -70,7 +87,8 @@
     return jnp.transpose(jnp.concatenate([node, node], 0)).astype(I32)
 
 
-def draft_kernel(owner_ref, thick_ref, out_ref):
+def draft_kernel(owner_ref, thick_ref, state_ref, diff_ref, wet_ref, col_ref, slot_ref, out_ref, lead_ref):
+    half, bx, by = place_of()
     lane = iota((128, 128), 1)
     parts = split3(thick_ref[...])
     node = columns_of(owner_ref)
@@ -83,7 +101,43 @@
         rows = rows + jnp.dot(pick, parts[2], preferred_element_type=F32)
         value = jnp.sum(jnp.where(lane == (column & 127), rows, 0.0), 1, keepdims=True)
         table = jnp.where((lane & 3) == s, 0.9 * value, table)
-    spread(table, lax.axis_index("grp"), out_ref)
+    spread(table, half, out_ref, 2)
+
+    col = col_ref[...]
+    slot = slot_ref[...]
+    hit = iota((8, 256), 0) == (col >> 7)
+    peer = jnp.where(hit, ((slot >> 2) + 1).astype(F32), 0.0)
+    which = jnp.where(hit, (slot & 3).astype(F32), 0.0)
+    lanes = onehot(iota((128, 256), 0) == (col & 127))
+    both = dot_nt(jnp.concatenate([peer, which], 0).astype(BF16), lanes)
+    for f in range(4):
+        lead_ref[8 * f : 8 * f + 8] = state_ref[f, 0]
+    lead_ref[32:40] = jnp.where(wet_ref[...] > 0, diff_ref[...], 0.0)
+    lead_ref[40:48] = jnp.where(both[:8] > 0.5, 4.0 * both[:8] + both[8:] - 3.0, 0.0)
+    lead_ref[48:64] = jnp.zeros((16, 128), F32)
+    side = edges(lambda r: lead_ref[pl.ds(r, 8, stride=8), :])
+    flat = iota((1, 128), 1)
+    for dy, join in ((1, first_of), (-1, last_of)):
+        pairs = [join(side[2 * j : 2 * j + 1], side[2 * j + 1 : 2 * j + 2]) for j in range(3)]
+        one = jnp.where(flat >= 64, pltpu.roll(pairs[2], 32, 1), 0.0)
+        two = jnp.where(flat < 64, pltpu.roll(pairs[0], 96, 1), pltpu.roll(pairs[1], 32, 1))
+        for dx in (-1, 0, 1):
+            to_x = bx + dx
+            to_y = by + dy
+
+            @pl.when((to_x >= 0) & (to_x < 16) & (to_y >= 0) & (to_y < 16))
+            def _():
+                at = 2 * (to_x * 16 + to_y)
+                out_ref[pl.ds(at, 1), :] = out_ref[pl.ds(at, 1), :] + one
+                out_ref[pl.ds(at + 1, 1), :] = two
+
+
+def edges(get):
+    place = iota((8, 128), 1) >> 3
+    acc = jnp.zeros((8, 128), F32)
+    for r in range(8):
+        acc = jnp.where(place == r + 4, pltpu.roll(get(r), (8 * (r + 4) + 4) % 128, 1), acc)
+    return acc
 
 
 def ice_fields(refs):
@@ -104,20 +158,37 @@
 
 
 def pack_y_kernel(
-    state_ref, diff_ref, wet_ref, col_ref, slot_ref, owner_ref,
+    state_ref, nodemap_ref,
     thick, visc, fric, ground, coup, drive, guess,
-    side_ref, slotmap_ref, nodemap_ref, lead_ref,
+    side_ref,
 ):
-    col = col_ref[...]
-    slot = slot_ref[...]
-    hit = iota((8, 256), 0) == (col >> 7)
-    peer = jnp.where(hit, ((slot >> 2) + 1).astype(F32), 0.0)
-    which = jnp.where(hit, (slot & 3).astype(F32), 0.0)
-    lanes = onehot(iota((128, 256), 0) == (col & 127))
-    both = dot_nt(jnp.concatenate([peer, which], 0).astype(BF16), lanes)
-    slotmap = jnp.where(both[:8] > 0.5, 4.0 * both[:8] + both[8:] - 3.0, 0.0)
-    slotmap_ref[...] = slotmap
-
+    def group(g, carry):
+        at = pl.multiple_of(g * 64, 64)
+        side_ref[pl.ds(pl.multiple_of(8 * g, 8), 8), :] = edges(
+            lambda r: state_ref[pl.ds(at + r, 8, stride=8), :]
+        )
+        return carry
+
+    lax.fori_loop(0, 30, group, 0, unroll=2)
+
+    gets = ice_fields((thick, visc, fric, ground, coup, drive, guess))
+    gets = gets + (lambda at: nodemap_ref[...],)
+    place = iota((128, 128), 1) >> 3
+    acc = jnp.zeros((128, 128), F32)
+    for a, get in enumerate(gets):
+        acc = jnp.where(place == a, pltpu.roll(get(WHOLE), 8 * a + 4, 1), acc)
+    side_ref[SIDE_Y : SIDE_Y + 128] = acc
+
+
+def merged(left, right):
+    return jnp.where((iota(left.shape, 1) & 4) == 0, left, right)
+
+
+def pack_x_kernel(
+    lead_ref, owner_ref,
+    thick, visc, fric, ground, coup, drive, guess,
+    up_ref, down_ref, nodemap_ref,
+):
     node = columns_of(owner_ref)
     lane = iota((128, 128), 1)
     number = iota((128, 128), 0).astype(F32) + 1.0
@@ -135,66 +206,18 @@
     which = dot_tn(jnp.concatenate(whichs, 0), cols)
     nodemap_ref[...] = jnp.where(peer > 0.5, 4.0 * peer + which - 3.0, 0.0)
 
-    for f in range(4):
-        lead_ref[8 * f : 8 * f + 8] = state_ref[480 * f : 480 * f + 8]
-    lead_ref[32:40] = diff_ref[...]
-    lead_ref[40:48] = wet_ref[...].astype(F32)
-    lead_ref[48:56] = slotmap
-    lead_ref[56:64] = jnp.zeros((8, 128), F32)
-
-    place = iota((8, 128), 1) >> 3
-
-    def edges(get):
-        acc = jnp.zeros((8, 128), F32)
-        for r in range(8):
-            acc = jnp.where(place == r + 4, pltpu.roll(get(r), (8 * (r + 4) + 4) % 128, 1), acc)
-        return acc
-
-    side_ref[0:8] = edges(lambda r: lead_ref[pl.ds(r, 8, stride=8), :])
-
-    def group(g, carry):
-        at = pl.multiple_of(g * 64, 64)
-        side_ref[pl.ds(pl.multiple_of(8 + 8 * g, 8), 8), :] = edges(
-            lambda r: state_ref[pl.ds(at + r, 8, stride=8), :]
-        )
-        return carry
-
-    lax.fori_loop(0, 30, group, 0)
-
-    gets = ice_fields((thick, visc, fric, ground, coup, drive, guess))
-    gets = gets + (lambda at: nodemap_ref[...],)
-    place = lane >> 3
-    acc = jnp.zeros((128, 128), F32)
-    for a, get in enumerate(gets):
-        acc = jnp.where(place == a, pltpu.roll(get(WHOLE), 8 * a + 4, 1), acc)
-    side_ref[SIDE_Y : SIDE_Y + 128] = acc
-
-
-def merged(left, right):
-    return jnp.where((iota(left.shape, 1) & 4) == 0, left, right)
-
-
-def pack_x_kernel(
-    lead_ref, nodemap_ref, left_ref, right_ref,
-    thick, visc, fric, ground, coup, drive, guess,
-    up_ref, down_ref,
-):
-    for i in range(8):
+    for i in range(6):
         up_ref[4 * i : 4 * i + 4] = lead_ref[8 * i + 4 : 8 * i + 8]
         down_ref[4 * i : 4 * i + 4] = lead_ref[8 * i : 8 * i + 4]
     top = (pl.ds(0, 4), slice(None))
     end = (pl.ds(124, 4), slice(None))
     gets = ice_fields((thick, visc, fric, ground, coup, drive, guess))
+    gets = gets + (lambda at: nodemap_ref[at],)
     for a, get in enumerate(gets):
-        up_ref[32 + 4 * a : 36 + 4 * a] = get(end)
-        down_ref[32 + 4 * a : 36 + 4 * a] = get(top)
-    up_ref[64:68] = nodemap_ref[124:128]
-    down_ref[64:68] = nodemap_ref[0:4]
-    up_ref[68:72] = merged(left_ref[SIDE_Y + 124 : SIDE_Y + 128], right_ref[SIDE_Y + 124 : SIDE_Y + 128])
-    down_ref[68:72] = merged(left_ref[SIDE_Y : SIDE_Y + 4], right_ref[SIDE_Y : SIDE_Y + 4])
-    side = merged(left_ref[0:8], right_ref[0:8])
-    up_ref[LEAD : LEAD + 8] = side
-    down_ref[LEAD : LEAD + 8] = side
+        up_ref[LEAD + 4 * a : LEAD + 4 * a + 4] = get(end)
+        down_ref[LEAD + 4 * a : LEAD + 4 * a + 4] = get(top)
+    up_ref[60:64] = jnp.zeros((4, 128), F32)
+    down_ref[60:64] = jnp.zeros((4, 128), F32)
 
 
 def pack_deep_kernel(state_ref, left_ref, right_ref, up_ref, down_ref):
@@ -206,16 +229,16 @@
             down_ref[pl.ds(to + r, 8, stride=4), :] = state_ref[pl.ds(at + r, 8, stride=8), :]
         return carry
 
-    lax.fori_loop(0, 30, group, 0)
-    side = merged(left_ref[8:SIDE_Y], right_ref[8:SIDE_Y])
+    lax.fori_loop(0, 30, group, 0, unroll=2)
+    side = merged(left_ref[0:SIDE_Y], right_ref[0:SIDE_Y])
     up_ref[DEEP : DEEP + 240] = side
     down_ref[DEEP : DEEP + 240] = side
 
 
-def whole_side(left, right, lo, hi):
-    lane = iota(left.shape, 1)
+def whole_side(own, lo, hi):
+    lane = iota(own.shape, 1)
     far = pltpu.roll(jnp.where(lane < 64, hi, lo), 64, 1)
-    return jnp.where((lane < 32) | (lane >= 96), far, merged(left, right))
+    return jnp.where((lane < 32) | (lane >= 96), far, own)
 
 
 def turn(x, shift, axis):
@@ -261,13 +284,31 @@
 
 
 def top_kernel(
-    lead_ref, lo_ref, hi_ref, left_ref, right_ref, table_ref,
+    lead_ref, lo_ref, hi_ref, table_ref, ice_ref,
     top_ref, melt_ref, weight_ref, send_ref, turn_ref,
 ):
     half, half_lo, half_hi = halves()
-    side = whole_side(
-        left_ref[0:8], right_ref[0:8], lo_ref[LEAD : LEAD + 8], hi_ref[LEAD : LEAD + 8]
-    )
+    _, bx, by = place_of()
+    flat = iota((1, 128), 1)
+
+    def pairs_from(x, y):
+        ok = (x >= 0) & (x < 16) & (y >= 0) & (y < 16)
+        at = jnp.where(ok, 2 * (x * 16 + y), 0)
+        one = table_ref[pl.ds(at, 1), :]
+        two = table_ref[pl.ds(at + 1, 1), :]
+        found = (pltpu.roll(two, 32, 1), pltpu.roll(two, 96, 1), pltpu.roll(one, 96, 1))
+        return [jnp.where(ok & (flat >= 32) & (flat < 96), f, 0.0) for f in found]
+
+    def columns_at(x):
+        from_left = pairs_from(x, by - 1)
+        from_right = pairs_from(x, by + 1)
+        rows = []
+        for j in range(3):
+            rows.append(merged(from_left[j], pltpu.roll(from_right[j], 4, 1)))
+            rows.append(merged(pltpu.roll(from_left[j], 124, 1), from_right[j]))
+        return jnp.concatenate(rows + [jnp.zeros((2, 128), F32)], 0)
+
+    side = whole_side(columns_at(bx), columns_at(bx - 1), columns_at(bx + 1))
     for c in range(16):
         p = (c + 4) % 16
         turn_ref[8 * c : 8 * c + 8] = pltpu.roll(side, (128 - 8 * p - 4) % 128, 1)
@@ -283,11 +324,11 @@
 
     fields = [padded(f) for f in range(4)]
     diff = padded(4)
-    wet = padded(5)
-    code = padded(6)
+    code = padded(5)
     weights = []
     for axis, shift in ((0, -1), (0, 1), (1, -1), (1, 1)):
-        weights.append(0.5 * (diff + turn(diff, shift, axis)) * wet * turn(wet, shift, axis))
+        other = turn(diff, shift, axis)
+        weights.append(jnp.where((diff > 0.0) & (other > 0.0), 0.5 * (diff + other), 0.0))
     keep = 1.0 - (weights[0] + weights[1] + weights[2] + weights[3])
     for j, w in enumerate(weights + [keep]):
         centre = w[:, 0:128]
@@ -305,13 +346,12 @@
     half_at = jnp.where(row < 8, half, jnp.where(row < 12, half_hi, half_lo))
     dx = jnp.where(row < 8, 1, jnp.where(row < 12, 2, 0))
     owner, lane_of = decode(code[:, 0:128], half_at, 3 * dx + 1)
-    flat = iota((1, 128), 1)
     place = flat >> 3
     half_at = jnp.where(place < 4, half_lo, jnp.where(place < 12, half, half_hi))
     dx = jnp.where(place < 4, 0, jnp.where(place < 12, 1, 2))
     dy = jnp.where((flat & 4) == 0, 0, 2)
-    side_owner, side_lane = decode(side[6:7], half_at, 3 * dx + dy)
-    parts = table_parts(table_ref[...])
+    side_owner, side_lane = decode(side[5:6], half_at, 3 * dx + dy)
+    parts = table_parts(table_ref[pl.ds(0, 256, stride=2), :])
     none = jnp.zeros((1, 128), F32)
     found = [
         none if r in (11, 12) else lookup(parts, owner[r : r + 1], lane_of[r : r + 1]) for r in range(16)
@@ -346,7 +386,7 @@
     mean = total * (1.0 / NSUB)
     melt_ref[...] = mean
 
-    number = lead_ref[48:56].astype(I32) - 1
+    number = lead_ref[40:48].astype(I32) - 1
     peers = []
     values = []
     for r in range(8):
@@ -356,7 +396,21 @@
     peers = jnp.concatenate(peers, 1)
     values = jnp.concatenate(split3(jnp.concatenate(values, 1)), 0)
     table = dot_nt(peers, values)
-    spread(table[:, 0:128] + table[:, 128:256] + table[:, 256:384], half, send_ref)
+    spread(table[:, 0:128] + table[:, 128:256] + table[:, 256:384], half, send_ref, 1)
+    for dy, join in ((1, first_of), (-1, last_of)):
+        for dx, near_row, far_row in ((1, 127, 126), (-1, 0, 1)):
+            to_x = bx + dx
+            to_y = by + dy
+            corner = join(
+                ice_ref[SIDE_Y + near_row : SIDE_Y + near_row + 1],
+                ice_ref[SIDE_Y + far_row : SIDE_Y + far_row + 1],
+            )
+            corner = pltpu.roll(jnp.where(flat < 72, corner, 0.0), 40, 1)
+
+            @pl.when((to_x >= 0) & (to_x < 16) & (to_y >= 0) & (to_y < 16))
+            def _():
+                at = to_x * 16 + to_y
+                send_ref[pl.ds(at, 1), :] = send_ref[pl.ds(at, 1), :] + corner
 
 
 def bulk_kernel(
@@ -382,8 +436,7 @@
         for p in range(16):
             own = jnp.where((lane >> 3) == p, pltpu.roll(x[p], (8 * p + 4) % 128, 1), own)
         near = whole_side(
-            left_ref[pl.ds(pl.multiple_of(side + 8, 8), 8), :],
-            right_ref[pl.ds(pl.multiple_of(side + 8, 8), 8), :],
+            merged(left_ref[pl.ds(side, 8), :], right_ref[pl.ds(side, 8), :]),
             lo_ref[pl.ds(pl.multiple_of(side + DEEP, 8), 8), :],
             hi_ref[pl.ds(pl.multiple_of(side + DEEP, 8), 8), :],
         )
@@ -469,15 +522,34 @@
     send_ref, res_ref, z_ref, y_ref, w_ref, v_ref,
 ):
     half, half_lo, half_hi = halves()
+    _, bx, by = place_of()
+    flat = iota((1, 128), 1)
+
+    def corner_from(x, y):
+        ok = (x >= 0) & (x < 16) & (y >= 0) & (y < 16)
+        got = pltpu.roll(table_ref[pl.ds(jnp.where(ok, x * 16 + y, 0), 1), :], 88, 1)
+        return jnp.where(ok & (flat < 72), got, 0.0)
+
+    def corners_at(x):
+        from_left = corner_from(x, by - 1)
+        from_right = corner_from(x, by + 1)
+        return (
+            merged(from_left, pltpu.roll(from_right, 4, 1)),
+            merged(pltpu.roll(from_left, 124, 1), from_right),
+        )
+
+    lo_near, lo_far = corners_at(bx - 1)
+    hi_near, hi_far = corners_at(bx + 1)
     side = merged(left_ref[SIDE_Y : SIDE_Y + 128], right_ref[SIDE_Y : SIDE_Y + 128])
-    side = jnp.concatenate([side, hi_ref[68:72], lo_ref[68:72]], 0)
+    gap = jnp.zeros((4, 128), F32)
+    side = jnp.concatenate([side, hi_near, hi_far, gap, lo_far, lo_near], 0)
     gets = ice_fields((thick, visc, fric, ground, coup, drive, guess))
     gets = gets + (lambda at: nodemap_ref[...],)
     lane = iota((136, 128), 1)
     edge = (lane < 4) | (lane >= 124)
 
     def padded(a):
-        at = 32 + 4 * a
+        at = LEAD + 4 * a
         centre = jnp.concatenate([gets[a](WHOLE), hi_ref[at : at + 4], lo_ref[at : at + 4]], 0)
         edges = jnp.where(edge, pltpu.roll(side, (128 - 8 * a - 4) % 128, 1), 0.0)
         return jnp.concatenate([centre, edges], 1)
@@ -597,10 +669,6 @@
 SMALL = 24 << 20
 
 
-def near(*shape):
-    return pltpu.VMEM(shape, F32)
-
-
 def call(kernel, outs, *args, stay=(), limit=None, **kw):
     args = [x if any(x is y for y in stay) else here(x) for x in args]
     vmem = pl.BlockSpec(memory_space=pltpu.VMEM)
@@ -614,6 +682,10 @@
     )(*args)
 
 
+def block(*shape):
+    return pl.BlockSpec(shape, lambda i: (0,) * len(shape))
+
+
 def here(x):
     return pltpu.with_memory_space_constraint(x, pltpu.VMEM)
 
@@ -641,22 +713,32 @@
     state = ocean_state.reshape(1920, 128)
     given = (state, diffusivity, wet_mask, columns, slots, owner) + ice
 
-    side, _, nodemap, lead = call(
+    send_draft, lead = pl.pallas_call(
+        draft_kernel,
+        name="draft",
+        grid=(1,),
+        in_specs=[block(4, 128), block(128, 128), block(4, 1, 8, 128), block(8, 128), block(8, 128)]
+        + [block(1, 256), block(1, 256)],
+        out_specs=[block(512, 128), block(64, 128)],
+        out_shape=[sds(512, 128), sds(64, 128)],
+    )(owner, thickness, ocean_state, diffusivity, wet_mask, columns, slots)
+    got_draft = exchange(send_draft)
+    up, down, nodemap = call(
+        pack_x_kernel,
+        [sds(64, 128), sds(64, 128), sds(128, 128)],
+        lead, owner, *ice,
+        stay=given + (lead,),
+        limit=SMALL,
+    )
+    lo, hi = swap(up, down, XAXES)
+    (side,) = call(
         pack_y_kernel,
-        [sds(SIDE_Y + 128, 128), near(8, 128), near(128, 128), near(64, 128)],
-        state, diffusivity, wet_mask, columns, slots, owner, *ice,
-        stay=given,
-    )
-    left, right = swap(side, side, GY)
-    (send_draft,) = call(draft_kernel, [sds(256, 128)], owner, thickness, stay=given, limit=SMALL)
-    up, down = call(
-        pack_x_kernel,
-        [sds(LEAD + 8, 128), sds(LEAD + 8, 128)],
-        lead, nodemap, left, right, *ice,
+        [sds(SIDE_Y + 128, 128)],
+        state, nodemap, *ice,
         stay=given,
         limit=SMALL,
     )
-    lo, hi = swap(up, down, XAXES)
+    left, right = swap(side, side, GY)
     up, down = call(
         pack_deep_kernel,
         [sds(DEEP + 240, 128), sds(DEEP + 240, 128)],
@@ -665,12 +747,11 @@
         limit=SMALL,
     )
     deep_lo, deep_hi = swap(up, down, XAXES)
-    got_draft = exchange(send_draft)
 
     top, melt_mean, weights, send_melt = call(
         top_kernel,
         [sds(32, 128), sds(8, 128), sds(96, 128), sds(256, 128)],
-        lead, lo, hi, left, right, got_draft,
+        lead, lo, hi, got_draft, side,
         scratch_shapes=[pltpu.VMEM((128, 128), F32)],
         limit=SMALL,
     )

time: 122 us -> 110 us (0.902)
  blocking collectives: 46.9 us -> 31.2 us
  starting transfers between devices: 38.6 us -> 43.1 us
  waiting for transfers between devices: 5.91 us -> 8.43 us
  local copies, waits for them, and re-layouts: 2.77 us -> 0.82 us
  Pallas kernels: 26.3 us -> 25 us
    all_to_all x2 -> x1, blocking collectives: 46.9 us -> 31.2 us  [exchange(): lax.all_to_all(table, ALL, split_axis=0, concat_axis=0, tiled=True)]
    pallas_call x8 -> x7, Pallas kernels: 26.3 us -> 22.5 us  [call(): pl.pallas_call(kernel, in_specs=[vmem] * len(args), out_specs=[vmem] * le...]
    all_to_all x1 -> x2, starting transfers between devices: 17.5 us -> 20.9 us  [exchange(): lax.all_to_all(table, ALL, split_axis=0, concat_axis=0, tiled=True)]
    ppermute x3, waiting for transfers between devices: 3.67 us -> 6.58 us  [swap(): high = lax.ppermute(down, axes, [(b, a) for a, b in forward])]
    pallas_call x0 -> x1, Pallas kernels: none -> 2.46 us  [shards(): pl.pallas_call(draft_kernel, name='draft', grid=(1,), in_specs=[block(4,...]
    ppermute x3, waiting for transfers between devices: 2.23 us -> 0.28 us  [swap(): low = lax.ppermute(up, axes, forward)]
    unnamed x28 -> x30, local copies, waits for them, and re-layouts: 2.77 us -> 0.82 us
    all_to_all x1 -> x2, waiting for transfers between devices: 0.01 us -> 1.58 us  [exchange(): lax.all_to_all(table, ALL, split_axis=0, concat_axis=0, tiled=True)]
  transfers between devices with their start and end apart: 7 -> 8, of which waited for: 2 -> 5; matrix products, arithmetic and copies ran while one was open for 0% -> 0% of each run, Pallas kernels for 8% -> 19%
where the time goes in v3:
time: 110 us; the launch traced here: 109 us
  starting transfers between devices  43.1 us (39%)
  blocking collectives  31.2 us (28%)
  Pallas kernels  25 us (23%)
  waiting for transfers between devices  8.43 us (8%)
    all_to_all x1, blocking collectives, exchange(): lax.all_to_all(table, ALL, split_axis=0, concat_axis=0, tiled=True)  31.2 us
    pallas_call x7, Pallas kernels, call(): pl.pallas_call(kernel, in_specs=[vmem] * len(args), out_specs=[vmem] * le...  22.5 us
    all_to_all x2, starting transfers between devices, exchange(): lax.all_to_all(table, ALL, split_axis=0, concat_axis=0, tiled=True)  20.9 us
    ppermute x3, starting transfers between devices, swap(): high = lax.ppermute(down, axes, [(b, a) for a, b in forward])  11.9 us
    ppermute x3, starting transfers between devices, swap(): low = lax.ppermute(up, axes, forward)  10.3 us
    ppermute x3, waiting for transfers between devices, swap(): high = lax.ppermute(down, axes, [(b, a) for a, b in forward])  6.58 us
    pallas_call x1, Pallas kernels, shards(): pl.pallas_call(draft_kernel, name='draft', grid=(1,), in_specs=[block(4,...  2.46 us
  transfers between devices with their start and end apart: 8, of which 5 were waited for; matrix products, arithmetic and copies ran while one was open for 0% of the time, Pallas kernels for 19%

profile of v3, /device:TPU:1, one launch (start us, length us, event | category | flops | bytes accessed | tf_op | source)
XLA Modules:
  0.0 109.5 jit_solution(17530944687965073674)
XLA Ops:
  0.7 2.5 %draft.1 = (f32[512,128]{1,0:T(8,128)}, f32[64,128]{1,0:T(8,128)}) custom-call(s32[4,128]{1,0:T(4,128)} %bitcast.24, f32[128,128]{1,0:T(8,128)} %thick.5, f32[4,60,8,128]{3,2,1,0:T(8,128)} %state_ref.1, f32[8,128]{1,0:T(8,128)} %diff_ref.1, s32[8,128]{1,0:T(8,128)} %wet_ref.1, s32[1,256]{1,0:T(1,128)} %bitcast.30, s32[1,256]{1,0:T(1,128)} %bitcast.31), custom_call_target="tpu_custom_call" | custom-call | tf_op jit(solution)/shard_map/draft/pallas_call | solution.py:716
  3.1 0.0 copy-start.4
  3.1 0.0 copy-start.5
  3.2 0.0 copy-start.6
  3.2 15.7 %all-to-all-start = ((f32[256,2,128]{2,1,0:T(2,128)}), f32[256,2,128]{2,1,0:T(2,128)S(1)}, u32[]{:S(2)}, u32[]{:S(2)}) async-start(f32[256,2,128]{2,1,0:T(2,128)} %bitcast.28), calls=%async_computation | async-start | bytes 524288 | tf_op jit(solution)/shard_map/all_to_all | solution.py:702
  18.9 0.0 copy-start.13
  18.9 0.7 copy-done.13
  19.7 0.6 shard_map.156
  20.3 1.5 %shard_map.157.ice_ref = f32[368,128]{1,0:T(8,128)S(1)} custom-call(f32[1920,128]{1,0:T(8,128)S(1)} %bitcast.17, f32[128,128]{1,0:T(8,128)S(1)} %get-tuple-element.24.nodemap_ref, f32[128,128]{1,0:T(8,128)S(1)} %copy-done.3, f32[128,128]{1,0:T(8,128)S(1)} %copy-done.4, f32[128,128]{1,0:T(8,128)S(1)} %copy-done.5, s32[128,128]{1,0:T(8,128)S(1)} %copy-done.6, ...), custom_call_target="tpu_custom_call" | custom-call | tf_op jit(solution)/shard_map/pallas_call | solution.py:675
  21.8 1.3 %collective-permute-start.1 = (f32[368,128]{1,0:T(8,128)S(1)}, f32[368,128]{1,0:T(8,128)S(1)}, u32[]{:S(2)}, u32[]{:S(2)}) collective-permute-start(f32[368,128]{1,0:T(8,128)S(1)} %shard_map.157.ice_ref), channel_id=1, source_target_pairs={{1,0},{2,1},{3,2},{4,3},{5,4},{6,5},{7,6},{8,7},{9,8},{10,9},{11,1... | collective-permute-start | bytes 565256 | tf_op jit(solution)/shard_map/ppermute | solution.py:697
  23.1 4.0 %collective-permute-start = (f32[368,128]{1,0:T(8,128)S(1)}, f32[368,128]{1,0:T(8,128)S(1)}, u32[]{:S(2)}, u32[]{:S(2)}) collective-permute-start(f32[368,128]{1,0:T(8,128)S(1)} %shard_map.157.ice_ref), channel_id=1, source_target_pairs={{0,1},{1,2},{2,3},{3,4},{4,5},{5,6},{6,7},{7,8},{8,9},{9,10},{10,1... | collective-permute-start | bytes 565256 | tf_op jit(solution)/shard_map/ppermute | solution.py:696
  27.1 2.7 %collective-permute-done.1.right_ref = f32[368,128]{1,0:T(8,128)S(1)} collective-permute-done((f32[368,128]{1,0:T(8,128)S(1)}, f32[368,128]{1,0:T(8,128)S(1)}, u32[]{:S(2)}, u32[]{:S(2)}) %collective-permute-start.1) | collective-permute-done | bytes 188448 | tf_op jit(solution)/shard_map/ppermute | solution.py:697
  29.7 0.1 collective-permute-done.left_ref
  29.9 1.3 %shard_map.158 = (f32[1200,128]{1,0:T(8,128)}, f32[1200,128]{1,0:T(8,128)}) custom-call(f32[1920,128]{1,0:T(8,128)S(1)} %bitcast.18, f32[368,128]{1,0:T(8,128)S(1)} %collective-permute-done.left_ref, f32[368,128]{1,0:T(8,128)S(1)} %collective-permute-done.1.right_ref), custom_call_target="tpu_custom_call" | custom-call | tf_op jit(solution)/shard_map/pallas_call | solution.py:675
  31.1 4.4 %collective-permute-start.2 = (f32[1200,128]{1,0:T(8,128)}, f32[1200,128]{1,0:T(8,128)S(1)}, u32[]{:S(2)}, u32[]{:S(2)}) collective-permute-start(f32[1200,128]{1,0:T(8,128)} %get-tuple-element.25), channel_id=1, source_target_pairs={{0,16},{16,32},{32,48},{48,64},{64,80},{80,96},{96,112},{112,128},... | collective-permute-start | bytes 1843208 | tf_op jit(solution)/shard_map/ppermute | solution.py:696
  35.5 5.7 %collective-permute-start.3 = (f32[1200,128]{1,0:T(8,128)}, f32[1200,128]{1,0:T(8,128)}, u32[]{:S(2)}, u32[]{:S(2)}) collective-permute-start(f32[1200,128]{1,0:T(8,128)} %get-tuple-element.26), channel_id=1, source_target_pairs={{16,0},{32,16},{48,32},{64,48},{80,64},{96,80},{112,96},{128,112},... | collective-permute-start | bytes 1843208 | tf_op jit(solution)/shard_map/ppermute | solution.py:697
  41.3 1.9 %collective-permute-start.4 = (f32[64,128]{1,0:T(8,128)S(1)}, f32[64,128]{1,0:T(8,128)S(1)}, u32[]{:S(2)}, u32[]{:S(2)}) collective-permute-start(f32[64,128]{1,0:T(8,128)S(1)} %get-tuple-element.27), channel_id=1, source_target_pairs={{0,16},{16,32},{32,48},{48,64},{64,80},{80,96},{96,112},{112,128},... | collective-permute-start | bytes 98312 | tf_op jit(solution)/shard_map/ppermute | solution.py:696
  43.2 4.9 %collective-permute-start.5 = (f32[64,128]{1,0:T(8,128)S(1)}, f32[64,128]{1,0:T(8,128)S(1)}, u32[]{:S(2)}, u32[]{:S(2)}) collective-permute-start(f32[64,128]{1,0:T(8,128)S(1)} %get-tuple-element.28), channel_id=1, source_target_pairs={{16,0},{32,16},{48,32},{64,48},{80,64},{96,80},{112,96},{128,112},... | collective-permute-start | bytes 98312 | tf_op jit(solution)/shard_map/ppermute | solution.py:697
  48.1 0.1 collective-permute-done.4.lo_ref
  48.2 3.9 %collective-permute-done.5.hi_ref = f32[64,128]{1,0:T(8,128)S(1)} collective-permute-done((f32[64,128]{1,0:T(8,128)S(1)}, f32[64,128]{1,0:T(8,128)S(1)}, u32[]{:S(2)}, u32[]{:S(2)}) %collective-permute-start.5) | collective-permute-done | bytes 32800 | tf_op jit(solution)/shard_map/ppermute | solution.py:697
  52.1 0.0 all-to-all-done
  52.1 2.4 %shard_map.159 = (f32[32,128]{1,0:T(8,128)S(1)}, f32[8,128]{1,0:T(8,128)}, f32[96,128]{1,0:T(8,128)S(1)}, f32[256,128]{1,0:T(8,128)S(1)}) custom-call(f32[64,128]{1,0:T(8,128)S(1)} %copy-done.13, f32[64,128]{1,0:T(8,128)S(1)} %collective-permute-done.4.lo_ref, f32[64,128]{1,0:T(8,128)S(1)} %collective-permute-done.5.hi_ref, f32[512,128]{1,0:T(8,128)S(1)} %bitcast.20, ...), custom_call_target="tpu_custom_call" | custom-call | tf_op jit(solution)/shard_map/pallas_call | solution.py:675
  54.5 31.2 %all_to_all.33 = f32[256,1,128]{2,1,0:T(1,128)S(1)} all-to-all(f32[256,1,128]{2,1,0:T(1,128)S(1)} %bitcast.23), channel_id=1, replica_groups=mesh['grp'=2,'gx'=8,'gy_0'=4,'gy_1'=4] {'grp','gx','gy_0','gy_1'}, dimensions={0} | all-to-all | bytes 262144 | tf_op jit(solution)/shard_map/all_to_all | solution.py:702
  85.7 3.7 %shard_map.161 = (f32[256,128]{1,0:T(8,128)}, f32[2,128,128]{2,1,0:T(8,128)}, f32[2,128,128]{2,1,0:T(8,128)}, f32[2,128,128]{2,1,0:T(8,128)}, f32[2,128,128]{2,1,0:T(8,128)}, /*index=5*/f32[2,128,128]{2,1,0:T(8,128)}) custom-call(s32[4,128]{1,0:T(4,128)S(1)} %bitcast.26, f32[256,128]{1,0:T(8,128)S(1)} %bitcast.22, ...), custom_call_target="tpu_custom_call" | custom-call | tf_op jit(solution)/shard_map/pallas_call | solution.py:675
  89.4 5.3 %all-to-all-start.2 = ((f32[256,1,128]{2,1,0:T(1,128)}), f32[256,1,128]{2,1,0:T(1,128)S(1)}, u32[]{:S(2)}, u32[]{:S(2)}) async-start(f32[256,1,128]{2,1,0:T(1,128)} %bitcast.29), calls=%async_computation.2 | async-start | bytes 262144 | tf_op jit(solution)/shard_map/all_to_all | solution.py:702
  94.7 0.0 collective-permute-done.2.lo_ref
  94.7 0.0 collective-permute-done.3.hi_ref
  94.7 0.0 copy-start.8
  94.7 0.0 copy-start.9
  94.8 11.5 %shard_map.160 = f32[1920,128]{1,0:T(8,128)} custom-call(f32[1920,128]{1,0:T(8,128)S(1)} %bitcast.19, f32[1200,128]{1,0:T(8,128)S(1)} %collective-permute-done.2.lo_ref, f32[1200,128]{1,0:T(8,128)} %collective-permute-done.3.hi_ref, f32[368,128]{1,0:T(8,128)S(1)} %collective-permute-done.left_ref, f32[368,128]{1,0:T(8,128)S(1)} %collective-permute-done.1.right_ref, ...), custom_call_target="tpu_custom_call" | custom-call | tf_op jit(solution)/shard_map/pallas_call | solution.py:675
  106.3 1.6 %all-to-all-done.2 = f32[256,1,128]{2,1,0:T(1,128)S(1)} async-done(((f32[256,1,128]{2,1,0:T(1,128)}), f32[256,1,128]{2,1,0:T(1,128)S(1)}, u32[]{:S(2)}, u32[]{:S(2)}) %all-to-all-start.2) | async-done | bytes 131104 | tf_op jit(solution)/shard_map/all_to_all | solution.py:702
  107.9 1.6 %shard_map.162 = (f32[2,128,128]{2,1,0:T(8,128)}, f32[2,128,128]{2,1,0:T(8,128)}) custom-call(f32[256,128]{1,0:T(8,128)S(1)} %bitcast.21, f32[2,128,128]{2,1,0:T(8,128)S(1)} %copy-done.1, f32[2,128,128]{2,1,0:T(8,128)S(1)} %copy-done.8, f32[2,128,128]{2,1,0:T(8,128)S(1)} %copy-done.9, f32[2,128,128]{2,1,0:T(8,128)S(1)} %copy-done.10, ...), custom_call_target="tpu_custom_call" | custom-call | tf_op jit(solution)/shard_map/pallas_call | solution.py:675
  (23 shorter events, 0.0 us)
Async XLA Ops:
  0.6 18.2 %copy-start.7 = (f32[128,128]{1,0:T(8,128)S(1)}, f32[128,128]{1,0:T(8,128)}, u32[]{:S(2)}) copy-start(f32[128,128]{1,0:T(8,128)} %coup.5) | copy-start | bytes 196612
  0.6 18.2 %copy-start.14 = (s32[1,1,128,4]{2,3,1,0:T(4,128)S(1)}, s32[1,1,128,4]{2,3,1,0:T(4,128)}, u32[]{:S(2)}) copy-start(s32[1,1,128,4]{2,3,1,0:T(4,128)} %param.18) | copy-start | bytes 6148
  0.7 19.6 %copy-start = (f32[4,60,8,128]{3,2,1,0:T(8,128)S(1)}, f32[4,60,8,128]{3,2,1,0:T(8,128)}, u32[]{:S(2)}) copy-start(f32[4,60,8,128]{3,2,1,0:T(8,128)} %state_ref.1) | copy-start | bytes 2949124
  3.1 15.7 %copy-start.1 = (f32[2,128,128]{2,1,0:T(8,128)S(1)}, f32[2,128,128]{2,1,0:T(8,128)}, u32[]{:S(2)}) copy-start(f32[2,128,128]{2,1,0:T(8,128)} %guess_ref.1) | copy-start | bytes 393220
  3.1 15.7 %copy-start.2 = (f32[2,128,128]{2,1,0:T(8,128)S(1)}, f32[2,128,128]{2,1,0:T(8,128)}, u32[]{:S(2)}) copy-start(f32[2,128,128]{2,1,0:T(8,128)} %drive.5) | copy-start | bytes 393220
  3.1 15.8 %copy-start.3 = (f32[128,128]{1,0:T(8,128)S(1)}, f32[128,128]{1,0:T(8,128)}, u32[]{:S(2)}) copy-start(f32[128,128]{1,0:T(8,128)} %thick.5) | copy-start | bytes 196612
  3.1 15.8 %copy-start.4 = (f32[128,128]{1,0:T(8,128)S(1)}, f32[128,128]{1,0:T(8,128)}, u32[]{:S(2)}) copy-start(f32[128,128]{1,0:T(8,128)} %visc.5) | copy-start | bytes 196612
  3.1 15.8 %copy-start.5 = (f32[128,128]{1,0:T(8,128)S(1)}, f32[128,128]{1,0:T(8,128)}, u32[]{:S(2)}) copy-start(f32[128,128]{1,0:T(8,128)} %fric.5) | copy-start | bytes 196612
  3.2 15.8 %copy-start.6 = (s32[128,128]{1,0:T(8,128)S(1)}, s32[128,128]{1,0:T(8,128)}, u32[]{:S(2)}) copy-start(s32[128,128]{1,0:T(8,128)} %ground.5) | copy-start | bytes 196612
  3.2 48.9 %all-to-all-start = ((f32[256,2,128]{2,1,0:T(2,128)}), f32[256,2,128]{2,1,0:T(2,128)S(1)}, u32[]{:S(2)}, u32[]{:S(2)}) async-start(f32[256,2,128]{2,1,0:T(2,128)} %bitcast.28), calls=%async_computation | async-start | bytes 524288 | tf_op jit(solution)/shard_map/all_to_all | solution.py:702
  18.9 0.8 copy-start.13
  21.8 8.0 %collective-permute-start.1 = (f32[368,128]{1,0:T(8,128)S(1)}, f32[368,128]{1,0:T(8,128)S(1)}, u32[]{:S(2)}, u32[]{:S(2)}) collective-permute-start(f32[368,128]{1,0:T(8,128)S(1)} %shard_map.157.ice_ref), channel_id=1, source_target_pairs={{1,0},{2,1},{3,2},{4,3},{5,4},{6,5},{7,6},{8,7},{9,8},{10,9},{11,1... | collective-permute-start | bytes 565256 | tf_op jit(solution)/shard_map/ppermute | solution.py:697
  23.1 6.8 %collective-permute-start = (f32[368,128]{1,0:T(8,128)S(1)}, f32[368,128]{1,0:T(8,128)S(1)}, u32[]{:S(2)}, u32[]{:S(2)}) collective-permute-start(f32[368,128]{1,0:T(8,128)S(1)} %shard_map.157.ice_ref), channel_id=1, source_target_pairs={{0,1},{1,2},{2,3},{3,4},{4,5},{5,6},{6,7},{7,8},{8,9},{9,10},{10,1... | collective-permute-start | bytes 565256 | tf_op jit(solution)/shard_map/ppermute | solution.py:696
  31.1 63.6 %collective-permute-start.2 = (f32[1200,128]{1,0:T(8,128)}, f32[1200,128]{1,0:T(8,128)S(1)}, u32[]{:S(2)}, u32[]{:S(2)}) collective-permute-start(f32[1200,128]{1,0:T(8,128)} %get-tuple-element.25), channel_id=1, source_target_pairs={{0,16},{16,32},{32,48},{48,64},{64,80},{80,96},{96,112},{112,128},... | collective-permute-start | bytes 1843208 | tf_op jit(solution)/shard_map/ppermute | solution.py:696
  35.5 59.2 %collective-permute-start.3 = (f32[1200,128]{1,0:T(8,128)}, f32[1200,128]{1,0:T(8,128)}, u32[]{:S(2)}, u32[]{:S(2)}) collective-permute-start(f32[1200,128]{1,0:T(8,128)} %get-tuple-element.26), channel_id=1, source_target_pairs={{16,0},{32,16},{48,32},{64,48},{80,64},{96,80},{112,96},{128,112},... | collective-permute-start | bytes 1843208 | tf_op jit(solution)/shard_map/ppermute | solution.py:697
  41.3 6.9 %collective-permute-start.4 = (f32[64,128]{1,0:T(8,128)S(1)}, f32[64,128]{1,0:T(8,128)S(1)}, u32[]{:S(2)}, u32[]{:S(2)}) collective-permute-start(f32[64,128]{1,0:T(8,128)S(1)} %get-tuple-element.27), channel_id=1, source_target_pairs={{0,16},{16,32},{32,48},{48,64},{64,80},{80,96},{96,112},{112,128},... | collective-permute-start | bytes 98312 | tf_op jit(solution)/shard_map/ppermute | solution.py:696
  43.2 8.9 %collective-permute-start.5 = (f32[64,128]{1,0:T(8,128)S(1)}, f32[64,128]{1,0:T(8,128)S(1)}, u32[]{:S(2)}, u32[]{:S(2)}) collective-permute-start(f32[64,128]{1,0:T(8,128)S(1)} %get-tuple-element.28), channel_id=1, source_target_pairs={{16,0},{32,16},{48,32},{64,48},{80,64},{96,80},{112,96},{128,112},... | collective-permute-start | bytes 98312 | tf_op jit(solution)/shard_map/ppermute | solution.py:697
  89.4 18.5 %all-to-all-start.2 = ((f32[256,1,128]{2,1,0:T(1,128)}), f32[256,1,128]{2,1,0:T(1,128)S(1)}, u32[]{:S(2)}, u32[]{:S(2)}) async-start(f32[256,1,128]{2,1,0:T(1,128)} %bitcast.29), calls=%async_computation.2 | async-start | bytes 262144 | tf_op jit(solution)/shard_map/all_to_all | solution.py:702
  94.7 13.2 %copy-start.8 = (f32[2,128,128]{2,1,0:T(8,128)S(1)}, f32[2,128,128]{2,1,0:T(8,128)}, u32[]{:S(2)}) copy-start(f32[2,128,128]{2,1,0:T(8,128)} %get-tuple-element.35.res_ref) | copy-start | bytes 393220
  94.7 13.2 %copy-start.9 = (f32[2,128,128]{2,1,0:T(8,128)S(1)}, f32[2,128,128]{2,1,0:T(8,128)}, u32[]{:S(2)}) copy-start(f32[2,128,128]{2,1,0:T(8,128)} %get-tuple-element.36.z_ref) | copy-start | bytes 393220
  94.7 13.2 %copy-start.10 = (f32[2,128,128]{2,1,0:T(8,128)S(1)}, f32[2,128,128]{2,1,0:T(8,128)}, u32[]{:S(2)}) copy-start(f32[2,128,128]{2,1,0:T(8,128)} %get-tuple-element.37.y_ref) | copy-start | bytes 393220
  94.8 13.1 %copy-start.11 = (f32[2,128,128]{2,1,0:T(8,128)S(1)}, f32[2,128,128]{2,1,0:T(8,128)}, u32[]{:S(2)}) copy-start(f32[2,128,128]{2,1,0:T(8,128)} %get-tuple-element.38.w_ref) | copy-start | bytes 393220
  94.8 13.1 %copy-start.12 = (f32[2,128,128]{2,1,0:T(8,128)S(1)}, f32[2,128,128]{2,1,0:T(8,128)}, u32[]{:S(2)}) copy-start(f32[2,128,128]{2,1,0:T(8,128)} %get-tuple-element.39.v_ref) | copy-start | bytes 393220

commit v4 on v3

--- a/solution.py
+++ b/solution.py
@@ -576,8 +576,10 @@
     dy = jnp.where(col < 128, 1, jnp.where(col < 192, 2, 0))
     owner, lane_of = decode(code, half_at, 3 * dx + dy)
     parts = table_parts(table)
+    unused = jnp.zeros((1, 128), F32)
     rim = [
-        lookup(parts, owner[r : r + 1, :128], lane_of[r : r + 1, :128]) for r in range(128, 136)
+        unused if r in (131, 132) else lookup(parts, owner[r : r + 1, :128], lane_of[r : r + 1, :128])
+        for r in range(128, 136)
     ]
     side_owner = (owner[:, 128:] + 1).astype(F32)
     side_lane = lane_of[:, 128:].astype(F32)
@@ -669,6 +671,10 @@
 SMALL = 24 << 20
 
 
+def near(*shape):
+    return pltpu.VMEM(shape, F32)
+
+
 def call(kernel, outs, *args, stay=(), limit=None, **kw):
     args = [x if any(x is y for y in stay) else here(x) for x in args]
     vmem = pl.BlockSpec(memory_space=pltpu.VMEM)
@@ -720,14 +726,14 @@
         in_specs=[block(4, 128), block(128, 128), block(4, 1, 8, 128), block(8, 128), block(8, 128)]
         + [block(1, 256), block(1, 256)],
         out_specs=[block(512, 128), block(64, 128)],
-        out_shape=[sds(512, 128), sds(64, 128)],
+        out_shape=[sds(512, 128), near(64, 128)],
     )(owner, thickness, ocean_state, diffusivity, wet_mask, columns, slots)
     got_draft = exchange(send_draft)
     up, down, nodemap = call(
         pack_x_kernel,
         [sds(64, 128), sds(64, 128), sds(128, 128)],
         lead, owner, *ice,
-        stay=given + (lead,),
+        stay=given,
         limit=SMALL,
     )
     lo, hi = swap(up, down, XAXES)

time: 110 us -> 109 us (level)
  no operation moved by 1% of the time
where the time goes in v4:
time: 109 us
  starting transfers between devices  42.9 us (39%)
  blocking collectives  31 us (28%)
  Pallas kernels  24.9 us (23%)
  waiting for transfers between devices  8.87 us (8%)
    all_to_all x1, blocking collectives, exchange(): lax.all_to_all(table, ALL, split_axis=0, concat_axis=0, tiled=True)  31 us
    pallas_call x7, Pallas kernels, call(): pl.pallas_call(kernel, in_specs=[vmem] * len(args), out_specs=[vmem] * le...  22.5 us
    all_to_all x2, starting transfers between devices, exchange(): lax.all_to_all(table, ALL, split_axis=0, concat_axis=0, tiled=True)  20.9 us
    ppermute x3, starting transfers between devices, swap(): high = lax.ppermute(down, axes, [(b, a) for a, b in forward])  11.8 us
    ppermute x3, starting transfers between devices, swap(): low = lax.ppermute(up, axes, forward)  10.2 us
    ppermute x3, waiting for transfers between devices, swap(): high = lax.ppermute(down, axes, [(b, a) for a, b in forward])  6.71 us
    pallas_call x1, Pallas kernels, shards(): pl.pallas_call(draft_kernel, name='draft', grid=(1,), in_specs=[block(4,...  2.45 us
  transfers between devices with their start and end apart: 8, of which 5 were waited for; matrix products, arithmetic and copies ran while one was open for 0% of the time, Pallas kernels for 19%

profile of v4, /device:TPU:1, one launch (start us, length us, event | category | flops | bytes accessed | tf_op | source)
XLA Modules:
  0.0 108.7 jit_solution(9258812304500626758)
XLA Ops:
  0.6 0.0 copy-start.7
  0.7 2.4 %draft.1 = (f32[512,128]{1,0:T(8,128)}, f32[64,128]{1,0:T(8,128)S(1)}) custom-call(s32[4,128]{1,0:T(4,128)} %bitcast.24, f32[128,128]{1,0:T(8,128)} %thick.5, f32[4,60,8,128]{3,2,1,0:T(8,128)} %state_ref.1, f32[8,128]{1,0:T(8,128)} %diff_ref.1, s32[8,128]{1,0:T(8,128)} %wet_ref.1, s32[1,256]{1,0:T(1,128)} %bitcast.30, s32[1,256]{1,0:T(1,128)} %bitcast.31), custom_call_target="tpu_custom_call" | custom-call | tf_op jit(solution)/shard_map/draft/pallas_call | solution.py:722
  3.1 0.0 copy-start.4
  3.1 0.0 copy-start.5
  3.1 0.0 copy-start.6
  3.2 15.7 %all-to-all-start = ((f32[256,2,128]{2,1,0:T(2,128)}), f32[256,2,128]{2,1,0:T(2,128)S(1)}, u32[]{:S(2)}, u32[]{:S(2)}) async-start(f32[256,2,128]{2,1,0:T(2,128)} %bitcast.28), calls=%async_computation | async-start | bytes 524288 | tf_op jit(solution)/shard_map/all_to_all | solution.py:708
  18.9 0.6 shard_map.156
  19.5 1.5 %shard_map.157.ice_ref = f32[368,128]{1,0:T(8,128)S(1)} custom-call(f32[1920,128]{1,0:T(8,128)S(1)} %bitcast.17, f32[128,128]{1,0:T(8,128)S(1)} %get-tuple-element.24.nodemap_ref, f32[128,128]{1,0:T(8,128)S(1)} %copy-done.3, f32[128,128]{1,0:T(8,128)S(1)} %copy-done.4, f32[128,128]{1,0:T(8,128)S(1)} %copy-done.5, s32[128,128]{1,0:T(8,128)S(1)} %copy-done.6, ...), custom_call_target="tpu_custom_call" | custom-call | tf_op jit(solution)/shard_map/pallas_call | solution.py:681
  21.0 1.3 %collective-permute-start.1 = (f32[368,128]{1,0:T(8,128)S(1)}, f32[368,128]{1,0:T(8,128)S(1)}, u32[]{:S(2)}, u32[]{:S(2)}) collective-permute-start(f32[368,128]{1,0:T(8,128)S(1)} %shard_map.157.ice_ref), channel_id=1, source_target_pairs={{1,0},{2,1},{3,2},{4,3},{5,4},{6,5},{7,6},{8,7},{9,8},{10,9},{11,1... | collective-permute-start | bytes 565256 | tf_op jit(solution)/shard_map/ppermute | solution.py:703
  22.3 4.0 %collective-permute-start = (f32[368,128]{1,0:T(8,128)S(1)}, f32[368,128]{1,0:T(8,128)S(1)}, u32[]{:S(2)}, u32[]{:S(2)}) collective-permute-start(f32[368,128]{1,0:T(8,128)S(1)} %shard_map.157.ice_ref), channel_id=1, source_target_pairs={{0,1},{1,2},{2,3},{3,4},{4,5},{5,6},{6,7},{7,8},{8,9},{9,10},{10,1... | collective-permute-start | bytes 565256 | tf_op jit(solution)/shard_map/ppermute | solution.py:702
  26.3 2.8 %collective-permute-done.1.right_ref = f32[368,128]{1,0:T(8,128)S(1)} collective-permute-done((f32[368,128]{1,0:T(8,128)S(1)}, f32[368,128]{1,0:T(8,128)S(1)}, u32[]{:S(2)}, u32[]{:S(2)}) %collective-permute-start.1) | collective-permute-done | bytes 188448 | tf_op jit(solution)/shard_map/ppermute | solution.py:703
  29.1 0.3 collective-permute-done.left_ref
  29.4 1.3 %shard_map.158 = (f32[1200,128]{1,0:T(8,128)}, f32[1200,128]{1,0:T(8,128)}) custom-call(f32[1920,128]{1,0:T(8,128)S(1)} %bitcast.18, f32[368,128]{1,0:T(8,128)S(1)} %collective-permute-done.left_ref, f32[368,128]{1,0:T(8,128)S(1)} %collective-permute-done.1.right_ref), custom_call_target="tpu_custom_call" | custom-call | tf_op jit(solution)/shard_map/pallas_call | solution.py:681
  30.6 4.3 %collective-permute-start.2 = (f32[1200,128]{1,0:T(8,128)}, f32[1200,128]{1,0:T(8,128)S(1)}, u32[]{:S(2)}, u32[]{:S(2)}) collective-permute-start(f32[1200,128]{1,0:T(8,128)} %get-tuple-element.25), channel_id=1, source_target_pairs={{0,16},{16,32},{32,48},{48,64},{64,80},{80,96},{96,112},{112,128},... | collective-permute-start | bytes 1843208 | tf_op jit(solution)/shard_map/ppermute | solution.py:702
  34.9 5.6 %collective-permute-start.3 = (f32[1200,128]{1,0:T(8,128)}, f32[1200,128]{1,0:T(8,128)}, u32[]{:S(2)}, u32[]{:S(2)}) collective-permute-start(f32[1200,128]{1,0:T(8,128)} %get-tuple-element.26), channel_id=1, source_target_pairs={{16,0},{32,16},{48,32},{64,48},{80,64},{96,80},{112,96},{128,112},... | collective-permute-start | bytes 1843208 | tf_op jit(solution)/shard_map/ppermute | solution.py:703
  40.5 1.9 %collective-permute-start.4 = (f32[64,128]{1,0:T(8,128)S(1)}, f32[64,128]{1,0:T(8,128)S(1)}, u32[]{:S(2)}, u32[]{:S(2)}) collective-permute-start(f32[64,128]{1,0:T(8,128)S(1)} %get-tuple-element.27), channel_id=1, source_target_pairs={{0,16},{16,32},{32,48},{48,64},{64,80},{80,96},{96,112},{112,128},... | collective-permute-start | bytes 98312 | tf_op jit(solution)/shard_map/ppermute | solution.py:702
  42.5 4.9 %collective-permute-start.5 = (f32[64,128]{1,0:T(8,128)S(1)}, f32[64,128]{1,0:T(8,128)S(1)}, u32[]{:S(2)}, u32[]{:S(2)}) collective-permute-start(f32[64,128]{1,0:T(8,128)S(1)} %get-tuple-element.28), channel_id=1, source_target_pairs={{16,0},{32,16},{48,32},{64,48},{80,64},{96,80},{112,96},{128,112},... | collective-permute-start | bytes 98312 | tf_op jit(solution)/shard_map/ppermute | solution.py:703
  47.3 0.3 collective-permute-done.4.lo_ref
  47.6 3.9 %collective-permute-done.5.hi_ref = f32[64,128]{1,0:T(8,128)S(1)} collective-permute-done((f32[64,128]{1,0:T(8,128)S(1)}, f32[64,128]{1,0:T(8,128)S(1)}, u32[]{:S(2)}, u32[]{:S(2)}) %collective-permute-start.5) | collective-permute-done | bytes 32800 | tf_op jit(solution)/shard_map/ppermute | solution.py:703
  51.5 0.0 all-to-all-done
  51.5 2.4 %shard_map.159 = (f32[32,128]{1,0:T(8,128)S(1)}, f32[8,128]{1,0:T(8,128)}, f32[96,128]{1,0:T(8,128)S(1)}, f32[256,128]{1,0:T(8,128)S(1)}) custom-call(f32[64,128]{1,0:T(8,128)S(1)} %get-tuple-element.23.lead_ref, f32[64,128]{1,0:T(8,128)S(1)} %collective-permute-done.4.lo_ref, f32[64,128]{1,0:T(8,128)S(1)} %collective-permute-done.5.hi_ref, ...), custom_call_target="tpu_custom_call" | custom-call | tf_op jit(solution)/shard_map/pallas_call | solution.py:681
  53.9 31.0 %all_to_all.33 = f32[256,1,128]{2,1,0:T(1,128)S(1)} all-to-all(f32[256,1,128]{2,1,0:T(1,128)S(1)} %bitcast.23), channel_id=1, replica_groups=mesh['grp'=2,'gx'=8,'gy_0'=4,'gy_1'=4] {'grp','gx','gy_0','gy_1'}, dimensions={0} | all-to-all | bytes 262144 | tf_op jit(solution)/shard_map/all_to_all | solution.py:708
  84.9 3.7 %shard_map.161 = (f32[256,128]{1,0:T(8,128)}, f32[2,128,128]{2,1,0:T(8,128)}, f32[2,128,128]{2,1,0:T(8,128)}, f32[2,128,128]{2,1,0:T(8,128)}, f32[2,128,128]{2,1,0:T(8,128)}, /*index=5*/f32[2,128,128]{2,1,0:T(8,128)}) custom-call(s32[4,128]{1,0:T(4,128)S(1)} %bitcast.26, f32[256,128]{1,0:T(8,128)S(1)} %bitcast.22, ...), custom_call_target="tpu_custom_call" | custom-call | tf_op jit(solution)/shard_map/pallas_call | solution.py:681
  88.6 5.3 %all-to-all-start.2 = ((f32[256,1,128]{2,1,0:T(1,128)}), f32[256,1,128]{2,1,0:T(1,128)S(1)}, u32[]{:S(2)}, u32[]{:S(2)}) async-start(f32[256,1,128]{2,1,0:T(1,128)} %bitcast.29), calls=%async_computation.2 | async-start | bytes 262144 | tf_op jit(solution)/shard_map/all_to_all | solution.py:708
  93.9 0.0 collective-permute-done.2.lo_ref
  93.9 0.0 collective-permute-done.3.hi_ref
  93.9 0.0 copy-start.8
  94.0 11.5 %shard_map.160 = f32[1920,128]{1,0:T(8,128)} custom-call(f32[1920,128]{1,0:T(8,128)S(1)} %bitcast.19, f32[1200,128]{1,0:T(8,128)S(1)} %collective-permute-done.2.lo_ref, f32[1200,128]{1,0:T(8,128)} %collective-permute-done.3.hi_ref, f32[368,128]{1,0:T(8,128)S(1)} %collective-permute-done.left_ref, f32[368,128]{1,0:T(8,128)S(1)} %collective-permute-done.1.right_ref, ...), custom_call_target="tpu_custom_call" | custom-call | tf_op jit(solution)/shard_map/pallas_call | solution.py:681
  105.5 1.6 %all-to-all-done.2 = f32[256,1,128]{2,1,0:T(1,128)S(1)} async-done(((f32[256,1,128]{2,1,0:T(1,128)}), f32[256,1,128]{2,1,0:T(1,128)S(1)}, u32[]{:S(2)}, u32[]{:S(2)}) %all-to-all-start.2) | async-done | bytes 131104 | tf_op jit(solution)/shard_map/all_to_all | solution.py:708
  107.1 0.0 copy-done.8
  107.1 0.0 copy-done.10
  107.1 1.6 %shard_map.162 = (f32[2,128,128]{2,1,0:T(8,128)}, f32[2,128,128]{2,1,0:T(8,128)}) custom-call(f32[256,128]{1,0:T(8,128)S(1)} %bitcast.21, f32[2,128,128]{2,1,0:T(8,128)S(1)} %copy-done.1, f32[2,128,128]{2,1,0:T(8,128)S(1)} %copy-done.8, f32[2,128,128]{2,1,0:T(8,128)S(1)} %copy-done.9, f32[2,128,128]{2,1,0:T(8,128)S(1)} %copy-done.10, ...), custom_call_target="tpu_custom_call" | custom-call | tf_op jit(solution)/shard_map/pallas_call | solution.py:681
  (21 shorter events, 0.0 us)
Async XLA Ops:
  0.6 18.2 %copy-start.7 = (f32[128,128]{1,0:T(8,128)S(1)}, f32[128,128]{1,0:T(8,128)}, u32[]{:S(2)}) copy-start(f32[128,128]{1,0:T(8,128)} %coup.5) | copy-start | bytes 196612
  0.6 18.2 %copy-start.13 = (s32[1,1,128,4]{2,3,1,0:T(4,128)S(1)}, s32[1,1,128,4]{2,3,1,0:T(4,128)}, u32[]{:S(2)}) copy-start(s32[1,1,128,4]{2,3,1,0:T(4,128)} %param.18) | copy-start | bytes 6148
  0.7 18.8 %copy-start = (f32[4,60,8,128]{3,2,1,0:T(8,128)S(1)}, f32[4,60,8,128]{3,2,1,0:T(8,128)}, u32[]{:S(2)}) copy-start(f32[4,60,8,128]{3,2,1,0:T(8,128)} %state_ref.1) | copy-start | bytes 2949124
  3.1 15.7 %copy-start.1 = (f32[2,128,128]{2,1,0:T(8,128)S(1)}, f32[2,128,128]{2,1,0:T(8,128)}, u32[]{:S(2)}) copy-start(f32[2,128,128]{2,1,0:T(8,128)} %guess_ref.1) | copy-start | bytes 393220
  3.1 15.7 %copy-start.2 = (f32[2,128,128]{2,1,0:T(8,128)S(1)}, f32[2,128,128]{2,1,0:T(8,128)}, u32[]{:S(2)}) copy-start(f32[2,128,128]{2,1,0:T(8,128)} %drive.5) | copy-start | bytes 393220
  3.1 15.8 %copy-start.3 = (f32[128,128]{1,0:T(8,128)S(1)}, f32[128,128]{1,0:T(8,128)}, u32[]{:S(2)}) copy-start(f32[128,128]{1,0:T(8,128)} %thick.5) | copy-start | bytes 196612
  3.1 15.8 %copy-start.4 = (f32[128,128]{1,0:T(8,128)S(1)}, f32[128,128]{1,0:T(8,128)}, u32[]{:S(2)}) copy-start(f32[128,128]{1,0:T(8,128)} %visc.5) | copy-start | bytes 196612
  3.1 15.8 %copy-start.5 = (f32[128,128]{1,0:T(8,128)S(1)}, f32[128,128]{1,0:T(8,128)}, u32[]{:S(2)}) copy-start(f32[128,128]{1,0:T(8,128)} %fric.5) | copy-start | bytes 196612
  3.1 15.8 %copy-start.6 = (s32[128,128]{1,0:T(8,128)S(1)}, s32[128,128]{1,0:T(8,128)}, u32[]{:S(2)}) copy-start(s32[128,128]{1,0:T(8,128)} %ground.5) | copy-start | bytes 196612
  3.2 48.4 %all-to-all-start = ((f32[256,2,128]{2,1,0:T(2,128)}), f32[256,2,128]{2,1,0:T(2,128)S(1)}, u32[]{:S(2)}, u32[]{:S(2)}) async-start(f32[256,2,128]{2,1,0:T(2,128)} %bitcast.28), calls=%async_computation | async-start | bytes 524288 | tf_op jit(solution)/shard_map/all_to_all | solution.py:708
  21.0 8.1 %collective-permute-start.1 = (f32[368,128]{1,0:T(8,128)S(1)}, f32[368,128]{1,0:T(8,128)S(1)}, u32[]{:S(2)}, u32[]{:S(2)}) collective-permute-start(f32[368,128]{1,0:T(8,128)S(1)} %shard_map.157.ice_ref), channel_id=1, source_target_pairs={{1,0},{2,1},{3,2},{4,3},{5,4},{6,5},{7,6},{8,7},{9,8},{10,9},{11,1... | collective-permute-start | bytes 565256 | tf_op jit(solution)/shard_map/ppermute | solution.py:703
  22.3 7.1 %collective-permute-start = (f32[368,128]{1,0:T(8,128)S(1)}, f32[368,128]{1,0:T(8,128)S(1)}, u32[]{:S(2)}, u32[]{:S(2)}) collective-permute-start(f32[368,128]{1,0:T(8,128)S(1)} %shard_map.157.ice_ref), channel_id=1, source_target_pairs={{0,1},{1,2},{2,3},{3,4},{4,5},{5,6},{6,7},{7,8},{8,9},{9,10},{10,1... | collective-permute-start | bytes 565256 | tf_op jit(solution)/shard_map/ppermute | solution.py:702
  30.6 63.3 %collective-permute-start.2 = (f32[1200,128]{1,0:T(8,128)}, f32[1200,128]{1,0:T(8,128)S(1)}, u32[]{:S(2)}, u32[]{:S(2)}) collective-permute-start(f32[1200,128]{1,0:T(8,128)} %get-tuple-element.25), channel_id=1, source_target_pairs={{0,16},{16,32},{32,48},{48,64},{64,80},{80,96},{96,112},{112,128},... | collective-permute-start | bytes 1843208 | tf_op jit(solution)/shard_map/ppermute | solution.py:702
  34.9 59.0 %collective-permute-start.3 = (f32[1200,128]{1,0:T(8,128)}, f32[1200,128]{1,0:T(8,128)}, u32[]{:S(2)}, u32[]{:S(2)}) collective-permute-start(f32[1200,128]{1,0:T(8,128)} %get-tuple-element.26), channel_id=1, source_target_pairs={{16,0},{32,16},{48,32},{64,48},{80,64},{96,80},{112,96},{128,112},... | collective-permute-start | bytes 1843208 | tf_op jit(solution)/shard_map/ppermute | solution.py:703
  40.5 7.1 %collective-permute-start.4 = (f32[64,128]{1,0:T(8,128)S(1)}, f32[64,128]{1,0:T(8,128)S(1)}, u32[]{:S(2)}, u32[]{:S(2)}) collective-permute-start(f32[64,128]{1,0:T(8,128)S(1)} %get-tuple-element.27), channel_id=1, source_target_pairs={{0,16},{16,32},{32,48},{48,64},{64,80},{80,96},{96,112},{112,128},... | collective-permute-start | bytes 98312 | tf_op jit(solution)/shard_map/ppermute | solution.py:702
  42.5 9.1 %collective-permute-start.5 = (f32[64,128]{1,0:T(8,128)S(1)}, f32[64,128]{1,0:T(8,128)S(1)}, u32[]{:S(2)}, u32[]{:S(2)}) collective-permute-start(f32[64,128]{1,0:T(8,128)S(1)} %get-tuple-element.28), channel_id=1, source_target_pairs={{16,0},{32,16},{48,32},{64,48},{80,64},{96,80},{112,96},{128,112},... | collective-permute-start | bytes 98312 | tf_op jit(solution)/shard_map/ppermute | solution.py:703
  88.6 18.5 %all-to-all-start.2 = ((f32[256,1,128]{2,1,0:T(1,128)}), f32[256,1,128]{2,1,0:T(1,128)S(1)}, u32[]{:S(2)}, u32[]{:S(2)}) async-start(f32[256,1,128]{2,1,0:T(1,128)} %bitcast.29), calls=%async_computation.2 | async-start | bytes 262144 | tf_op jit(solution)/shard_map/all_to_all | solution.py:708
  93.9 13.2 %copy-start.8 = (f32[2,128,128]{2,1,0:T(8,128)S(1)}, f32[2,128,128]{2,1,0:T(8,128)}, u32[]{:S(2)}) copy-start(f32[2,128,128]{2,1,0:T(8,128)} %get-tuple-element.35.res_ref) | copy-start | bytes 393220
  93.9 13.2 %copy-start.9 = (f32[2,128,128]{2,1,0:T(8,128)S(1)}, f32[2,128,128]{2,1,0:T(8,128)}, u32[]{:S(2)}) copy-start(f32[2,128,128]{2,1,0:T(8,128)} %get-tuple-element.36.z_ref) | copy-start | bytes 393220
  94.0 13.2 %copy-start.10 = (f32[2,128,128]{2,1,0:T(8,128)S(1)}, f32[2,128,128]{2,1,0:T(8,128)}, u32[]{:S(2)}) copy-start(f32[2,128,128]{2,1,0:T(8,128)} %get-tuple-element.37.y_ref) | copy-start | bytes 393220
  94.0 13.1 %copy-start.11 = (f32[2,128,128]{2,1,0:T(8,128)S(1)}, f32[2,128,128]{2,1,0:T(8,128)}, u32[]{:S(2)}) copy-start(f32[2,128,128]{2,1,0:T(8,128)} %get-tuple-element.38.w_ref) | copy-start | bytes 393220
  94.0 13.1 %copy-start.12 = (f32[2,128,128]{2,1,0:T(8,128)S(1)}, f32[2,128,128]{2,1,0:T(8,128)}, u32[]{:S(2)}) copy-start(f32[2,128,128]{2,1,0:T(8,128)} %get-tuple-element.39.v_ref) | copy-start | bytes 393220
